TPU v7x, 512 devices: a whole 4x4x16 slice. The times are simulated.
512 devices in a mesh: gx: 16 (over x_hi, y, core), gy: 32 (over x_lo, z).
Axes of the slice: x: 4 (x_hi: 2, x_lo: 2; x = x_hi * 2 + x_lo), y: 4, z: 16, core: 2. Of those that a mesh axis runs over, the one named last changes fastest.
Arguments:
- entity_table: float32 [131072, 256], P(('gx', 'gy')), may hold values from -2.5 to 2.5
- relations: float32 [4, 256, 256], replicated, may hold values from -0.375 to 0.375
- rel_ids: int32 [3, 2048], P(None, ('gx', 'gy')), may hold values from 0 to 3
- edge_src: int32 [3, 3145728], P(None, ('gx', 'gy')), may hold values from 0 to 255
- edge_dst: int32 [3, 3145728], P(None, ('gx', 'gy')), may hold values from 0 to 255
Outputs:
- new_table: float32 [131072, 256], P(('gx', 'gy'))
- rel_grad: float32 [4, 256, 256], replicated
All inputs are finite; a program needn't handle non-finite values.
Results may differ from a plain program's by a relative error of at most 0.0089.
Values may be sent and summed in bfloat16 or wider, within the bound.
No kernel may reach another device: no remote copies, remote signals or barrier semaphores. Data moves between devices by JAX's collectives and lax.ppermute only.
A program may use at most 64 MiB of HBM per device.

v0:
```python
import functools
import math

import jax
import jax.numpy as jnp
from jax import lax
from jax.experimental import pallas as pl
from jax.experimental.pallas import tpu as pltpu
from jax.sharding import Mesh
from jax.sharding import PartitionSpec as P


AXES = ("xh", "y", "c", "xl", "zh", "zl")
GX = ("xh", "y", "c")
GY = ("xl", "zh", "zl")
NEAR = ("xh", "y", "c", "xl", "zl")
FAR = "zh"
LEARN_RATE = 0.5
FIRST_GRANT = 60 * 1024 * 1024 - 320 * 1024
VMEM = pl.BlockSpec(memory_space=pltpu.VMEM)
SMEM = pl.BlockSpec(memory_space=pltpu.SMEM)
HBM = pl.BlockSpec(memory_space=pltpu.HBM)
F32 = jnp.float32
BF16 = jnp.bfloat16


def shifted(value, axes, steps):
    count = lax.axis_size(axes)
    pairs = [(source, (source + steps) % count) for source in range(count)]
    return lax.ppermute(value, axes, pairs)


def dot_nn(left, right):
    return lax.dot_general(left, right, (((1,), (0,)), ((), ())), preferred_element_type=F32)


def dot_nt(left, right):
    return lax.dot_general(left, right, (((1,), (1,)), ((), ())), preferred_element_type=F32)


def dot_tn(left, right):
    return lax.dot_general(left, right, (((0,), (0,)), ((), ())), preferred_element_type=F32)


def call(kernel, outs, in_specs, flops, aliases=None, scratch=(), grant=16 * 2**20):
    moved = sum(math.prod(o.shape) * o.dtype.itemsize for o in outs)
    return pl.pallas_call(
        kernel,
        out_shape=tuple(outs),
        in_specs=list(in_specs),
        out_specs=tuple(VMEM for _ in outs),
        scratch_shapes=list(scratch),
        input_output_aliases=aliases or {},
        compiler_params=pltpu.CompilerParams(vmem_limit_bytes=grant),
        cost_estimate=pl.CostEstimate(
            flops=flops, bytes_accessed=4 * moved, transcendentals=0
        ),
    )


def map_rows(rows_b, rel_ref, ids_ref, turn, out_ref):
    groups = ids_ref.shape[1]
    size = rows_b.shape[0] // groups
    for g in range(groups):
        chosen = rel_ref[ids_ref[turn, g]].astype(BF16)
        part = slice(g * size, (g + 1) * size)
        out_ref[part, :] = dot_nn(rows_b[part, :], chosen).astype(BF16)


def folded(edge_ref, turn, width):
    pieces = edge_ref.shape[1] // width
    rows = [edge_ref[turn : turn + 1, i * width : (i + 1) * width] for i in range(pieces)]
    return jnp.concatenate(rows, axis=0).astype(F32).astype(BF16)


def one_hot(row, size):
    count = row.shape[1]
    wide = jnp.broadcast_to(row.astype(F32), (16, count)).astype(BF16)
    index = lax.broadcasted_iota(jnp.int32, (16, count), 0).astype(F32).astype(BF16)
    one = jnp.ones((16, count), BF16)
    zero = jnp.zeros((16, count), BF16)
    parts = [jnp.where(wide == index + BF16(16 * i), one, zero) for i in range(size // 16)]
    return jnp.concatenate(parts, axis=0)


def counted(row_of, col_of, pieces, size):
    acc = jnp.zeros((size, size), F32)
    for i in range(pieces):
        acc = acc + dot_nt(one_hot(row_of(i), size), one_hot(col_of(i), size))
    return acc


def pieces_of(ref, first):
    return lambda i: ref[first + i : first + i + 1, :]


def own_count(ends_ref, size, first=0):
    pieces = (ends_ref.shape[0] - first) // 2
    return counted(pieces_of(ends_ref, first), pieces_of(ends_ref, first + pieces), pieces, size)


def far_count(ends_ref, size, first=0):
    pieces = (ends_ref.shape[0] - first) // 2
    return counted(pieces_of(ends_ref, first + pieces), pieces_of(ends_ref, first), pieces, size)


def slopes(scores, counts):
    scaling = 1.0 / math.sqrt(scores.shape[0])
    return ((jax.nn.sigmoid(scores) - counts) * scaling).astype(BF16)


def source_grad(pulled_b, rel_ref, ids_ref, turn):
    groups = ids_ref.shape[1]
    size = pulled_b.shape[0] // groups
    parts = []
    for g in range(groups):
        chosen = rel_ref[ids_ref[turn, g]].astype(BF16)
        parts.append(dot_nt(pulled_b[g * size : (g + 1) * size, :], chosen))
    return jnp.concatenate(parts, axis=0)


def target_grad(xb_ref, ap_ref, counts_t):
    mapped = ap_ref[: xb_ref.shape[0], :]
    slopes_t = slopes(dot_nt(xb_ref[...], mapped), counts_t)
    return dot_nn(slopes_t, mapped).astype(BF16).astype(F32)


def add_relation(acc_ref, xb_ref, pulled_b, ids_ref, turn):
    groups = ids_ref.shape[1]
    size = pulled_b.shape[0] // groups
    for g in range(groups):
        part = slice(g * size, (g + 1) * size)
        kind = ids_ref[turn, g]
        acc_ref[kind] = acc_ref[kind] + dot_tn(xb_ref[part, :], pulled_b[part, :])


def fetched(pairs, sems):
    copies = [
        pltpu.make_async_copy(source, target, sems.at[i])
        for i, (source, target) in enumerate(pairs)
    ]
    for copy in copies:
        copy.start()
    return copies


def prepare_kernel(
    ids_ref, x_hbm, rel_hbm, src_hbm, dst_hbm, xb_ref, pay_ref, x_ref, rel_ref, src_ref, dst_ref, sems
):
    size, width = x_ref.shape
    pairs = [(x_hbm, x_ref), (rel_hbm, rel_ref), (src_hbm, src_ref), (dst_hbm, dst_ref)]
    copies = fetched(pairs, sems)
    copies[0].wait()
    rows_b = x_ref[...].astype(BF16)
    xb_ref[...] = rows_b
    copies[2].wait()
    copies[3].wait()
    pieces = (pay_ref.shape[0] - size) // 2
    pay_ref[size : size + pieces, :] = folded(src_ref, 0, width)
    pay_ref[size + pieces :, :] = folded(dst_ref, 0, width)
    copies[1].wait()
    map_rows(rows_b, rel_ref, ids_ref, 0, pay_ref)


def first_window_kernel(src_hbm, dst_hbm, c_ref, near_ref, last_ref, src_ref, dst_ref, ends_ref, sems):
    for copy in fetched([(src_hbm, src_ref), (dst_hbm, dst_ref)], sems):
        copy.wait()
    size = c_ref.shape[0]
    pieces = ends_ref.shape[0] // 2
    for turn, out in ((1, near_ref), (2, last_ref), (0, ends_ref)):
        out[:pieces, :] = folded(src_ref, turn, size)
        out[pieces:, :] = folded(dst_ref, turn, size)
    c_ref[...] = own_count(ends_ref, size)


def window_kernel(turn, fresh, ids_ref, ends_ref, xb_ref, h_ref, *refs):
    size = xb_ref.shape[0]
    refs = list(refs)
    if fresh:
        far_ref, c_ref, acc_ref, ct_ref = refs
        acc_ref[...] = jnp.zeros_like(acc_ref)
        ct_ref[...] = far_count(far_ref, size)
    else:
        acc_in_ref, c_ref, acc_ref = refs
        acc_ref[...] = acc_in_ref[...]
    add_relation(acc_ref, xb_ref, h_ref[...], ids_ref, turn - 1)
    c_ref[...] = own_count(ends_ref, size)


def round_kernel(
    turn, ids_ref, xb_ref, xq_ref, pay_ref, far_ref, c_ref, extra_ref, x_ref, rel_ref,
    xn_ref, xbn_ref, payn_ref, h_ref,
):
    size = xb_ref.shape[0]
    slopes_b = slopes(dot_nt(pay_ref[:size, :], xq_ref[...]), c_ref[...])
    pulled = dot_nn(slopes_b, xq_ref[...]).astype(BF16)
    h_ref[...] = pulled
    counts_t = far_count(far_ref, size, size) if turn == 0 else extra_ref[0][...]
    grad = source_grad(pulled, rel_ref, ids_ref, turn) + target_grad(xb_ref, far_ref, counts_t)
    moved = x_ref[...] - LEARN_RATE * grad
    xn_ref[...] = moved
    moved_b = moved.astype(BF16)
    xbn_ref[...] = moved_b
    map_rows(moved_b, rel_ref, ids_ref, turn + 1, payn_ref)
    if turn == 1:
        payn_ref[size:, :] = extra_ref[1][...]


def first_round_kernel(*refs):
    round_kernel(0, *refs[:6], None, *refs[6:])


def second_round_kernel(*refs):
    round_kernel(1, *refs[:6], refs[6:8], *refs[8:])


def last_kernel(turn, ids_ref, xb_ref, xq_ref, pay_ref, c_ref, acc_in_ref, h_ref, out_ref, acc_ref):
    size = xb_ref.shape[0]
    slopes_b = slopes(dot_nt(pay_ref[:size, :], xq_ref[...]), c_ref[...])
    pulled = dot_nn(slopes_b, xq_ref[...]).astype(BF16)
    h_ref[...] = pulled
    acc_ref[...] = acc_in_ref[...]
    add_relation(acc_ref, xb_ref, pulled, ids_ref, turn)
    kinds, width = acc_ref.shape[:2]
    for k in range(kinds):
        out_ref[k * width : (k + 1) * width, :] = acc_ref[k].astype(BF16)


def finish_kernel(turn, ids_ref, xb_ref, far_ref, h_ref, x_ref, rel_ref, xn_ref):
    counts_t = far_count(far_ref, xb_ref.shape[0], xb_ref.shape[0])
    grad = source_grad(h_ref[...], rel_ref, ids_ref, turn) + target_grad(xb_ref, far_ref, counts_t)
    xn_ref[...] = x_ref[...] - LEARN_RATE * grad


def sum_kernel(in_ref, out_ref):
    acc = in_ref[0].astype(F32)
    for i in range(1, in_ref.shape[0]):
        acc = acc + in_ref[i].astype(F32)
    total = acc.astype(BF16)
    for i in range(out_ref.shape[0]):
        out_ref[i] = total


def summed_for(parts, copies):
    count, share, width = parts.shape
    out = jax.ShapeDtypeStruct((copies, share, width), BF16)
    return call(sum_kernel, [out], [VMEM], count * share * width)(parts)[0]


def reduce_everywhere(payload):
    rows, width = payload.shape
    near = lax.axis_size(NEAR)
    far = lax.axis_size(FAR)
    part = lax.all_to_all(payload.reshape(near, rows // near, width), NEAR, 0, 0)
    part = lax.all_to_all(summed_for(part, far), FAR, 0, 0)
    part = lax.all_to_all(summed_for(part, near), NEAR, 0, 0)
    return part.reshape(rows, width).astype(F32)


def training(entity, relations, rel_ids, edge_src, edge_dst):
    rows, width = entity.shape
    kinds = relations.shape[0]
    turns, edges = edge_src.shape
    square = 2 * rows * rows * width
    counting = 2 * rows * rows * edges
    ends_rows = 2 * edges // width
    f_rows = jax.ShapeDtypeStruct((rows, width), F32)
    b_rows = jax.ShapeDtypeStruct((rows, width), BF16)
    b_pay = jax.ShapeDtypeStruct((rows + ends_rows, width), BF16)
    b_ends = jax.ShapeDtypeStruct((ends_rows, width), BF16)
    f_count = jax.ShapeDtypeStruct((rows, rows), F32)
    f_rel = jax.ShapeDtypeStruct(relations.shape, F32)
    b_rel = jax.ShapeDtypeStruct((kinds * width, width), BF16)
    edge_scratch = [pltpu.VMEM(edge_src.shape, jnp.int32)] * 2
    buckets = ((GY, 1), (GX, 1), (GY, -1))

    def exchanged(turn, rows_b, payload):
        axes, offset = buckets[turn]
        got = shifted(rows_b, axes, offset)
        far = shifted(payload, axes, -offset)
        return got, far

    xb0, pay0 = call(
        prepare_kernel, [b_rows, b_pay], [SMEM] + [HBM] * 4, square,
        scratch=[pltpu.VMEM(entity.shape, F32), pltpu.VMEM(relations.shape, F32)]
        + edge_scratch + [pltpu.SemaphoreType.DMA((4,))],
        grant=FIRST_GRANT,
    )(rel_ids, entity, relations, edge_src, edge_dst)

    xq, far = exchanged(0, xb0, pay0)
    c, ends1, ends2 = call(
        first_window_kernel, [f_count, b_ends, b_ends], [HBM] * 2, counting,
        scratch=edge_scratch + [pltpu.VMEM(b_ends.shape, BF16), pltpu.SemaphoreType.DMA((2,))],
    )(edge_src, edge_dst)
    far_ends = shifted(ends1, buckets[1][0], -buckets[1][1])
    x1, xb1, pay1, h0 = call(
        first_round_kernel, [f_rows, b_rows, b_rows, b_rows],
        [SMEM] + [VMEM] * 7, 7 * square + counting,
    )(rel_ids, xb0, xq, pay0, far, c, entity, relations)

    xq, far = exchanged(1, xb1, pay1)
    c, acc, ct = call(
        functools.partial(window_kernel, 1, True), [f_count, f_rel, f_count],
        [SMEM] + [VMEM] * 4, 2 * counting + square,
    )(rel_ids, ends1, xb0, h0, far_ends)
    x2, xb2, pay2, h1 = call(
        second_round_kernel, [f_rows, b_rows, b_pay, b_rows],
        [SMEM] + [VMEM] * 9, 7 * square,
    )(rel_ids, xb1, xq, pay1, far, c, ct, ends2, x1, relations)

    xq, far = exchanged(2, xb2, pay2)
    c, acc = call(
        functools.partial(window_kernel, 2, False), [f_count, f_rel],
        [SMEM] + [VMEM] * 4, counting + square, aliases={4: 1},
    )(rel_ids, ends2, xb1, h1, acc)
    h2, payload, _ = call(
        functools.partial(last_kernel, 2), [b_rows, b_rel, f_rel],
        [SMEM] + [VMEM] * 5, 3 * square, aliases={5: 2},
    )(rel_ids, xb2, xq, pay2, c, acc)
    x3 = call(
        functools.partial(finish_kernel, 2), [f_rows],
        [SMEM] + [VMEM] * 5, 3 * square + counting,
    )(rel_ids, xb2, far, h2, x2, relations)[0]

    summed = reduce_everywhere(payload)
    divisor = math.sqrt(turns * lax.axis_size(AXES))
    return x3, (summed / divisor).reshape(relations.shape)


def solution(mesh):
    inner = Mesh(mesh.devices.reshape(2, 4, 2, 2, 8, 2), AXES)
    return jax.shard_map(
        training,
        mesh=inner,
        in_specs=(P(AXES, None), P(), P(None, AXES), P(None, AXES), P(None, AXES)),
        out_specs=(P(AXES, None), P()),
        check_vma=False,
    )
```

profile of v0, /device:TPU:1, one launch (start us, length us, event | category | flops | bytes accessed | tf_op | source)
XLA Modules:
  0.0 111.9 jit_solution(16760672056816509184)
XLA Ops:
  0.6 3.1 %shard_map.68 = (bf16[256,256]{1,0:T(8,128)(2,1)}, bf16[304,256]{1,0:T(8,128)(2,1)}) custom-call(s32[3,4]{1,0:T(4,128)} %ids_ref.9, f32[256,256]{1,0:T(8,128)} %refs_6_.1, f32[4,256,256]{2,1,0:T(8,128)} %rel_ref.1, s32[3,6144]{1,0:T(4,128)} %src_hbm.3, s32[3,6144]{1,0:T(4,128)} %dst_hbm.3), custom_call_target="tpu_custom_call" | custom-call | flops 33554432 | bytes 1146880 | tf_op jit(solution)/shard_map/pallas_call | solution.py:283
  3.7 12.9 %collective-permute-start.1 = (bf16[304,256]{1,0:T(8,128)(2,1)}, bf16[304,256]{1,0:T(8,128)(2,1)S(1)}, u32[]{:S(2)}, u32[]{:S(2)}) collective-permute-start(bf16[304,256]{1,0:T(8,128)(2,1)} %get-tuple-element.23.refs_3_), channel_id=1, source_target_pairs={{0,31},{1,0},{2,1},{3,2},{4,3},{5,4},{6,5},{7,6},{8,7},{9,8},{10,9... | collective-permute-start | bytes 466952 | tf_op jit(solution)/shard_map/ppermute | solution.py:30
  16.6 0.0 copy-start
  16.6 0.0 copy-start.1
  16.6 0.0 copy-start.5
  16.6 0.0 copy-start.6
  16.7 2.1 %collective-permute-start = (bf16[256,256]{1,0:T(8,128)(2,1)}, bf16[256,256]{1,0:T(8,128)(2,1)S(1)}, u32[]{:S(2)}, u32[]{:S(2)}) collective-permute-start(bf16[256,256]{1,0:T(8,128)(2,1)} %get-tuple-element.22.refs_1_.xb_ref), channel_id=1, source_target_pairs={{0,1},{1,2},{2,3},{3,4},{4,5},{5,6},{6,7},{7,8},{8,9},{9,10},{10,1... | collective-permute-start | bytes 393224 | tf_op jit(solution)/shard_map/ppermute | solution.py:30
  18.7 1.3 %shard_map.69 = (f32[256,256]{1,0:T(8,128)S(1)}, bf16[48,256]{1,0:T(8,128)(2,1)S(1)}, bf16[48,256]{1,0:T(8,128)(2,1)S(1)}) custom-call(s32[3,6144]{1,0:T(4,128)S(1)} %copy-done.2, s32[3,6144]{1,0:T(4,128)S(1)} %copy-done.3), custom_call_target="tpu_custom_call" | custom-call | flops 805306368 | bytes 1245184 | tf_op jit(solution)/shard_map/pallas_call | solution.py:291
  20.1 0.0 copy-start.4
  20.1 2.9 %collective-permute-start.4 = (bf16[48,256]{1,0:T(8,128)(2,1)S(1)}, bf16[48,256]{1,0:T(8,128)(2,1)S(1)}, u32[]{:S(2)}, u32[]{:S(2)}) collective-permute-start(bf16[48,256]{1,0:T(8,128)(2,1)S(1)} %get-tuple-element.27.ends_ref), channel_id=1, source_target_pairs={{0,480},{32,0},{64,32},{96,64},{128,96},{160,128},{192,160},{224,1... | collective-permute-start | bytes 73736 | tf_op jit(solution)/shard_map/ppermute | solution.py:30
  23.0 1.9 %collective-permute-done.refs_2_ = bf16[256,256]{1,0:T(8,128)(2,1)S(1)} collective-permute-done((bf16[256,256]{1,0:T(8,128)(2,1)}, bf16[256,256]{1,0:T(8,128)(2,1)S(1)}, u32[]{:S(2)}, u32[]{:S(2)}) %collective-permute-start) | collective-permute-done | bytes 131104 | tf_op jit(solution)/shard_map/ppermute | solution.py:30
  24.9 2.3 %shard_map.70 = (f32[256,256]{1,0:T(8,128)S(1)}, bf16[256,256]{1,0:T(8,128)(2,1)S(1)}, bf16[256,256]{1,0:T(8,128)(2,1)S(1)}, bf16[256,256]{1,0:T(8,128)(2,1)S(1)}) custom-call(s32[3,4]{1,0:T(4,128)S(1)} %copy-done.4, bf16[256,256]{1,0:T(8,128)(2,1)S(1)} %copy-done.6, bf16[256,256]{1,0:T(8,128)(2,1)S(1)} %collective-permute-done.refs_2_, ...), custom_call_target="tpu_custom_call" | custom-call | flops 1040187392 | bytes 2621440 | tf_op jit(solution)/shard_map/pallas_call | solution.py:296
  27.2 5.2 %collective-permute-start.2 = (bf16[256,256]{1,0:T(8,128)(2,1)S(1)}, bf16[256,256]{1,0:T(8,128)(2,1)S(1)}, u32[]{:S(2)}, u32[]{:S(2)}) collective-permute-start(bf16[256,256]{1,0:T(8,128)(2,1)S(1)} %get-tuple-element.25.refs_1_.xb_ref), channel_id=1, source_target_pairs={{0,32},{32,64},{64,96},{96,128},{128,160},{160,192},{192,224},{224... | collective-permute-start | bytes 393224 | tf_op jit(solution)/shard_map/ppermute | solution.py:30
  32.4 1.9 %collective-permute-start.3 = (bf16[256,256]{1,0:T(8,128)(2,1)S(1)}, bf16[256,256]{1,0:T(8,128)(2,1)S(1)}, u32[]{:S(2)}, u32[]{:S(2)}) collective-permute-start(bf16[256,256]{1,0:T(8,128)(2,1)S(1)} %get-tuple-element.26.refs_3_), channel_id=1, source_target_pairs={{0,480},{32,0},{64,32},{96,64},{128,96},{160,128},{192,160},{224,1... | collective-permute-start | bytes 393224 | tf_op jit(solution)/shard_map/ppermute | solution.py:30
  34.3 2.6 %shard_map.71 = (f32[256,256]{1,0:T(8,128)S(1)}, f32[4,256,256]{2,1,0:T(8,128)S(1)}, f32[256,256]{1,0:T(8,128)S(1)}) custom-call(s32[3,4]{1,0:T(4,128)S(1)} %copy-done.4, bf16[48,256]{1,0:T(8,128)(2,1)S(1)} %get-tuple-element.27.ends_ref, bf16[256,256]{1,0:T(8,128)(2,1)S(1)} %copy-done.6, bf16[256,256]{1,0:T(8,128)(2,1)S(1)} %get-tuple-element.28.h_ref, ...), custom_call_target="tpu_custom_call" | custom-call | flops 1644167168 | bytes 6291456 | tf_op jit(solution)/shard_map/pallas_call | solution.py:302
  37.0 0.0 collective-permute-done.2.refs_2_
  37.0 2.0 %collective-permute-done.3.refs_4_ = bf16[256,256]{1,0:T(8,128)(2,1)S(1)} collective-permute-done((bf16[256,256]{1,0:T(8,128)(2,1)S(1)}, bf16[256,256]{1,0:T(8,128)(2,1)S(1)}, u32[]{:S(2)}, u32[]{:S(2)}) %collective-permute-start.3) | collective-permute-done | bytes 131104 | tf_op jit(solution)/shard_map/ppermute | solution.py:30
  39.0 1.4 %shard_map.72 = (f32[256,256]{1,0:T(8,128)S(1)}, bf16[256,256]{1,0:T(8,128)(2,1)S(1)}, bf16[304,256]{1,0:T(8,128)(2,1)S(1)}, bf16[256,256]{1,0:T(8,128)(2,1)S(1)}) custom-call(s32[3,4]{1,0:T(4,128)S(1)} %copy-done.4, bf16[256,256]{1,0:T(8,128)(2,1)S(1)} %get-tuple-element.25.refs_1_.xb_ref, bf16[256,256]{1,0:T(8,128)(2,1)S(1)} %collective-permute-done.2.refs_2_, ...), custom_call_target="tpu_custom_call" | custom-call | flops 234881024 | bytes 2719744 | tf_op jit(solution)/shard_map/pallas_call | solution.py:306
  40.4 2.1 %collective-permute-start.6 = (bf16[256,256]{1,0:T(8,128)(2,1)S(1)}, bf16[256,256]{1,0:T(8,128)(2,1)S(1)}, u32[]{:S(2)}, u32[]{:S(2)}) collective-permute-start(bf16[256,256]{1,0:T(8,128)(2,1)S(1)} %get-tuple-element.33.xb_ref), channel_id=1, source_target_pairs={{0,31},{1,0},{2,1},{3,2},{4,3},{5,4},{6,5},{7,6},{8,7},{9,8},{10,9... | collective-permute-start | bytes 393224 | tf_op jit(solution)/shard_map/ppermute | solution.py:30
  42.6 1.8 %shard_map.73 = (f32[256,256]{1,0:T(8,128)S(1)}, f32[4,256,256]{2,1,0:T(8,128)S(1)}) custom-call(s32[3,4]{1,0:T(4,128)S(1)} %copy-done.4, bf16[48,256]{1,0:T(8,128)(2,1)S(1)} %get-tuple-element.31.refs_7_.ends_ref, bf16[256,256]{1,0:T(8,128)(2,1)S(1)} %get-tuple-element.25.refs_1_.xb_ref, ...), custom_call_target="tpu_custom_call", output_to_operand_aliasing={{1}: (4, {})} | custom-call | flops 838860800 | bytes 5242880 | tf_op jit(solution)/shard_map/pallas_call | solution.py:312
  44.4 1.8 %collective-permute-done.6.xq_ref = bf16[256,256]{1,0:T(8,128)(2,1)S(1)} collective-permute-done((bf16[256,256]{1,0:T(8,128)(2,1)S(1)}, bf16[256,256]{1,0:T(8,128)(2,1)S(1)}, u32[]{:S(2)}, u32[]{:S(2)}) %collective-permute-start.6) | collective-permute-done | bytes 131104 | tf_op jit(solution)/shard_map/ppermute | solution.py:30
  46.2 1.3 %shard_map.74 = (bf16[256,256]{1,0:T(8,128)(2,1)S(1)}, bf16[1024,256]{1,0:T(8,128)(2,1)S(1)}, f32[4,256,256]{2,1,0:T(8,128)S(1)}) custom-call(s32[3,4]{1,0:T(4,128)S(1)} %copy-done.4, bf16[256,256]{1,0:T(8,128)(2,1)S(1)} %get-tuple-element.33.xb_ref, bf16[256,256]{1,0:T(8,128)(2,1)S(1)} %collective-permute-done.6.xq_ref, ...), custom_call_target="tpu_custom_call", output_to_operand_aliasing={{2}: (5, {})} | custom-call | flops 100663296 | bytes 6815744 | tf_op jit(solution)/shard_map/pallas_call | solution.py:316
  47.5 24.0 %all_to_all.15.in_ref = bf16[64,16,256]{2,1,0:T(8,128)(2,1)S(1)} all-to-all(bf16[64,16,256]{2,1,0:T(8,128)(2,1)S(1)} %bitcast.2), channel_id=1, replica_groups=mesh['xh'=2,'y'=4,'c'=2,'xl'=2,'zh'=8,'zl'=2] {'xh','y','c','xl','zl'}, dimensions={0} | all-to-all | bytes 1048576 | tf_op jit(solution)/shard_map/all_to_all | solution.py:254
  71.5 0.1 shard_map.76
  71.6 18.7 %all_to_all.16.in_ref = bf16[8,16,256]{2,1,0:T(8,128)(2,1)S(1)} all-to-all(bf16[8,16,256]{2,1,0:T(8,128)(2,1)S(1)} %shard_map.76), channel_id=1, replica_groups=mesh['xh'=2,'y'=4,'c'=2,'xl'=2,'zh'=8,'zl'=2] {'zh'}, dimensions={0} | all-to-all | bytes 131072 | tf_op jit(solution)/shard_map/all_to_all | solution.py:255
  90.2 0.8 shard_map.77
  91.0 6.1 %all-to-all-start.2 = ((bf16[64,16,256]{2,1,0:T(8,128)(2,1)}), bf16[64,16,256]{2,1,0:T(8,128)(2,1)S(1)}, u32[]{:S(2)}, u32[]{:S(2)}) async-start(bf16[64,16,256]{2,1,0:T(8,128)(2,1)} %shard_map.77), calls=%async_computation.2 | async-start | bytes 1048576 | tf_op jit(solution)/shard_map/all_to_all | solution.py:256
  97.1 3.3 %collective-permute-start.5 = (bf16[304,256]{1,0:T(8,128)(2,1)S(1)}, bf16[304,256]{1,0:T(8,128)(2,1)S(1)}, u32[]{:S(2)}, u32[]{:S(2)}) collective-permute-start(bf16[304,256]{1,0:T(8,128)(2,1)S(1)} %get-tuple-element.34.pay_ref), channel_id=1, source_target_pairs={{0,1},{1,2},{2,3},{3,4},{4,5},{5,6},{6,7},{7,8},{8,9},{9,10},{10,1... | collective-permute-start | bytes 466952 | tf_op jit(solution)/shard_map/ppermute | solution.py:30
  100.4 6.7 %collective-permute-done.5.far_ref = bf16[304,256]{1,0:T(8,128)(2,1)S(1)} collective-permute-done((bf16[304,256]{1,0:T(8,128)(2,1)S(1)}, bf16[304,256]{1,0:T(8,128)(2,1)S(1)}, u32[]{:S(2)}, u32[]{:S(2)}) %collective-permute-start.5) | collective-permute-done | bytes 155680 | tf_op jit(solution)/shard_map/ppermute | solution.py:30
  107.1 2.6 %shard_map.75 = f32[256,256]{1,0:T(8,128)} custom-call(s32[3,4]{1,0:T(4,128)S(1)} %copy-done.4, bf16[256,256]{1,0:T(8,128)(2,1)S(1)} %get-tuple-element.33.xb_ref, bf16[304,256]{1,0:T(8,128)(2,1)S(1)} %collective-permute-done.5.far_ref, bf16[256,256]{1,0:T(8,128)(2,1)S(1)} %get-tuple-element.39.h_ref, f32[256,256]{1,0:T(8,128)S(1)} %get-tuple-element.40.x_ref, ...), custom_call_target="tpu_custom_call" | custom-call | flops 905969664 | bytes 1048576 | tf_op jit(solution)/shard_map/pallas_call | solution.py:320
  109.7 1.0 all-to-all-done.2
  110.8 1.1 convert_multiply_fusion
  (11 shorter events, 0.0 us)
Async XLA Ops:
  0.6 18.1 %copy-start.2 = (s32[3,6144]{1,0:T(4,128)S(1)}, s32[3,6144]{1,0:T(4,128)}, u32[]{:S(2)}) copy-start(s32[3,6144]{1,0:T(4,128)} %src_hbm.3) | copy-start | bytes 221188
  0.6 18.1 %copy-start.3 = (s32[3,6144]{1,0:T(4,128)S(1)}, s32[3,6144]{1,0:T(4,128)}, u32[]{:S(2)}) copy-start(s32[3,6144]{1,0:T(4,128)} %dst_hbm.3) | copy-start | bytes 221188
  3.7 21.1 %collective-permute-start.1 = (bf16[304,256]{1,0:T(8,128)(2,1)}, bf16[304,256]{1,0:T(8,128)(2,1)S(1)}, u32[]{:S(2)}, u32[]{:S(2)}) collective-permute-start(bf16[304,256]{1,0:T(8,128)(2,1)} %get-tuple-element.23.refs_3_), channel_id=1, source_target_pairs={{0,31},{1,0},{2,1},{3,2},{4,3},{5,4},{6,5},{7,6},{8,7},{9,8},{10,9... | collective-permute-start | bytes 466952 | tf_op jit(solution)/shard_map/ppermute | solution.py:30
  16.6 8.2 %copy-start = (f32[4,256,256]{2,1,0:T(8,128)S(1)}, f32[4,256,256]{2,1,0:T(8,128)}, u32[]{:S(2)}) copy-start(f32[4,256,256]{2,1,0:T(8,128)} %rel_ref.1) | copy-start | bytes 3145732
  16.6 8.2 %copy-start.1 = (f32[256,256]{1,0:T(8,128)S(1)}, f32[256,256]{1,0:T(8,128)}, u32[]{:S(2)}) copy-start(f32[256,256]{1,0:T(8,128)} %refs_6_.1) | copy-start | bytes 786436
  16.6 8.2 %copy-start.5 = (bf16[304,256]{1,0:T(8,128)(2,1)S(1)}, bf16[304,256]{1,0:T(8,128)(2,1)}, u32[]{:S(2)}) copy-start(bf16[304,256]{1,0:T(8,128)(2,1)} %get-tuple-element.23.refs_3_) | copy-start | bytes 466948
  16.6 8.2 %copy-start.6 = (bf16[256,256]{1,0:T(8,128)(2,1)S(1)}, bf16[256,256]{1,0:T(8,128)(2,1)}, u32[]{:S(2)}) copy-start(bf16[256,256]{1,0:T(8,128)(2,1)} %get-tuple-element.22.refs_1_.xb_ref) | copy-start | bytes 393220
  16.7 8.2 %collective-permute-start = (bf16[256,256]{1,0:T(8,128)(2,1)}, bf16[256,256]{1,0:T(8,128)(2,1)S(1)}, u32[]{:S(2)}, u32[]{:S(2)}) collective-permute-start(bf16[256,256]{1,0:T(8,128)(2,1)} %get-tuple-element.22.refs_1_.xb_ref), channel_id=1, source_target_pairs={{0,1},{1,2},{2,3},{3,4},{4,5},{5,6},{6,7},{7,8},{8,9},{9,10},{10,1... | collective-permute-start | bytes 393224 | tf_op jit(solution)/shard_map/ppermute | solution.py:30
  20.1 4.8 %copy-start.4 = (s32[3,4]{1,0:T(4,128)S(1)}, s32[3,4]{1,0:T(4,128)}, u32[]{:S(2)}) copy-start(s32[3,4]{1,0:T(4,128)} %ids_ref.9) | copy-start | bytes 148
  20.1 14.2 %collective-permute-start.4 = (bf16[48,256]{1,0:T(8,128)(2,1)S(1)}, bf16[48,256]{1,0:T(8,128)(2,1)S(1)}, u32[]{:S(2)}, u32[]{:S(2)}) collective-permute-start(bf16[48,256]{1,0:T(8,128)(2,1)S(1)} %get-tuple-element.27.ends_ref), channel_id=1, source_target_pairs={{0,480},{32,0},{64,32},{96,64},{128,96},{160,128},{192,160},{224,1... | collective-permute-start | bytes 73736 | tf_op jit(solution)/shard_map/ppermute | solution.py:30
  27.2 9.8 %collective-permute-start.2 = (bf16[256,256]{1,0:T(8,128)(2,1)S(1)}, bf16[256,256]{1,0:T(8,128)(2,1)S(1)}, u32[]{:S(2)}, u32[]{:S(2)}) collective-permute-start(bf16[256,256]{1,0:T(8,128)(2,1)S(1)} %get-tuple-element.25.refs_1_.xb_ref), channel_id=1, source_target_pairs={{0,32},{32,64},{64,96},{96,128},{128,160},{160,192},{192,224},{224... | collective-permute-start | bytes 393224 | tf_op jit(solution)/shard_map/ppermute | solution.py:30
  32.4 6.6 %collective-permute-start.3 = (bf16[256,256]{1,0:T(8,128)(2,1)S(1)}, bf16[256,256]{1,0:T(8,128)(2,1)S(1)}, u32[]{:S(2)}, u32[]{:S(2)}) collective-permute-start(bf16[256,256]{1,0:T(8,128)(2,1)S(1)} %get-tuple-element.26.refs_3_), channel_id=1, source_target_pairs={{0,480},{32,0},{64,32},{96,64},{128,96},{160,128},{192,160},{224,1... | collective-permute-start | bytes 393224 | tf_op jit(solution)/shard_map/ppermute | solution.py:30
  40.4 5.7 %collective-permute-start.6 = (bf16[256,256]{1,0:T(8,128)(2,1)S(1)}, bf16[256,256]{1,0:T(8,128)(2,1)S(1)}, u32[]{:S(2)}, u32[]{:S(2)}) collective-permute-start(bf16[256,256]{1,0:T(8,128)(2,1)S(1)} %get-tuple-element.33.xb_ref), channel_id=1, source_target_pairs={{0,31},{1,0},{2,1},{3,2},{4,3},{5,4},{6,5},{7,6},{8,7},{9,8},{10,9... | collective-permute-start | bytes 393224 | tf_op jit(solution)/shard_map/ppermute | solution.py:30
  91.0 19.7 %all-to-all-start.2 = ((bf16[64,16,256]{2,1,0:T(8,128)(2,1)}), bf16[64,16,256]{2,1,0:T(8,128)(2,1)S(1)}, u32[]{:S(2)}, u32[]{:S(2)}) async-start(bf16[64,16,256]{2,1,0:T(8,128)(2,1)} %shard_map.77), calls=%async_computation.2 | async-start | bytes 1048576 | tf_op jit(solution)/shard_map/all_to_all | solution.py:256
  97.1 10.0 %collective-permute-start.5 = (bf16[304,256]{1,0:T(8,128)(2,1)S(1)}, bf16[304,256]{1,0:T(8,128)(2,1)S(1)}, u32[]{:S(2)}, u32[]{:S(2)}) collective-permute-start(bf16[304,256]{1,0:T(8,128)(2,1)S(1)} %get-tuple-element.34.pay_ref), channel_id=1, source_target_pairs={{0,1},{1,2},{2,3},{3,4},{4,5},{5,6},{6,7},{7,8},{8,9},{9,10},{10,1... | collective-permute-start | bytes 466952 | tf_op jit(solution)/shard_map/ppermute | solution.py:30
where the time goes:
time: 112 us
  blocking collectives  42.6 us (38%)
  starting transfers between devices  36.3 us (32%)
  Pallas kernels  17.5 us (16%)
  waiting for transfers between devices  13.4 us (12%)
  other arithmetic  1.12 us (1%)
    ppermute x7, starting transfers between devices, shifted(): return lax.ppermute(value, axes, pairs)  30.3 us
    all_to_all x1, blocking collectives, reduce_everywhere(): lax.all_to_all(payload.reshape(near, rows // near, width), NEAR, 0, 0)  24 us
    all_to_all x1, blocking collectives, reduce_everywhere(): part = lax.all_to_all(summed_for(part, far), FAR, 0, 0)  18.7 us
    ppermute x7, waiting for transfers between devices, shifted(): return lax.ppermute(value, axes, pairs)  12.3 us
    all_to_all x1, starting transfers between devices, reduce_everywhere(): part = lax.all_to_all(summed_for(part, near), NEAR, 0, 0)  6.06 us
    pallas_call x1, Pallas kernels, training(): call(prepare_kernel, [b_rows, b_pay], [SMEM] + [HBM] * 4, square, scratch...  3.07 us
    pallas_call x1, Pallas kernels, training(): call(functools.partial(finish_kernel, 2), [f_rows], [SMEM] + [VMEM] * 5,...  2.63 us
    pallas_call x1, Pallas kernels, training(): call(functools.partial(window_kernel, 1, True), [f_count, f_rel, f_count]...  2.62 us
  transfers between devices with their start and end apart: 8, of which 5 were waited for; matrix products, arithmetic and copies ran while one was open for 0% of the time, Pallas kernels for 10%

commit v1 on v0

v1 whole, which is shorter than its diff:
```python
import math

import jax
import jax.numpy as jnp
from jax import lax
from jax.experimental import pallas as pl
from jax.experimental.pallas import tpu as pltpu
from jax.sharding import Mesh
from jax.sharding import PartitionSpec as P


AXES = ("xh", "y", "c", "xl", "zh", "zl")
GX = ("xh", "y", "c")
GY = ("xl", "zh", "zl")
NEAR = ("xh", "y", "c", "xl", "zl")
FAR = "zh"
LEARN_RATE = 0.5
FIRST_GRANT = 60 * 1024 * 1024 - 320 * 1024
VMEM = pl.BlockSpec(memory_space=pltpu.VMEM)
SMEM = pl.BlockSpec(memory_space=pltpu.SMEM)
HBM = pl.BlockSpec(memory_space=pltpu.HBM)
F32 = jnp.float32
BF16 = jnp.bfloat16


def shifted(value, axes, steps):
    count = lax.axis_size(axes)
    pairs = [(source, (source + steps) % count) for source in range(count)]
    return lax.ppermute(value, axes, pairs)


def swapped_inner(value, axes):
    return lax.ppermute(value, axes, [(i, i ^ 1) for i in range(lax.axis_size(axes))])


def swapped_outer(value, axes):
    count = lax.axis_size(axes)
    pairs = [(i, (i + (1 if i % 2 else -1)) % count) for i in range(count)]
    return lax.ppermute(value, axes, pairs)


def dot_nn(left, right):
    return lax.dot_general(left, right, (((1,), (0,)), ((), ())), preferred_element_type=F32)


def dot_nt(left, right):
    return lax.dot_general(left, right, (((1,), (1,)), ((), ())), preferred_element_type=F32)


def dot_tn(left, right):
    return lax.dot_general(left, right, (((0,), (0,)), ((), ())), preferred_element_type=F32)


def call(kernel, outs, in_specs, flops, aliases=None, scratch=(), grant=16 * 2**20):
    moved = sum(math.prod(o.shape) * o.dtype.itemsize for o in outs)
    return pl.pallas_call(
        kernel,
        out_shape=tuple(outs),
        in_specs=list(in_specs),
        out_specs=tuple(VMEM for _ in outs),
        scratch_shapes=list(scratch),
        input_output_aliases=aliases or {},
        compiler_params=pltpu.CompilerParams(vmem_limit_bytes=grant),
        cost_estimate=pl.CostEstimate(
            flops=flops, bytes_accessed=4 * moved, transcendentals=0
        ),
    )


def map_rows(rows_b, rel_ref, ids_ref, turn):
    groups = ids_ref.shape[1]
    size = rows_b.shape[0] // groups
    parts = []
    for g in range(groups):
        chosen = rel_ref[ids_ref[turn, g]].astype(BF16)
        part = slice(g * size, (g + 1) * size)
        parts.append(dot_nn(rows_b[part, :], chosen).astype(BF16))
    return jnp.concatenate(parts, axis=0)


def folded(edge_ref, turn, width):
    pieces = edge_ref.shape[1] // width
    rows = [edge_ref[turn : turn + 1, i * width : (i + 1) * width] for i in range(pieces)]
    return jnp.concatenate(rows, axis=0).astype(F32).astype(BF16)


def one_hot(row, size):
    count = row.shape[1]
    wide = jnp.broadcast_to(row.astype(F32), (16, count)).astype(BF16)
    index = lax.broadcasted_iota(jnp.int32, (16, count), 0).astype(F32).astype(BF16)
    one = jnp.ones((16, count), BF16)
    zero = jnp.zeros((16, count), BF16)
    parts = [jnp.where(wide == index + BF16(16 * i), one, zero) for i in range(size // 16)]
    return jnp.concatenate(parts, axis=0)


def counted(row_of, col_of, pieces, size):
    acc = jnp.zeros((size, size), F32)
    for i in range(pieces):
        acc = acc + dot_nt(one_hot(row_of(i), size), one_hot(col_of(i), size))
    return acc


def own_count(ends, size):
    pieces = ends.shape[0] // 2
    return counted(
        lambda i: ends[i : i + 1, :], lambda i: ends[pieces + i : pieces + i + 1, :], pieces, size
    )


def far_count(ends, size):
    pieces = ends.shape[0] // 2
    return counted(
        lambda i: ends[pieces + i : pieces + i + 1, :], lambda i: ends[i : i + 1, :], pieces, size
    )


def slopes(scores, counts):
    scaling = 1.0 / math.sqrt(scores.shape[0])
    return ((jax.nn.sigmoid(scores) - counts) * scaling).astype(BF16)


def source_grad(pulled_b, rel_ref, ids_ref, turn):
    groups = ids_ref.shape[1]
    size = pulled_b.shape[0] // groups
    parts = []
    for g in range(groups):
        chosen = rel_ref[ids_ref[turn, g]].astype(BF16)
        parts.append(dot_nt(pulled_b[g * size : (g + 1) * size, :], chosen))
    return jnp.concatenate(parts, axis=0)


def target_grad(rows_b, mapped, counts_t):
    slopes_t = slopes(dot_nt(rows_b, mapped), counts_t)
    return dot_nn(slopes_t, mapped).astype(BF16).astype(F32)


def add_relation(acc_ref, rows_b, pulled_b, ids_ref, turn):
    groups = ids_ref.shape[1]
    size = pulled_b.shape[0] // groups
    for g in range(groups):
        part = slice(g * size, (g + 1) * size)
        kind = ids_ref[turn, g]
        acc_ref[kind] = acc_ref[kind] + dot_tn(rows_b[part, :], pulled_b[part, :])


def fetched(pairs, sems):
    copies = [
        pltpu.make_async_copy(source, target, sems.at[i])
        for i, (source, target) in enumerate(pairs)
    ]
    for copy in copies:
        copy.start()
    return copies


def is_even(axis):
    return lax.axis_index(axis) == 0


def put(even, rows, mapped, inner_ref, outer_ref, part):
    inner_ref[part, :] = jnp.where(even, rows, mapped)
    outer_ref[part, :] = jnp.where(even, mapped, rows)


def sent(even, inner_ref, outer_ref, part):
    inner, outer = inner_ref[part, :], outer_ref[part, :]
    return jnp.where(even, inner, outer), jnp.where(even, outer, inner)


def got(even, inner_ref, outer_ref, part):
    inner, outer = inner_ref[part, :], outer_ref[part, :]
    return jnp.where(even, outer, inner), jnp.where(even, inner, outer)


def folded_both(src_ref, dst_ref, turn, width):
    return jnp.concatenate(
        [folded(src_ref, turn, width), folded(dst_ref, turn, width)], axis=0
    )


def prepare_kernel(
    ids_ref, x_hbm, rel_hbm, src_hbm, dst_hbm, inner_ref, outer_ref, x_ref, rel_ref, src_ref, dst_ref, sems
):
    size, width = x_ref.shape
    even = is_even(GY[-1])
    copies = fetched(
        [(src_hbm, src_ref), (dst_hbm, dst_ref), (x_hbm, x_ref), (rel_hbm, rel_ref)], sems
    )
    copies[0].wait()
    copies[1].wait()
    ends = [folded_both(src_ref, dst_ref, turn, width) for turn in (2, 0)]
    put(even, ends[0], ends[1], inner_ref, outer_ref, slice(size, inner_ref.shape[0]))
    copies[2].wait()
    rows_b = x_ref[...].astype(BF16)
    copies[3].wait()
    mapped = map_rows(rows_b, rel_ref, ids_ref, 0)
    put(even, rows_b, mapped, inner_ref, outer_ref, slice(0, size))


def first_window_kernel(src_hbm, dst_hbm, inner_ref, outer_ref, c_ref, near_ref, src_ref, dst_ref, sems):
    copies = fetched([(src_hbm, src_ref), (dst_hbm, dst_ref)], sems)
    size = c_ref.shape[0]
    _, ends = sent(is_even(GY[-1]), inner_ref, outer_ref, slice(size, inner_ref.shape[0]))
    c_ref[...] = own_count(ends.astype(F32), size)
    for copy in copies:
        copy.wait()
    near_ref[...] = folded_both(src_ref, dst_ref, 1, near_ref.shape[1])


def second_window_kernel(
    ids_ref, inner_ref, outer_ref, h_ref, ends_ref, c_ref, acc_ref
):
    size = h_ref.shape[0]
    acc_ref[...] = jnp.zeros_like(acc_ref)
    rows_b, _ = sent(is_even(GY[-1]), inner_ref, outer_ref, slice(0, size))
    add_relation(acc_ref, rows_b, h_ref[...], ids_ref, 0)
    c_ref[...] = own_count(ends_ref[...].astype(F32), size)


def third_window_kernel(
    ids_ref, inner_ref, outer_ref, h_ref, inner0_ref, outer0_ref, acc_in_ref, c_ref, acc_ref
):
    size = h_ref.shape[0]
    acc_ref[...] = acc_in_ref[...]
    rows_b, _ = sent(is_even(GX[-1]), inner_ref, outer_ref, slice(0, size))
    add_relation(acc_ref, rows_b, h_ref[...], ids_ref, 1)
    ends, _ = sent(is_even(GY[-1]), inner0_ref, outer0_ref, slice(size, inner0_ref.shape[0]))
    c_ref[...] = own_count(ends.astype(F32), size)


def stepped(turn, axis, ids_ref, sent_refs, got_refs, c_ref, x_ref, rel_ref, xn_ref, h_ref):
    size = x_ref.shape[0]
    even = is_even(axis)
    top, tail = slice(0, size), slice(size, sent_refs[0].shape[0])
    rows_b, mapped = sent(even, *sent_refs, top)
    target, far = got(even, *got_refs, top)
    slopes_b = slopes(dot_nt(mapped, target), c_ref[...])
    pulled = dot_nn(slopes_b, target).astype(BF16)
    h_ref[...] = pulled
    _, far_ends = got(even, *got_refs, tail)
    counts_t = far_count(far_ends.astype(F32), size)
    grad = source_grad(pulled, rel_ref, ids_ref, turn) + target_grad(rows_b, far, counts_t)
    moved = x_ref[...] - LEARN_RATE * grad
    xn_ref[...] = moved
    moved_b = moved.astype(BF16)
    return moved_b, map_rows(moved_b, rel_ref, ids_ref, turn + 1)


def first_round_kernel(
    ids_ref, si_ref, so_ref, gi_ref, go_ref, c_ref, near_ref, x_ref, rel_ref,
    xn_ref, h_ref, inner_ref, outer_ref,
):
    size = x_ref.shape[0]
    rows_b, mapped = stepped(
        0, GY[-1], ids_ref, (si_ref, so_ref), (gi_ref, go_ref), c_ref, x_ref, rel_ref, xn_ref, h_ref
    )
    put(is_even(GX[-1]), rows_b, mapped, inner_ref, outer_ref, slice(0, size))
    inner_ref[size:, :] = near_ref[...]
    outer_ref[size:, :] = near_ref[...]


def second_round_kernel(
    ids_ref, si_ref, so_ref, gi_ref, go_ref, c_ref, x_ref, rel_ref,
    xn_ref, h_ref, rows_ref, mapped_ref,
):
    rows_b, mapped = stepped(
        1, GX[-1], ids_ref, (si_ref, so_ref), (gi_ref, go_ref), c_ref, x_ref, rel_ref, xn_ref, h_ref
    )
    rows_ref[...] = rows_b
    mapped_ref[...] = mapped


def last_kernel(ids_ref, rows_ref, xq_ref, mapped_ref, c_ref, acc_in_ref, h_ref, out_ref, acc_ref):
    slopes_b = slopes(dot_nt(mapped_ref[...], xq_ref[...]), c_ref[...])
    pulled = dot_nn(slopes_b, xq_ref[...]).astype(BF16)
    h_ref[...] = pulled
    acc_ref[...] = acc_in_ref[...]
    add_relation(acc_ref, rows_ref, pulled, ids_ref, 2)
    kinds, width = acc_ref.shape[:2]
    for k in range(kinds):
        out_ref[k * width : (k + 1) * width, :] = acc_ref[k].astype(BF16)


def finish_kernel(ids_ref, rows_ref, far_ref, gi_ref, go_ref, h_ref, x_ref, rel_ref, xn_ref):
    size = x_ref.shape[0]
    ends, _ = got(is_even(GY[-1]), gi_ref, go_ref, slice(size, gi_ref.shape[0]))
    counts_t = far_count(ends.astype(F32), size)
    grad = source_grad(h_ref[...], rel_ref, ids_ref, 2)
    grad = grad + target_grad(rows_ref[...], far_ref[...], counts_t)
    xn_ref[...] = x_ref[...] - LEARN_RATE * grad


def sum_kernel(in_ref, out_ref):
    acc = in_ref[0].astype(F32)
    for i in range(1, in_ref.shape[0]):
        acc = acc + in_ref[i].astype(F32)
    total = acc.astype(BF16)
    for i in range(out_ref.shape[0]):
        out_ref[i] = total


def summed_for(parts, copies):
    count, share, width = parts.shape
    out = jax.ShapeDtypeStruct((copies, share, width), BF16)
    return call(sum_kernel, [out], [VMEM], count * share * width)(parts)[0]


def reduce_everywhere(payload):
    rows, width = payload.shape
    near = lax.axis_size(NEAR)
    far = lax.axis_size(FAR)
    part = lax.all_to_all(payload.reshape(near, rows // near, width), NEAR, 0, 0)
    part = lax.all_to_all(summed_for(part, far), FAR, 0, 0)
    part = lax.all_to_all(summed_for(part, near), NEAR, 0, 0)
    return part.reshape(rows, width).astype(F32)


def training(entity, relations, rel_ids, edge_src, edge_dst):
    rows, width = entity.shape
    kinds = relations.shape[0]
    turns, edges = edge_src.shape
    square = 2 * rows * rows * width
    counting = 2 * rows * rows * edges
    ends_rows = 2 * edges // width
    f_rows = jax.ShapeDtypeStruct((rows, width), F32)
    b_rows = jax.ShapeDtypeStruct((rows, width), BF16)
    b_pay = jax.ShapeDtypeStruct((rows + ends_rows, width), BF16)
    b_ends = jax.ShapeDtypeStruct((ends_rows, width), BF16)
    f_count = jax.ShapeDtypeStruct((rows, rows), F32)
    f_rel = jax.ShapeDtypeStruct(relations.shape, F32)
    b_rel = jax.ShapeDtypeStruct((kinds * width, width), BF16)
    edge_scratch = [pltpu.VMEM(edge_src.shape, jnp.int32)] * 2
    buckets = ((GY, 1), (GX, 1), (GY, -1))

    def exchanged(turn, inner, outer):
        axes = buckets[turn][0]
        outer_got = swapped_outer(outer, axes)
        inner_got = swapped_inner(inner, axes)
        return inner_got, outer_got

    sent0 = call(
        prepare_kernel, [b_pay, b_pay], [SMEM] + [HBM] * 4, square,
        scratch=[pltpu.VMEM(entity.shape, F32), pltpu.VMEM(relations.shape, F32)]
        + edge_scratch + [pltpu.SemaphoreType.DMA((4,))],
        grant=FIRST_GRANT,
    )(rel_ids, entity, relations, edge_src, edge_dst)

    got0 = exchanged(0, *sent0)
    c, ends1 = call(
        first_window_kernel, [f_count, b_ends], [HBM] * 2 + [VMEM] * 2, counting,
        scratch=edge_scratch + [pltpu.SemaphoreType.DMA((2,))],
    )(edge_src, edge_dst, *sent0)
    x1, h0, *sent1 = call(
        first_round_kernel, [f_rows, b_rows, b_pay, b_pay],
        [SMEM] + [VMEM] * 8, 7 * square + counting,
    )(rel_ids, *sent0, *got0, c, ends1, entity, relations)

    got1 = exchanged(1, *sent1)
    c, acc = call(
        second_window_kernel, [f_count, f_rel], [SMEM] + [VMEM] * 4, counting + square,
    )(rel_ids, *sent0, h0, ends1)
    x2, h1, rows2, mapped2 = call(
        second_round_kernel, [f_rows, b_rows, b_rows, b_rows],
        [SMEM] + [VMEM] * 7, 7 * square + counting,
    )(rel_ids, *sent1, *got1, c, x1, relations)

    axes, offset = buckets[2]
    xq = shifted(rows2, axes, offset)
    far = shifted(mapped2, axes, -offset)
    c, acc = call(
        third_window_kernel, [f_count, f_rel],
        [SMEM] + [VMEM] * 6, counting + square, aliases={6: 1},
    )(rel_ids, *sent1, h1, *sent0, acc)
    h2, payload, _ = call(
        last_kernel, [b_rows, b_rel, f_rel],
        [SMEM] + [VMEM] * 5, 3 * square, aliases={5: 2},
    )(rel_ids, rows2, xq, mapped2, c, acc)
    x3 = call(
        finish_kernel, [f_rows], [SMEM] + [VMEM] * 7, 3 * square + counting,
    )(rel_ids, rows2, far, *got0, h2, x2, relations)[0]

    summed = reduce_everywhere(payload)
    divisor = math.sqrt(turns * lax.axis_size(AXES))
    return x3, (summed / divisor).reshape(relations.shape)


def solution(mesh):
    inner = Mesh(mesh.devices.reshape(2, 4, 2, 2, 8, 2), AXES)
    return jax.shard_map(
        training,
        mesh=inner,
        in_specs=(P(AXES, None), P(), P(None, AXES), P(None, AXES), P(None, AXES)),
        out_specs=(P(AXES, None), P()),
        check_vma=False,
    )
```

time: 112 us -> 111 us (level)
  waiting for transfers between devices: 13.4 us -> 9.95 us
  local copies, waits for them, and re-layouts: 0.04 us -> 2.03 us
    ppermute x0 -> x4, starting transfers between devices: none -> 22 us  [the longest x2 14.4 us: swapped_outer(): return lax.ppermute(value, axes, pairs)]
    ppermute x7 -> x2, starting transfers between devices: 30.3 us -> 8.74 us  [shifted(): return lax.ppermute(value, axes, pairs)]
    ppermute x7 -> x2, waiting for transfers between devices: 12.3 us -> 5.93 us  [shifted(): return lax.ppermute(value, axes, pairs)]
    ppermute x0 -> x4, waiting for transfers between devices: none -> 2.17 us  [the longest x2 2.16 us: swapped_outer(): return lax.ppermute(value, axes, pairs)]
    unnamed x14 -> x18, local copies, waits for them, and re-layouts: 0.04 us -> 2.03 us
  transfers between devices with their start and end apart: 8 -> 7, of which waited for: 5 -> 4; matrix products, arithmetic and copies ran while one was open for 0% -> 0% of each run, Pallas kernels for 10% -> 7%
where the time goes in v1:
time: 111 us; the launch traced here: 110 us
  blocking collectives  41.9 us (38%)
  starting transfers between devices  36.8 us (33%)
  Pallas kernels  17.7 us (16%)
  waiting for transfers between devices  9.95 us (9%)
  local copies, waits for them, and re-layouts  2.03 us (2%)
  other arithmetic  1.12 us (1%)
    all_to_all x1, blocking collectives, reduce_everywhere(): lax.all_to_all(payload.reshape(near, rows // near, width), NEAR, 0, 0)  23.3 us
    all_to_all x1, blocking collectives, reduce_everywhere(): part = lax.all_to_all(summed_for(part, far), FAR, 0, 0)  18.7 us
    ppermute x2, starting transfers between devices, swapped_outer(): return lax.ppermute(value, axes, pairs)  14.4 us
    ppermute x2, starting transfers between devices, shifted(): return lax.ppermute(value, axes, pairs)  8.74 us
    ppermute x2, starting transfers between devices, swapped_inner(): lax.ppermute(value, axes, [(i, i ^ 1) for i in range(lax.axis_size(axes))])  7.63 us
    all_to_all x1, starting transfers between devices, reduce_everywhere(): part = lax.all_to_all(summed_for(part, near), NEAR, 0, 0)  6.06 us
    ppermute x2, waiting for transfers between devices, shifted(): return lax.ppermute(value, axes, pairs)  5.93 us
    pallas_call x1, Pallas kernels, training(): call(prepare_kernel, [b_pay, b_pay], [SMEM] + [HBM] * 4, square, scratch=...  3.2 us
  transfers between devices with their start and end apart: 7, of which 4 were waited for; matrix products, arithmetic and copies ran while one was open for 0% of the time, Pallas kernels for 7%

profile of v1, /device:TPU:1, one launch (start us, length us, event | category | flops | bytes accessed | tf_op | source)
XLA Modules:
  0.0 110.3 jit_solution(5536562268370214950)
XLA Ops:
  0.6 3.2 %shard_map.68 = (bf16[304,256]{1,0:T(8,128)(2,1)}, bf16[304,256]{1,0:T(8,128)(2,1)}) custom-call(s32[3,4]{1,0:T(4,128)} %ids_ref.13, f32[256,256]{1,0:T(8,128)} %x_ref.1, f32[4,256,256]{2,1,0:T(8,128)} %rel_ref.5, s32[3,6144]{1,0:T(4,128)} %src_hbm.3, s32[3,6144]{1,0:T(4,128)} %dst_hbm.3), custom_call_target="tpu_custom_call" | custom-call | flops 33554432 | bytes 1245184 | tf_op jit(solution)/shard_map/pallas_call | solution.py:342
  3.9 4.4 %collective-permute-start = (bf16[304,256]{1,0:T(8,128)(2,1)}, bf16[304,256]{1,0:T(8,128)(2,1)S(1)}, u32[]{:S(2)}, u32[]{:S(2)}) collective-permute-start(bf16[304,256]{1,0:T(8,128)(2,1)} %get-tuple-element.20.inner_ref.si_ref.inner0_ref), channel_id=1, source_target_pairs={{0,1},{1,0},{2,3},{3,2},{4,5},{5,4},{6,7},{7,6},{8,9},{9,8},{10,11... | collective-permute-start | bytes 466952 | tf_op jit(solution)/shard_map/ppermute | solution.py:33
  8.2 0.0 copy-start
  8.2 0.0 copy-start.1
  8.3 11.3 %collective-permute-start.1 = (bf16[304,256]{1,0:T(8,128)(2,1)}, bf16[304,256]{1,0:T(8,128)(2,1)S(1)}, u32[]{:S(2)}, u32[]{:S(2)}) collective-permute-start(bf16[304,256]{1,0:T(8,128)(2,1)} %get-tuple-element.21.outer_ref.so_ref.outer0_ref), channel_id=1, source_target_pairs={{0,31},{1,2},{2,1},{3,4},{4,3},{5,6},{6,5},{7,8},{8,7},{9,10},{10,... | collective-permute-start | bytes 466952 | tf_op jit(solution)/shard_map/ppermute | solution.py:39
  19.6 0.0 copy-start.5
  19.6 0.9 copy-done.5
  20.5 0.9 copy-done.7
  21.4 1.3 %shard_map.69 = (f32[256,256]{1,0:T(8,128)S(1)}, bf16[48,256]{1,0:T(8,128)(2,1)S(1)}) custom-call(s32[3,6144]{1,0:T(4,128)S(1)} %copy-done.2, s32[3,6144]{1,0:T(4,128)S(1)} %copy-done.3, bf16[304,256]{1,0:T(8,128)(2,1)S(1)} %copy-done.5, bf16[304,256]{1,0:T(8,128)(2,1)S(1)} %copy-done.7), custom_call_target="tpu_custom_call" | custom-call | flops 805306368 | bytes 1146880 | tf_op jit(solution)/shard_map/pallas_call | solution.py:350
  22.7 0.0 copy-start.4
  22.7 0.5 collective-permute-done.1.go_ref
  23.2 0.2 copy-done.4
  23.4 2.4 %shard_map.70 = (f32[256,256]{1,0:T(8,128)S(1)}, bf16[256,256]{1,0:T(8,128)(2,1)S(1)}, bf16[304,256]{1,0:T(8,128)(2,1)S(1)}, bf16[304,256]{1,0:T(8,128)(2,1)S(1)}) custom-call(s32[3,4]{1,0:T(4,128)S(1)} %copy-done.4, bf16[304,256]{1,0:T(8,128)(2,1)S(1)} %copy-done.5, bf16[304,256]{1,0:T(8,128)(2,1)S(1)} %copy-done.7, ...), custom_call_target="tpu_custom_call" | custom-call | flops 1040187392 | bytes 2818048 | tf_op jit(solution)/shard_map/pallas_call | solution.py:354
  25.7 3.3 %collective-permute-start.2 = (bf16[304,256]{1,0:T(8,128)(2,1)S(1)}, bf16[304,256]{1,0:T(8,128)(2,1)S(1)}, u32[]{:S(2)}, u32[]{:S(2)}) collective-permute-start(bf16[304,256]{1,0:T(8,128)(2,1)S(1)} %get-tuple-element.24.si_ref.inner_ref), channel_id=1, source_target_pairs={{0,32},{32,0},{64,96},{96,64},{128,160},{160,128},{192,224},{224,1... | collective-permute-start | bytes 466952 | tf_op jit(solution)/shard_map/ppermute | solution.py:33
  29.0 3.1 %collective-permute-start.3 = (bf16[304,256]{1,0:T(8,128)(2,1)S(1)}, bf16[304,256]{1,0:T(8,128)(2,1)S(1)}, u32[]{:S(2)}, u32[]{:S(2)}) collective-permute-start(bf16[304,256]{1,0:T(8,128)(2,1)S(1)} %get-tuple-element.25.so_ref.outer_ref), channel_id=1, source_target_pairs={{0,480},{32,64},{64,32},{96,128},{128,96},{160,192},{192,160},{224... | collective-permute-start | bytes 466952 | tf_op jit(solution)/shard_map/ppermute | solution.py:39
  32.1 1.7 %shard_map.71 = (f32[256,256]{1,0:T(8,128)S(1)}, f32[4,256,256]{2,1,0:T(8,128)S(1)}) custom-call(s32[3,4]{1,0:T(4,128)S(1)} %copy-done.4, bf16[304,256]{1,0:T(8,128)(2,1)S(1)} %copy-done.5, bf16[304,256]{1,0:T(8,128)(2,1)S(1)} %copy-done.7, bf16[256,256]{1,0:T(8,128)(2,1)S(1)} %get-tuple-element.26.h_ref, bf16[48,256]{1,0:T(8,128)(2,1)S(1)} %get-tuple-element.23.near_ref.ends_ref), custom_call_target="tpu_custom_call" | custom-call | flops 838860800 | bytes 5242880 | tf_op jit(solution)/shard_map/pallas_call | solution.py:360
  33.9 1.7 %collective-permute-done.3.go_ref = bf16[304,256]{1,0:T(8,128)(2,1)S(1)} collective-permute-done((bf16[304,256]{1,0:T(8,128)(2,1)S(1)}, bf16[304,256]{1,0:T(8,128)(2,1)S(1)}, u32[]{:S(2)}, u32[]{:S(2)}) %collective-permute-start.3) | collective-permute-done | bytes 155680 | tf_op jit(solution)/shard_map/ppermute | solution.py:39
  35.6 2.4 %shard_map.72 = (f32[256,256]{1,0:T(8,128)S(1)}, bf16[256,256]{1,0:T(8,128)(2,1)S(1)}, bf16[256,256]{1,0:T(8,128)(2,1)S(1)}, bf16[256,256]{1,0:T(8,128)(2,1)S(1)}) custom-call(s32[3,4]{1,0:T(4,128)S(1)} %copy-done.4, bf16[304,256]{1,0:T(8,128)(2,1)S(1)} %get-tuple-element.24.si_ref.inner_ref, bf16[304,256]{1,0:T(8,128)(2,1)S(1)} %get-tuple-element.25.so_ref.outer_ref, ...), custom_call_target="tpu_custom_call" | custom-call | flops 1040187392 | bytes 2621440 | tf_op jit(solution)/shard_map/pallas_call | solution.py:363
  37.9 5.5 %collective-permute-start.5 = (bf16[256,256]{1,0:T(8,128)(2,1)S(1)}, bf16[256,256]{1,0:T(8,128)(2,1)S(1)}, u32[]{:S(2)}, u32[]{:S(2)}) collective-permute-start(bf16[256,256]{1,0:T(8,128)(2,1)S(1)} %get-tuple-element.29.rows_ref), channel_id=1, source_target_pairs={{0,31},{1,0},{2,1},{3,2},{4,3},{5,4},{6,5},{7,6},{8,7},{9,8},{10,9... | collective-permute-start | bytes 393224 | tf_op jit(solution)/shard_map/ppermute | solution.py:29
  43.4 1.9 %shard_map.73 = (f32[256,256]{1,0:T(8,128)S(1)}, f32[4,256,256]{2,1,0:T(8,128)S(1)}) custom-call(s32[3,4]{1,0:T(4,128)S(1)} %copy-done.4, bf16[304,256]{1,0:T(8,128)(2,1)S(1)} %get-tuple-element.24.si_ref.inner_ref, bf16[304,256]{1,0:T(8,128)(2,1)S(1)} %get-tuple-element.25.so_ref.outer_ref, ...), custom_call_target="tpu_custom_call", output_to_operand_aliasing={{1}: (6, {})} | custom-call | flops 838860800 | bytes 5242880 | tf_op jit(solution)/shard_map/pallas_call | solution.py:371
  45.3 0.0 collective-permute-done.5.xq_ref
  45.3 1.3 %shard_map.74 = (bf16[256,256]{1,0:T(8,128)(2,1)S(1)}, bf16[1024,256]{1,0:T(8,128)(2,1)S(1)}, f32[4,256,256]{2,1,0:T(8,128)S(1)}) custom-call(s32[3,4]{1,0:T(4,128)S(1)} %copy-done.4, bf16[256,256]{1,0:T(8,128)(2,1)S(1)} %get-tuple-element.29.rows_ref, bf16[256,256]{1,0:T(8,128)(2,1)S(1)} %collective-permute-done.5.xq_ref, ...), custom_call_target="tpu_custom_call", output_to_operand_aliasing={{2}: (5, {})} | custom-call | flops 100663296 | bytes 6815744 | tf_op jit(solution)/shard_map/pallas_call | solution.py:375
  46.7 23.3 %all_to_all.15.in_ref = bf16[64,16,256]{2,1,0:T(8,128)(2,1)S(1)} all-to-all(bf16[64,16,256]{2,1,0:T(8,128)(2,1)S(1)} %bitcast.2), channel_id=1, replica_groups=mesh['xh'=2,'y'=4,'c'=2,'xl'=2,'zh'=8,'zl'=2] {'xh','y','c','xl','zl'}, dimensions={0} | all-to-all | bytes 1048576 | tf_op jit(solution)/shard_map/all_to_all | solution.py:313
  69.9 0.1 shard_map.76
  70.0 18.7 %all_to_all.16.in_ref = bf16[8,16,256]{2,1,0:T(8,128)(2,1)S(1)} all-to-all(bf16[8,16,256]{2,1,0:T(8,128)(2,1)S(1)} %shard_map.76), channel_id=1, replica_groups=mesh['xh'=2,'y'=4,'c'=2,'xl'=2,'zh'=8,'zl'=2] {'zh'}, dimensions={0} | all-to-all | bytes 131072 | tf_op jit(solution)/shard_map/all_to_all | solution.py:314
  88.7 0.8 shard_map.77
  89.5 6.1 %all-to-all-start.2 = ((bf16[64,16,256]{2,1,0:T(8,128)(2,1)}), bf16[64,16,256]{2,1,0:T(8,128)(2,1)S(1)}, u32[]{:S(2)}, u32[]{:S(2)}) async-start(bf16[64,16,256]{2,1,0:T(8,128)(2,1)} %shard_map.77), calls=%async_computation.2 | async-start | bytes 1048576 | tf_op jit(solution)/shard_map/all_to_all | solution.py:315
  95.6 3.3 %collective-permute-start.4 = (bf16[256,256]{1,0:T(8,128)(2,1)S(1)}, bf16[256,256]{1,0:T(8,128)(2,1)S(1)}, u32[]{:S(2)}, u32[]{:S(2)}) collective-permute-start(bf16[256,256]{1,0:T(8,128)(2,1)S(1)} %get-tuple-element.30.mapped_ref), channel_id=1, source_target_pairs={{0,1},{1,2},{2,3},{3,4},{4,5},{5,6},{6,7},{7,8},{8,9},{9,10},{10,1... | collective-permute-start | bytes 393224 | tf_op jit(solution)/shard_map/ppermute | solution.py:29
  98.9 5.9 %collective-permute-done.4.far_ref = bf16[256,256]{1,0:T(8,128)(2,1)S(1)} collective-permute-done((bf16[256,256]{1,0:T(8,128)(2,1)S(1)}, bf16[256,256]{1,0:T(8,128)(2,1)S(1)}, u32[]{:S(2)}, u32[]{:S(2)}) %collective-permute-start.4) | collective-permute-done | bytes 131104 | tf_op jit(solution)/shard_map/ppermute | solution.py:29
  104.7 2.6 %shard_map.75 = f32[256,256]{1,0:T(8,128)} custom-call(s32[3,4]{1,0:T(4,128)S(1)} %copy-done.4, bf16[256,256]{1,0:T(8,128)(2,1)S(1)} %get-tuple-element.29.rows_ref, bf16[256,256]{1,0:T(8,128)(2,1)S(1)} %collective-permute-done.4.far_ref, bf16[304,256]{1,0:T(8,128)(2,1)S(1)} %collective-permute-done.gi_ref, ...), custom_call_target="tpu_custom_call" | custom-call | flops 905969664 | bytes 1048576 | tf_op jit(solution)/shard_map/pallas_call | solution.py:379
  107.4 1.9 %all-to-all-done.2 = bf16[64,16,256]{2,1,0:T(8,128)(2,1)S(1)} async-done(((bf16[64,16,256]{2,1,0:T(8,128)(2,1)}), bf16[64,16,256]{2,1,0:T(8,128)(2,1)S(1)}, u32[]{:S(2)}, u32[]{:S(2)}) %all-to-all-start.2) | async-done | bytes 524320 | tf_op jit(solution)/shard_map/all_to_all | solution.py:315
  109.2 1.1 %convert_multiply_fusion = f32[64,16,256]{2,1,0:T(8,128)} fusion(bf16[64,16,256]{2,1,0:T(8,128)(2,1)S(1)} %all-to-all-done.2), kind=kLoop, calls=%fused_computation | loop fusion | flops 524288 | bytes 1572864 | tf_op jit(solution)/shard_map/div | solution.py:385
  (13 shorter events, 0.0 us)
Async XLA Ops:
  0.6 18.9 %copy-start.2 = (s32[3,6144]{1,0:T(4,128)S(1)}, s32[3,6144]{1,0:T(4,128)}, u32[]{:S(2)}) copy-start(s32[3,6144]{1,0:T(4,128)} %src_hbm.3) | copy-start | bytes 221188
  0.6 18.9 %copy-start.3 = (s32[3,6144]{1,0:T(4,128)S(1)}, s32[3,6144]{1,0:T(4,128)}, u32[]{:S(2)}) copy-start(s32[3,6144]{1,0:T(4,128)} %dst_hbm.3) | copy-start | bytes 221188
  3.9 18.8 %collective-permute-start = (bf16[304,256]{1,0:T(8,128)(2,1)}, bf16[304,256]{1,0:T(8,128)(2,1)S(1)}, u32[]{:S(2)}, u32[]{:S(2)}) collective-permute-start(bf16[304,256]{1,0:T(8,128)(2,1)} %get-tuple-element.20.inner_ref.si_ref.inner0_ref), channel_id=1, source_target_pairs={{0,1},{1,0},{2,3},{3,2},{4,5},{5,4},{6,7},{7,6},{8,9},{9,8},{10,11... | collective-permute-start | bytes 466952 | tf_op jit(solution)/shard_map/ppermute | solution.py:33
  8.2 14.9 %copy-start = (f32[4,256,256]{2,1,0:T(8,128)S(1)}, f32[4,256,256]{2,1,0:T(8,128)}, u32[]{:S(2)}) copy-start(f32[4,256,256]{2,1,0:T(8,128)} %rel_ref.5) | copy-start | bytes 3145732
  8.2 14.9 %copy-start.1 = (f32[256,256]{1,0:T(8,128)S(1)}, f32[256,256]{1,0:T(8,128)}, u32[]{:S(2)}) copy-start(f32[256,256]{1,0:T(8,128)} %x_ref.1) | copy-start | bytes 786436
  8.3 14.9 %collective-permute-start.1 = (bf16[304,256]{1,0:T(8,128)(2,1)}, bf16[304,256]{1,0:T(8,128)(2,1)S(1)}, u32[]{:S(2)}, u32[]{:S(2)}) collective-permute-start(bf16[304,256]{1,0:T(8,128)(2,1)} %get-tuple-element.21.outer_ref.so_ref.outer0_ref), channel_id=1, source_target_pairs={{0,31},{1,2},{2,1},{3,4},{4,3},{5,6},{6,5},{7,8},{8,7},{9,10},{10,... | collective-permute-start | bytes 466952 | tf_op jit(solution)/shard_map/ppermute | solution.py:39
  19.6 0.9 copy-start.5
  20.5 0.9 copy-start.7
  22.7 0.7 copy-start.4
  25.7 8.1 %collective-permute-start.2 = (bf16[304,256]{1,0:T(8,128)(2,1)S(1)}, bf16[304,256]{1,0:T(8,128)(2,1)S(1)}, u32[]{:S(2)}, u32[]{:S(2)}) collective-permute-start(bf16[304,256]{1,0:T(8,128)(2,1)S(1)} %get-tuple-element.24.si_ref.inner_ref), channel_id=1, source_target_pairs={{0,32},{32,0},{64,96},{96,64},{128,160},{160,128},{192,224},{224,1... | collective-permute-start | bytes 466952 | tf_op jit(solution)/shard_map/ppermute | solution.py:33
  29.0 6.5 %collective-permute-start.3 = (bf16[304,256]{1,0:T(8,128)(2,1)S(1)}, bf16[304,256]{1,0:T(8,128)(2,1)S(1)}, u32[]{:S(2)}, u32[]{:S(2)}) collective-permute-start(bf16[304,256]{1,0:T(8,128)(2,1)S(1)} %get-tuple-element.25.so_ref.outer_ref), channel_id=1, source_target_pairs={{0,480},{32,64},{64,32},{96,128},{128,96},{160,192},{192,160},{224... | collective-permute-start | bytes 466952 | tf_op jit(solution)/shard_map/ppermute | solution.py:39
  35.6 7.8 %copy-start.6 = (bf16[304,256]{1,0:T(8,128)(2,1)S(1)}, bf16[304,256]{1,0:T(8,128)(2,1)}, u32[]{:S(2)}) copy-start(bf16[304,256]{1,0:T(8,128)(2,1)} %get-tuple-element.20.inner_ref.si_ref.inner0_ref) | copy-start | bytes 466948
  35.6 7.9 %copy-start.8 = (bf16[304,256]{1,0:T(8,128)(2,1)S(1)}, bf16[304,256]{1,0:T(8,128)(2,1)}, u32[]{:S(2)}) copy-start(bf16[304,256]{1,0:T(8,128)(2,1)} %get-tuple-element.21.outer_ref.so_ref.outer0_ref) | copy-start | bytes 466948
  37.9 7.4 %collective-permute-start.5 = (bf16[256,256]{1,0:T(8,128)(2,1)S(1)}, bf16[256,256]{1,0:T(8,128)(2,1)S(1)}, u32[]{:S(2)}, u32[]{:S(2)}) collective-permute-start(bf16[256,256]{1,0:T(8,128)(2,1)S(1)} %get-tuple-element.29.rows_ref), channel_id=1, source_target_pairs={{0,31},{1,0},{2,1},{3,2},{4,3},{5,4},{6,5},{7,6},{8,7},{9,8},{10,9... | collective-permute-start | bytes 393224 | tf_op jit(solution)/shard_map/ppermute | solution.py:29
  89.5 19.7 %all-to-all-start.2 = ((bf16[64,16,256]{2,1,0:T(8,128)(2,1)}), bf16[64,16,256]{2,1,0:T(8,128)(2,1)S(1)}, u32[]{:S(2)}, u32[]{:S(2)}) async-start(bf16[64,16,256]{2,1,0:T(8,128)(2,1)} %shard_map.77), calls=%async_computation.2 | async-start | bytes 1048576 | tf_op jit(solution)/shard_map/all_to_all | solution.py:315
  95.6 9.2 %collective-permute-start.4 = (bf16[256,256]{1,0:T(8,128)(2,1)S(1)}, bf16[256,256]{1,0:T(8,128)(2,1)S(1)}, u32[]{:S(2)}, u32[]{:S(2)}) collective-permute-start(bf16[256,256]{1,0:T(8,128)(2,1)S(1)} %get-tuple-element.30.mapped_ref), channel_id=1, source_target_pairs={{0,1},{1,2},{2,3},{3,4},{4,5},{5,6},{6,7},{7,8},{8,9},{9,10},{10,1... | collective-permute-start | bytes 393224 | tf_op jit(solution)/shard_map/ppermute | solution.py:29

commit v2 on v1

--- a/solution.py
+++ b/solution.py
@@ -12,8 +12,8 @@
 AXES = ("xh", "y", "c", "xl", "zh", "zl")
 GX = ("xh", "y", "c")
 GY = ("xl", "zh", "zl")
-NEAR = ("xh", "y", "c", "xl", "zl")
-FAR = "zh"
+NEAR = ("xh", "y", "c", "xl")
+FAR = ("zh", "zl")
 LEARN_RATE = 0.5
 FIRST_GRANT = 60 * 1024 * 1024 - 320 * 1024
 VMEM = pl.BlockSpec(memory_space=pltpu.VMEM)
@@ -198,35 +198,26 @@
     put(even, rows_b, mapped, inner_ref, outer_ref, slice(0, size))
 
 
-def first_window_kernel(src_hbm, dst_hbm, inner_ref, outer_ref, c_ref, near_ref, src_ref, dst_ref, sems):
-    copies = fetched([(src_hbm, src_ref), (dst_hbm, dst_ref)], sems)
-    size = c_ref.shape[0]
-    _, ends = sent(is_even(GY[-1]), inner_ref, outer_ref, slice(size, inner_ref.shape[0]))
-    c_ref[...] = own_count(ends.astype(F32), size)
-    for copy in copies:
+def first_window_kernel(src_hbm, dst_hbm, *refs):
+    *out_refs, src_ref, dst_ref, sems = refs
+    near_ref = out_refs.pop()
+    for copy in fetched([(src_hbm, src_ref), (dst_hbm, dst_ref)], sems):
         copy.wait()
-    near_ref[...] = folded_both(src_ref, dst_ref, 1, near_ref.shape[1])
-
-
-def second_window_kernel(
-    ids_ref, inner_ref, outer_ref, h_ref, ends_ref, c_ref, acc_ref
-):
-    size = h_ref.shape[0]
+    size = out_refs[0].shape[0]
+    for turn, out_ref in enumerate(out_refs):
+        ends = folded_both(src_ref, dst_ref, turn, size)
+        if turn == 1:
+            near_ref[...] = ends
+        out_ref[...] = own_count(ends.astype(F32), size)
+
+
+def relation_kernel(ids_ref, si0_ref, so0_ref, h0_ref, si1_ref, so1_ref, h1_ref, acc_ref):
+    top = slice(0, h0_ref.shape[0])
     acc_ref[...] = jnp.zeros_like(acc_ref)
-    rows_b, _ = sent(is_even(GY[-1]), inner_ref, outer_ref, slice(0, size))
-    add_relation(acc_ref, rows_b, h_ref[...], ids_ref, 0)
-    c_ref[...] = own_count(ends_ref[...].astype(F32), size)
-
-
-def third_window_kernel(
-    ids_ref, inner_ref, outer_ref, h_ref, inner0_ref, outer0_ref, acc_in_ref, c_ref, acc_ref
-):
-    size = h_ref.shape[0]
-    acc_ref[...] = acc_in_ref[...]
-    rows_b, _ = sent(is_even(GX[-1]), inner_ref, outer_ref, slice(0, size))
-    add_relation(acc_ref, rows_b, h_ref[...], ids_ref, 1)
-    ends, _ = sent(is_even(GY[-1]), inner0_ref, outer0_ref, slice(size, inner0_ref.shape[0]))
-    c_ref[...] = own_count(ends.astype(F32), size)
+    rows_b, _ = sent(is_even(GY[-1]), si0_ref, so0_ref, top)
+    add_relation(acc_ref, rows_b, h0_ref[...], ids_ref, 0)
+    rows_b, _ = sent(is_even(GX[-1]), si1_ref, so1_ref, top)
+    add_relation(acc_ref, rows_b, h1_ref[...], ids_ref, 1)
 
 
 def stepped(turn, axis, ids_ref, sent_refs, got_refs, c_ref, x_ref, rel_ref, xn_ref, h_ref):
@@ -311,7 +302,8 @@
     near = lax.axis_size(NEAR)
     far = lax.axis_size(FAR)
     part = lax.all_to_all(payload.reshape(near, rows // near, width), NEAR, 0, 0)
-    part = lax.all_to_all(summed_for(part, far), FAR, 0, 0)
+    part = summed_for(part, far)
+    part = lax.all_to_all(part, FAR, 0, 0)
     part = lax.all_to_all(summed_for(part, near), NEAR, 0, 0)
     return part.reshape(rows, width).astype(F32)
 
@@ -347,35 +339,31 @@
     )(rel_ids, entity, relations, edge_src, edge_dst)
 
     got0 = exchanged(0, *sent0)
-    c, ends1 = call(
-        first_window_kernel, [f_count, b_ends], [HBM] * 2 + [VMEM] * 2, counting,
+    c0, c1, c2, ends1 = call(
+        first_window_kernel, [f_count] * turns + [b_ends], [HBM] * 2, turns * counting,
         scratch=edge_scratch + [pltpu.SemaphoreType.DMA((2,))],
-    )(edge_src, edge_dst, *sent0)
+    )(edge_src, edge_dst)
     x1, h0, *sent1 = call(
         first_round_kernel, [f_rows, b_rows, b_pay, b_pay],
         [SMEM] + [VMEM] * 8, 7 * square + counting,
-    )(rel_ids, *sent0, *got0, c, ends1, entity, relations)
+    )(rel_ids, *sent0, *got0, c0, ends1, entity, relations)
 
     got1 = exchanged(1, *sent1)
-    c, acc = call(
-        second_window_kernel, [f_count, f_rel], [SMEM] + [VMEM] * 4, counting + square,
-    )(rel_ids, *sent0, h0, ends1)
     x2, h1, rows2, mapped2 = call(
         second_round_kernel, [f_rows, b_rows, b_rows, b_rows],
         [SMEM] + [VMEM] * 7, 7 * square + counting,
-    )(rel_ids, *sent1, *got1, c, x1, relations)
+    )(rel_ids, *sent1, *got1, c1, x1, relations)
 
     axes, offset = buckets[2]
     xq = shifted(rows2, axes, offset)
     far = shifted(mapped2, axes, -offset)
-    c, acc = call(
-        third_window_kernel, [f_count, f_rel],
-        [SMEM] + [VMEM] * 6, counting + square, aliases={6: 1},
-    )(rel_ids, *sent1, h1, *sent0, acc)
+    acc = call(
+        relation_kernel, [f_rel], [SMEM] + [VMEM] * 6, 2 * square,
+    )(rel_ids, *sent0, h0, *sent1, h1)[0]
     h2, payload, _ = call(
         last_kernel, [b_rows, b_rel, f_rel],
         [SMEM] + [VMEM] * 5, 3 * square, aliases={5: 2},
-    )(rel_ids, rows2, xq, mapped2, c, acc)
+    )(rel_ids, rows2, xq, mapped2, c2, acc)
     x3 = call(
         finish_kernel, [f_rows], [SMEM] + [VMEM] * 7, 3 * square + counting,
     )(rel_ids, rows2, far, *got0, h2, x2, relations)[0]

time: 111 us -> 112 us (level)
  starting transfers between devices: 36.8 us -> 41.5 us
  blocking collectives: 41.9 us -> 39.4 us
  local copies, waits for them, and re-layouts: 2.03 us -> 0.04 us
  waiting for transfers between devices: 9.95 us -> 11.9 us
    all_to_all x1, starting transfers between devices: 6.06 us -> 10.5 us  [reduce_everywhere(): part = lax.all_to_all(summed_for(part, near), NEAR, 0, 0)]
    all_to_all x1, blocking collectives: 23.3 us -> 20.9 us  [reduce_everywhere(): lax.all_to_all(payload.reshape(near, rows // near, width), NEAR, 0, 0)]
    unnamed x18 -> x14, local copies, waits for them, and re-layouts: 2.03 us -> 0.04 us
    ppermute x2, waiting for transfers between devices: 2.16 us -> 4.1 us  [swapped_outer(): return lax.ppermute(value, axes, pairs)]
    ppermute x2, waiting for transfers between devices: 5.93 us -> 7.84 us  [shifted(): return lax.ppermute(value, axes, pairs)]
    all_to_all x1, waiting for transfers between devices: 1.85 us -> 0.01 us  [reduce_everywhere(): part = lax.all_to_all(summed_for(part, near), NEAR, 0, 0)]
    pallas_call x3 -> x2, Pallas kernels: 4.87 us -> 4 us  [the longest x1 2.93 us: training(): call(first_window_kernel, [f_count] * turns + [b_ends], [HBM] * 2, turns...]
  transfers between devices with their start and end apart: 7 -> 7, of which waited for: 4 -> 4; matrix products, arithmetic and copies ran while one was open for 0% -> 0% of each run, Pallas kernels for 7% -> 6%
where the time goes in v2:
time: 112 us
  starting transfers between devices  41.5 us (37%)
  blocking collectives  39.4 us (35%)
  Pallas kernels  16.8 us (15%)
  waiting for transfers between devices  11.9 us (11%)
    all_to_all x1, blocking collectives, reduce_everywhere(): lax.all_to_all(payload.reshape(near, rows // near, width), NEAR, 0, 0)  20.9 us
    all_to_all x1, blocking collectives, reduce_everywhere(): part = lax.all_to_all(part, FAR, 0, 0)  18.6 us
    ppermute x2, starting transfers between devices, swapped_outer(): return lax.ppermute(value, axes, pairs)  14.4 us
    all_to_all x1, starting transfers between devices, reduce_everywhere(): part = lax.all_to_all(summed_for(part, near), NEAR, 0, 0)  10.5 us
    ppermute x2, starting transfers between devices, shifted(): return lax.ppermute(value, axes, pairs)  8.86 us
    ppermute x2, waiting for transfers between devices, shifted(): return lax.ppermute(value, axes, pairs)  7.84 us
    ppermute x2, starting transfers between devices, swapped_inner(): lax.ppermute(value, axes, [(i, i ^ 1) for i in range(lax.axis_size(axes))])  7.8 us
    ppermute x2, waiting for transfers between devices, swapped_outer(): return lax.ppermute(value, axes, pairs)  4.1 us
  transfers between devices with their start and end apart: 7, of which 4 were waited for; matrix products, arithmetic and copies ran while one was open for 0% of the time, Pallas kernels for 6%

profile of v2, /device:TPU:1, one launch (start us, length us, event | category | flops | bytes accessed | tf_op | source)
XLA Modules:
  0.0 111.7 jit_solution(9215155407536035684)
XLA Ops:
  0.6 0.0 copy-start.4
  0.6 3.2 %shard_map.68 = (bf16[304,256]{1,0:T(8,128)(2,1)}, bf16[304,256]{1,0:T(8,128)(2,1)}) custom-call(s32[3,4]{1,0:T(4,128)} %ids_ref.11, f32[256,256]{1,0:T(8,128)} %x_ref.1, f32[4,256,256]{2,1,0:T(8,128)} %rel_ref.5, s32[3,6144]{1,0:T(4,128)} %src_hbm.3, s32[3,6144]{1,0:T(4,128)} %dst_hbm.3), custom_call_target="tpu_custom_call" | custom-call | flops 33554432 | bytes 1245184 | tf_op jit(solution)/shard_map/pallas_call | solution.py:334
  3.9 4.4 %collective-permute-start = (bf16[304,256]{1,0:T(8,128)(2,1)}, bf16[304,256]{1,0:T(8,128)(2,1)S(1)}, u32[]{:S(2)}, u32[]{:S(2)}) collective-permute-start(bf16[304,256]{1,0:T(8,128)(2,1)} %get-tuple-element.18.si_ref.si0_ref), channel_id=1, source_target_pairs={{0,1},{1,0},{2,3},{3,2},{4,5},{5,4},{6,7},{7,6},{8,9},{9,8},{10,11... | collective-permute-start | bytes 466952 | tf_op jit(solution)/shard_map/ppermute | solution.py:33
  8.2 0.0 copy-start
  8.2 0.0 copy-start.1
  8.3 0.0 copy-start.2
  8.3 0.0 copy-start.3
  8.3 11.3 %collective-permute-start.1 = (bf16[304,256]{1,0:T(8,128)(2,1)}, bf16[304,256]{1,0:T(8,128)(2,1)S(1)}, u32[]{:S(2)}, u32[]{:S(2)}) collective-permute-start(bf16[304,256]{1,0:T(8,128)(2,1)} %get-tuple-element.19.so_ref.so0_ref), channel_id=1, source_target_pairs={{0,31},{1,2},{2,1},{3,4},{4,3},{5,6},{6,5},{7,8},{8,7},{9,10},{10,... | collective-permute-start | bytes 466952 | tf_op jit(solution)/shard_map/ppermute | solution.py:39
  19.6 2.9 %shard_map.69 = (f32[256,256]{1,0:T(8,128)S(1)}, f32[256,256]{1,0:T(8,128)S(1)}, f32[256,256]{1,0:T(8,128)S(1)}, bf16[48,256]{1,0:T(8,128)(2,1)S(1)}) custom-call(s32[3,6144]{1,0:T(4,128)S(1)} %copy-done.4, s32[3,6144]{1,0:T(4,128)S(1)} %copy-done.5), custom_call_target="tpu_custom_call" | custom-call | flops 2415919104 | bytes 3244032 | tf_op jit(solution)/shard_map/pallas_call | solution.py:342
  22.5 0.0 copy-start.6
  22.5 0.0 collective-permute-done.gi_ref
  22.5 0.7 collective-permute-done.1.go_ref
  23.2 2.4 %shard_map.70 = (f32[256,256]{1,0:T(8,128)S(1)}, bf16[256,256]{1,0:T(8,128)(2,1)S(1)}, bf16[304,256]{1,0:T(8,128)(2,1)S(1)}, bf16[304,256]{1,0:T(8,128)(2,1)S(1)}) custom-call(s32[3,4]{1,0:T(4,128)S(1)} %copy-done.6, bf16[304,256]{1,0:T(8,128)(2,1)S(1)} %copy-done.2, bf16[304,256]{1,0:T(8,128)(2,1)S(1)} %copy-done.3, ...), custom_call_target="tpu_custom_call" | custom-call | flops 1040187392 | bytes 2818048 | tf_op jit(solution)/shard_map/pallas_call | solution.py:346
  25.6 3.4 %collective-permute-start.2 = (bf16[304,256]{1,0:T(8,128)(2,1)S(1)}, bf16[304,256]{1,0:T(8,128)(2,1)S(1)}, u32[]{:S(2)}, u32[]{:S(2)}) collective-permute-start(bf16[304,256]{1,0:T(8,128)(2,1)S(1)} %get-tuple-element.22.si_ref.si1_ref), channel_id=1, source_target_pairs={{0,32},{32,0},{64,96},{96,64},{128,160},{160,128},{192,224},{224,1... | collective-permute-start | bytes 466952 | tf_op jit(solution)/shard_map/ppermute | solution.py:33
  29.0 3.1 %collective-permute-start.3 = (bf16[304,256]{1,0:T(8,128)(2,1)S(1)}, bf16[304,256]{1,0:T(8,128)(2,1)S(1)}, u32[]{:S(2)}, u32[]{:S(2)}) collective-permute-start(bf16[304,256]{1,0:T(8,128)(2,1)S(1)} %get-tuple-element.23.so_ref.so1_ref), channel_id=1, source_target_pairs={{0,480},{32,64},{64,32},{96,128},{128,96},{160,192},{192,160},{224... | collective-permute-start | bytes 466952 | tf_op jit(solution)/shard_map/ppermute | solution.py:39
  32.2 0.0 collective-permute-done.2.gi_ref
  32.2 3.4 %collective-permute-done.3.go_ref = bf16[304,256]{1,0:T(8,128)(2,1)S(1)} collective-permute-done((bf16[304,256]{1,0:T(8,128)(2,1)S(1)}, bf16[304,256]{1,0:T(8,128)(2,1)S(1)}, u32[]{:S(2)}, u32[]{:S(2)}) %collective-permute-start.3) | collective-permute-done | bytes 155680 | tf_op jit(solution)/shard_map/ppermute | solution.py:39
  35.6 2.4 %shard_map.71 = (f32[256,256]{1,0:T(8,128)S(1)}, bf16[256,256]{1,0:T(8,128)(2,1)S(1)}, bf16[256,256]{1,0:T(8,128)(2,1)S(1)}, bf16[256,256]{1,0:T(8,128)(2,1)S(1)}) custom-call(s32[3,4]{1,0:T(4,128)S(1)} %copy-done.6, bf16[304,256]{1,0:T(8,128)(2,1)S(1)} %get-tuple-element.22.si_ref.si1_ref, bf16[304,256]{1,0:T(8,128)(2,1)S(1)} %get-tuple-element.23.so_ref.so1_ref, ...), custom_call_target="tpu_custom_call" | custom-call | flops 1040187392 | bytes 2621440 | tf_op jit(solution)/shard_map/pallas_call | solution.py:352
  38.0 5.5 %collective-permute-start.5 = (bf16[256,256]{1,0:T(8,128)(2,1)S(1)}, bf16[256,256]{1,0:T(8,128)(2,1)S(1)}, u32[]{:S(2)}, u32[]{:S(2)}) collective-permute-start(bf16[256,256]{1,0:T(8,128)(2,1)S(1)} %get-tuple-element.26.rows_ref), channel_id=1, source_target_pairs={{0,31},{1,0},{2,1},{3,2},{4,3},{5,4},{6,5},{7,6},{8,7},{9,8},{10,9... | collective-permute-start | bytes 393224 | tf_op jit(solution)/shard_map/ppermute | solution.py:29
  43.4 1.1 shard_map.72.acc_in_ref
  44.5 0.8 collective-permute-done.5.xq_ref
  45.4 1.3 %shard_map.73 = (bf16[256,256]{1,0:T(8,128)(2,1)S(1)}, bf16[1024,256]{1,0:T(8,128)(2,1)S(1)}, f32[4,256,256]{2,1,0:T(8,128)S(1)}) custom-call(s32[3,4]{1,0:T(4,128)S(1)} %copy-done.6, bf16[256,256]{1,0:T(8,128)(2,1)S(1)} %get-tuple-element.26.rows_ref, bf16[256,256]{1,0:T(8,128)(2,1)S(1)} %collective-permute-done.5.xq_ref, ...), custom_call_target="tpu_custom_call", output_to_operand_aliasing={{2}: (5, {})} | custom-call | flops 100663296 | bytes 6815744 | tf_op jit(solution)/shard_map/pallas_call | solution.py:363
  46.7 20.9 %all_to_all.15.in_ref = bf16[32,32,256]{2,1,0:T(8,128)(2,1)S(1)} all-to-all(bf16[32,32,256]{2,1,0:T(8,128)(2,1)S(1)} %bitcast.2), channel_id=1, replica_groups=mesh['xh'=2,'y'=4,'c'=2,'xl'=2,'zh'=8,'zl'=2] {'xh','y','c','xl'}, dimensions={0} | all-to-all | bytes 1048576 | tf_op jit(solution)/shard_map/all_to_all | solution.py:304
  67.6 0.1 shard_map.75
  67.7 18.6 %all_to_all.16.in_ref = bf16[16,32,256]{2,1,0:T(8,128)(2,1)S(1)} all-to-all(bf16[16,32,256]{2,1,0:T(8,128)(2,1)S(1)} %shard_map.75), channel_id=1, replica_groups=mesh['xh'=2,'y'=4,'c'=2,'xl'=2,'zh'=8,'zl'=2] {'zh','zl'}, dimensions={0} | all-to-all | bytes 524288 | tf_op jit(solution)/shard_map/all_to_all | solution.py:306
  86.2 0.9 shard_map.76
  87.1 10.5 %all-to-all-start.2 = ((bf16[32,32,256]{2,1,0:T(8,128)(2,1)}), bf16[32,32,256]{2,1,0:T(8,128)(2,1)S(1)}, u32[]{:S(2)}, u32[]{:S(2)}) async-start(bf16[32,32,256]{2,1,0:T(8,128)(2,1)} %shard_map.76), calls=%async_computation.2 | async-start | bytes 1048576 | tf_op jit(solution)/shard_map/all_to_all | solution.py:307
  97.6 3.4 %collective-permute-start.4 = (bf16[256,256]{1,0:T(8,128)(2,1)S(1)}, bf16[256,256]{1,0:T(8,128)(2,1)S(1)}, u32[]{:S(2)}, u32[]{:S(2)}) collective-permute-start(bf16[256,256]{1,0:T(8,128)(2,1)S(1)} %get-tuple-element.27.mapped_ref), channel_id=1, source_target_pairs={{0,1},{1,2},{2,3},{3,4},{4,5},{5,6},{6,7},{7,8},{8,9},{9,10},{10,1... | collective-permute-start | bytes 393224 | tf_op jit(solution)/shard_map/ppermute | solution.py:29
  101.0 7.0 %collective-permute-done.4.far_ref = bf16[256,256]{1,0:T(8,128)(2,1)S(1)} collective-permute-done((bf16[256,256]{1,0:T(8,128)(2,1)S(1)}, bf16[256,256]{1,0:T(8,128)(2,1)S(1)}, u32[]{:S(2)}, u32[]{:S(2)}) %collective-permute-start.4) | collective-permute-done | bytes 131104 | tf_op jit(solution)/shard_map/ppermute | solution.py:29
  108.0 2.6 %shard_map.74 = f32[256,256]{1,0:T(8,128)} custom-call(s32[3,4]{1,0:T(4,128)S(1)} %copy-done.6, bf16[256,256]{1,0:T(8,128)(2,1)S(1)} %get-tuple-element.26.rows_ref, bf16[256,256]{1,0:T(8,128)(2,1)S(1)} %collective-permute-done.4.far_ref, bf16[304,256]{1,0:T(8,128)(2,1)S(1)} %collective-permute-done.gi_ref, ...), custom_call_target="tpu_custom_call" | custom-call | flops 905969664 | bytes 1048576 | tf_op jit(solution)/shard_map/pallas_call | solution.py:367
  110.6 0.0 all-to-all-done.2
  110.6 1.1 convert_multiply_fusion
  (8 shorter events, 0.0 us)
Async XLA Ops:
  0.6 18.9 %copy-start.4 = (s32[3,6144]{1,0:T(4,128)S(1)}, s32[3,6144]{1,0:T(4,128)}, u32[]{:S(2)}) copy-start(s32[3,6144]{1,0:T(4,128)} %src_hbm.3) | copy-start | bytes 221188
  0.6 18.9 %copy-start.5 = (s32[3,6144]{1,0:T(4,128)S(1)}, s32[3,6144]{1,0:T(4,128)}, u32[]{:S(2)}) copy-start(s32[3,6144]{1,0:T(4,128)} %dst_hbm.3) | copy-start | bytes 221188
  3.9 18.7 %collective-permute-start = (bf16[304,256]{1,0:T(8,128)(2,1)}, bf16[304,256]{1,0:T(8,128)(2,1)S(1)}, u32[]{:S(2)}, u32[]{:S(2)}) collective-permute-start(bf16[304,256]{1,0:T(8,128)(2,1)} %get-tuple-element.18.si_ref.si0_ref), channel_id=1, source_target_pairs={{0,1},{1,0},{2,3},{3,2},{4,5},{5,4},{6,7},{7,6},{8,9},{9,8},{10,11... | collective-permute-start | bytes 466952 | tf_op jit(solution)/shard_map/ppermute | solution.py:33
  8.2 15.0 %copy-start = (f32[4,256,256]{2,1,0:T(8,128)S(1)}, f32[4,256,256]{2,1,0:T(8,128)}, u32[]{:S(2)}) copy-start(f32[4,256,256]{2,1,0:T(8,128)} %rel_ref.5) | copy-start | bytes 3145732
  8.2 15.0 %copy-start.1 = (f32[256,256]{1,0:T(8,128)S(1)}, f32[256,256]{1,0:T(8,128)}, u32[]{:S(2)}) copy-start(f32[256,256]{1,0:T(8,128)} %x_ref.1) | copy-start | bytes 786436
  8.3 15.0 %copy-start.2 = (bf16[304,256]{1,0:T(8,128)(2,1)S(1)}, bf16[304,256]{1,0:T(8,128)(2,1)}, u32[]{:S(2)}) copy-start(bf16[304,256]{1,0:T(8,128)(2,1)} %get-tuple-element.18.si_ref.si0_ref) | copy-start | bytes 466948
  8.3 14.9 %copy-start.3 = (bf16[304,256]{1,0:T(8,128)(2,1)S(1)}, bf16[304,256]{1,0:T(8,128)(2,1)}, u32[]{:S(2)}) copy-start(bf16[304,256]{1,0:T(8,128)(2,1)} %get-tuple-element.19.so_ref.so0_ref) | copy-start | bytes 466948
  8.3 14.9 %collective-permute-start.1 = (bf16[304,256]{1,0:T(8,128)(2,1)}, bf16[304,256]{1,0:T(8,128)(2,1)S(1)}, u32[]{:S(2)}, u32[]{:S(2)}) collective-permute-start(bf16[304,256]{1,0:T(8,128)(2,1)} %get-tuple-element.19.so_ref.so0_ref), channel_id=1, source_target_pairs={{0,31},{1,2},{2,1},{3,4},{4,3},{5,6},{6,5},{7,8},{8,7},{9,10},{10,... | collective-permute-start | bytes 466952 | tf_op jit(solution)/shard_map/ppermute | solution.py:39
  22.5 0.7 copy-start.6
  25.6 6.6 %collective-permute-start.2 = (bf16[304,256]{1,0:T(8,128)(2,1)S(1)}, bf16[304,256]{1,0:T(8,128)(2,1)S(1)}, u32[]{:S(2)}, u32[]{:S(2)}) collective-permute-start(bf16[304,256]{1,0:T(8,128)(2,1)S(1)} %get-tuple-element.22.si_ref.si1_ref), channel_id=1, source_target_pairs={{0,32},{32,0},{64,96},{96,64},{128,160},{160,128},{192,224},{224,1... | collective-permute-start | bytes 466952 | tf_op jit(solution)/shard_map/ppermute | solution.py:33
  29.0 6.5 %collective-permute-start.3 = (bf16[304,256]{1,0:T(8,128)(2,1)S(1)}, bf16[304,256]{1,0:T(8,128)(2,1)S(1)}, u32[]{:S(2)}, u32[]{:S(2)}) collective-permute-start(bf16[304,256]{1,0:T(8,128)(2,1)S(1)} %get-tuple-element.23.so_ref.so1_ref), channel_id=1, source_target_pairs={{0,480},{32,64},{64,32},{96,128},{128,96},{160,192},{192,160},{224... | collective-permute-start | bytes 466952 | tf_op jit(solution)/shard_map/ppermute | solution.py:39
  38.0 7.4 %collective-permute-start.5 = (bf16[256,256]{1,0:T(8,128)(2,1)S(1)}, bf16[256,256]{1,0:T(8,128)(2,1)S(1)}, u32[]{:S(2)}, u32[]{:S(2)}) collective-permute-start(bf16[256,256]{1,0:T(8,128)(2,1)S(1)} %get-tuple-element.26.rows_ref), channel_id=1, source_target_pairs={{0,31},{1,0},{2,1},{3,2},{4,3},{5,4},{6,5},{7,6},{8,7},{9,8},{10,9... | collective-permute-start | bytes 393224 | tf_op jit(solution)/shard_map/ppermute | solution.py:29
  87.1 23.5 %all-to-all-start.2 = ((bf16[32,32,256]{2,1,0:T(8,128)(2,1)}), bf16[32,32,256]{2,1,0:T(8,128)(2,1)S(1)}, u32[]{:S(2)}, u32[]{:S(2)}) async-start(bf16[32,32,256]{2,1,0:T(8,128)(2,1)} %shard_map.76), calls=%async_computation.2 | async-start | bytes 1048576 | tf_op jit(solution)/shard_map/all_to_all | solution.py:307
  97.6 10.4 %collective-permute-start.4 = (bf16[256,256]{1,0:T(8,128)(2,1)S(1)}, bf16[256,256]{1,0:T(8,128)(2,1)S(1)}, u32[]{:S(2)}, u32[]{:S(2)}) collective-permute-start(bf16[256,256]{1,0:T(8,128)(2,1)S(1)} %get-tuple-element.27.mapped_ref), channel_id=1, source_target_pairs={{0,1},{1,2},{2,3},{3,4},{4,5},{5,6},{6,7},{7,8},{8,9},{9,10},{10,1... | collective-permute-start | bytes 393224 | tf_op jit(solution)/shard_map/ppermute | solution.py:29

commit v3 on v2

--- a/solution.py
+++ b/solution.py
@@ -15,7 +15,6 @@
 NEAR = ("xh", "y", "c", "xl")
 FAR = ("zh", "zl")
 LEARN_RATE = 0.5
-FIRST_GRANT = 60 * 1024 * 1024 - 320 * 1024
 VMEM = pl.BlockSpec(memory_space=pltpu.VMEM)
 SMEM = pl.BlockSpec(memory_space=pltpu.SMEM)
 HBM = pl.BlockSpec(memory_space=pltpu.HBM)
@@ -51,7 +50,7 @@
     return lax.dot_general(left, right, (((0,), (0,)), ((), ())), preferred_element_type=F32)
 
 
-def call(kernel, outs, in_specs, flops, aliases=None, scratch=(), grant=16 * 2**20):
+def call(kernel, outs, in_specs, flops, aliases=None, scratch=()):
     moved = sum(math.prod(o.shape) * o.dtype.itemsize for o in outs)
     return pl.pallas_call(
         kernel,
@@ -60,7 +59,7 @@
         out_specs=tuple(VMEM for _ in outs),
         scratch_shapes=list(scratch),
         input_output_aliases=aliases or {},
-        compiler_params=pltpu.CompilerParams(vmem_limit_bytes=grant),
+        compiler_params=pltpu.CompilerParams(vmem_limit_bytes=16 * 2**20),
         cost_estimate=pl.CostEstimate(
             flops=flops, bytes_accessed=4 * moved, transcendentals=0
         ),
@@ -173,6 +172,10 @@
     return jnp.where(even, outer, inner), jnp.where(even, inner, outer)
 
 
+def in_hbm(*values):
+    return [pltpu.with_memory_space_constraint(value, pltpu.HBM) for value in values]
+
+
 def folded_both(src_ref, dst_ref, turn, width):
     return jnp.concatenate(
         [folded(src_ref, turn, width), folded(dst_ref, turn, width)], axis=0
@@ -180,12 +183,17 @@
 
 
 def prepare_kernel(
-    ids_ref, x_hbm, rel_hbm, src_hbm, dst_hbm, inner_ref, outer_ref, x_ref, rel_ref, src_ref, dst_ref, sems
+    ids_hbm, x_hbm, rel_hbm, src_hbm, dst_hbm, inner_ref, outer_ref,
+    ids_ref, x_ref, rel_ref, src_ref, dst_ref, sems,
 ):
     size, width = x_ref.shape
     even = is_even(GY[-1])
     copies = fetched(
-        [(src_hbm, src_ref), (dst_hbm, dst_ref), (x_hbm, x_ref), (rel_hbm, rel_ref)], sems
+        [
+            (src_hbm, src_ref), (dst_hbm, dst_ref), (x_hbm, x_ref), (rel_hbm, rel_ref),
+            (ids_hbm, ids_ref),
+        ],
+        sems,
     )
     copies[0].wait()
     copies[1].wait()
@@ -194,6 +202,7 @@
     copies[2].wait()
     rows_b = x_ref[...].astype(BF16)
     copies[3].wait()
+    copies[4].wait()
     mapped = map_rows(rows_b, rel_ref, ids_ref, 0)
     put(even, rows_b, mapped, inner_ref, outer_ref, slice(0, size))
 
@@ -332,17 +341,16 @@
         return inner_got, outer_got
 
     sent0 = call(
-        prepare_kernel, [b_pay, b_pay], [SMEM] + [HBM] * 4, square,
-        scratch=[pltpu.VMEM(entity.shape, F32), pltpu.VMEM(relations.shape, F32)]
-        + edge_scratch + [pltpu.SemaphoreType.DMA((4,))],
-        grant=FIRST_GRANT,
-    )(rel_ids, entity, relations, edge_src, edge_dst)
+        prepare_kernel, [b_pay, b_pay], [HBM] * 5, square,
+        scratch=[pltpu.SMEM(rel_ids.shape, jnp.int32), pltpu.VMEM(entity.shape, F32)]
+        + [pltpu.VMEM(relations.shape, F32)] + edge_scratch + [pltpu.SemaphoreType.DMA((5,))],
+    )(*in_hbm(rel_ids, entity, relations, edge_src, edge_dst))
 
     got0 = exchanged(0, *sent0)
     c0, c1, c2, ends1 = call(
         first_window_kernel, [f_count] * turns + [b_ends], [HBM] * 2, turns * counting,
         scratch=edge_scratch + [pltpu.SemaphoreType.DMA((2,))],
-    )(edge_src, edge_dst)
+    )(*in_hbm(edge_src, edge_dst))
     x1, h0, *sent1 = call(
         first_round_kernel, [f_rows, b_rows, b_pay, b_pay],
         [SMEM] + [VMEM] * 8, 7 * square + counting,

time: 112 us -> 110 us (0.982)
    pallas_call x1, Pallas kernels: 3.2 us -> 1.69 us  [training(): call(prepare_kernel, [b_pay, b_pay], [HBM] * 5, square, scratch=[pltpu.SM...]
  transfers between devices with their start and end apart: 7 -> 7, of which waited for: 4 -> 3; matrix products, arithmetic and copies ran while one was open for 0% -> 0% of each run, Pallas kernels for 6% -> 7%
where the time goes in v3:
time: 110 us
  starting transfers between devices  40.7 us (37%)
  blocking collectives  39.4 us (36%)
  Pallas kernels  16 us (15%)
  waiting for transfers between devices  11.3 us (10%)
  other arithmetic  1.1 us (1%)
    all_to_all x1, blocking collectives, reduce_everywhere(): lax.all_to_all(payload.reshape(near, rows // near, width), NEAR, 0, 0)  20.9 us
    all_to_all x1, blocking collectives, reduce_everywhere(): part = lax.all_to_all(part, FAR, 0, 0)  18.6 us
    ppermute x2, starting transfers between devices, swapped_outer(): return lax.ppermute(value, axes, pairs)  14.4 us
    all_to_all x1, starting transfers between devices, reduce_everywhere(): part = lax.all_to_all(summed_for(part, near), NEAR, 0, 0)  10.5 us
    ppermute x2, starting transfers between devices, shifted(): return lax.ppermute(value, axes, pairs)  8.3 us
    ppermute x2, waiting for transfers between devices, shifted(): return lax.ppermute(value, axes, pairs)  7.84 us
    ppermute x2, starting transfers between devices, swapped_inner(): lax.ppermute(value, axes, [(i, i ^ 1) for i in range(lax.axis_size(axes))])  7.51 us
    pallas_call x1, Pallas kernels, training(): call(first_window_kernel, [f_count] * turns + [b_ends], [HBM] * 2, turns...  3.61 us
  transfers between devices with their start and end apart: 7, of which 3 were waited for; matrix products, arithmetic and copies ran while one was open for 0% of the time, Pallas kernels for 7%

profile of v3, /device:TPU:1, one launch (start us, length us, event | category | flops | bytes accessed | tf_op | source)
XLA Modules:
  0.0 109.9 jit_solution(12880878001593458682)
XLA Ops:
  0.6 1.7 %shard_map.68 = (bf16[304,256]{1,0:T(8,128)(2,1)S(1)}, bf16[304,256]{1,0:T(8,128)(2,1)S(1)}) custom-call(s32[3,4]{1,0:T(4,128)} %ids_ref.9, f32[256,256]{1,0:T(8,128)} %x_ref.1, f32[4,256,256]{2,1,0:T(8,128)} %rel_ref.5, s32[3,6144]{1,0:T(4,128)} %src_hbm.3, s32[3,6144]{1,0:T(4,128)} %dst_hbm.3), custom_call_target="tpu_custom_call" | custom-call | flops 33554432 | bytes 1245184 | tf_op jit(solution)/shard_map/pallas_call | solution.py:343
  2.3 4.4 %collective-permute-start = (bf16[304,256]{1,0:T(8,128)(2,1)S(1)}, bf16[304,256]{1,0:T(8,128)(2,1)S(1)}, u32[]{:S(2)}, u32[]{:S(2)}) collective-permute-start(bf16[304,256]{1,0:T(8,128)(2,1)S(1)} %get-tuple-element.18.si_ref.si0_ref), channel_id=1, source_target_pairs={{0,1},{1,0},{2,3},{3,2},{4,5},{5,4},{6,7},{7,6},{8,9},{9,8},{10,11... | collective-permute-start | bytes 466952 | tf_op jit(solution)/shard_map/ppermute | solution.py:32
  6.7 0.0 copy-start
  6.7 0.0 copy-start.1
  6.7 11.3 %collective-permute-start.1 = (bf16[304,256]{1,0:T(8,128)(2,1)S(1)}, bf16[304,256]{1,0:T(8,128)(2,1)S(1)}, u32[]{:S(2)}, u32[]{:S(2)}) collective-permute-start(bf16[304,256]{1,0:T(8,128)(2,1)S(1)} %get-tuple-element.19.so_ref.so0_ref), channel_id=1, source_target_pairs={{0,31},{1,2},{2,1},{3,4},{4,3},{5,6},{6,5},{7,8},{8,7},{9,10},{10,... | collective-permute-start | bytes 466952 | tf_op jit(solution)/shard_map/ppermute | solution.py:38
  18.0 3.6 %shard_map.69 = (f32[256,256]{1,0:T(8,128)S(1)}, f32[256,256]{1,0:T(8,128)S(1)}, f32[256,256]{1,0:T(8,128)S(1)}, bf16[48,256]{1,0:T(8,128)(2,1)S(1)}) custom-call(s32[3,6144]{1,0:T(4,128)} %src_hbm.3, s32[3,6144]{1,0:T(4,128)} %dst_hbm.3), custom_call_target="tpu_custom_call" | custom-call | flops 2415919104 | bytes 3244032 | tf_op jit(solution)/shard_map/pallas_call | solution.py:350
  21.6 0.0 copy-start.2
  21.6 0.0 collective-permute-done.gi_ref
  21.6 0.0 collective-permute-done.1.go_ref
  21.7 0.0 copy-done
  21.7 0.0 copy-done.1
  21.7 0.6 copy-done.2
  22.3 2.4 %shard_map.70 = (f32[256,256]{1,0:T(8,128)S(1)}, bf16[256,256]{1,0:T(8,128)(2,1)S(1)}, bf16[304,256]{1,0:T(8,128)(2,1)S(1)}, bf16[304,256]{1,0:T(8,128)(2,1)S(1)}) custom-call(s32[3,4]{1,0:T(4,128)S(1)} %copy-done.2, bf16[304,256]{1,0:T(8,128)(2,1)S(1)} %get-tuple-element.18.si_ref.si0_ref, bf16[304,256]{1,0:T(8,128)(2,1)S(1)} %get-tuple-element.19.so_ref.so0_ref, ...), custom_call_target="tpu_custom_call" | custom-call | flops 1040187392 | bytes 2818048 | tf_op jit(solution)/shard_map/pallas_call | solution.py:354
  24.7 3.1 %collective-permute-start.2 = (bf16[304,256]{1,0:T(8,128)(2,1)S(1)}, bf16[304,256]{1,0:T(8,128)(2,1)S(1)}, u32[]{:S(2)}, u32[]{:S(2)}) collective-permute-start(bf16[304,256]{1,0:T(8,128)(2,1)S(1)} %get-tuple-element.22.si_ref.si1_ref), channel_id=1, source_target_pairs={{0,32},{32,0},{64,96},{96,64},{128,160},{160,128},{192,224},{224,1... | collective-permute-start | bytes 466952 | tf_op jit(solution)/shard_map/ppermute | solution.py:32
  27.8 3.1 %collective-permute-start.3 = (bf16[304,256]{1,0:T(8,128)(2,1)S(1)}, bf16[304,256]{1,0:T(8,128)(2,1)S(1)}, u32[]{:S(2)}, u32[]{:S(2)}) collective-permute-start(bf16[304,256]{1,0:T(8,128)(2,1)S(1)} %get-tuple-element.23.so_ref.so1_ref), channel_id=1, source_target_pairs={{0,480},{32,64},{64,32},{96,128},{128,96},{160,192},{192,160},{224... | collective-permute-start | bytes 466952 | tf_op jit(solution)/shard_map/ppermute | solution.py:38
  30.9 0.0 collective-permute-done.2.gi_ref
  30.9 3.4 %collective-permute-done.3.go_ref = bf16[304,256]{1,0:T(8,128)(2,1)S(1)} collective-permute-done((bf16[304,256]{1,0:T(8,128)(2,1)S(1)}, bf16[304,256]{1,0:T(8,128)(2,1)S(1)}, u32[]{:S(2)}, u32[]{:S(2)}) %collective-permute-start.3) | collective-permute-done | bytes 155680 | tf_op jit(solution)/shard_map/ppermute | solution.py:38
  34.4 2.3 %shard_map.71 = (f32[256,256]{1,0:T(8,128)S(1)}, bf16[256,256]{1,0:T(8,128)(2,1)S(1)}, bf16[256,256]{1,0:T(8,128)(2,1)S(1)}, bf16[256,256]{1,0:T(8,128)(2,1)S(1)}) custom-call(s32[3,4]{1,0:T(4,128)S(1)} %copy-done.2, bf16[304,256]{1,0:T(8,128)(2,1)S(1)} %get-tuple-element.22.si_ref.si1_ref, bf16[304,256]{1,0:T(8,128)(2,1)S(1)} %get-tuple-element.23.so_ref.so1_ref, ...), custom_call_target="tpu_custom_call" | custom-call | flops 1040187392 | bytes 2621440 | tf_op jit(solution)/shard_map/pallas_call | solution.py:360
  36.7 4.9 %collective-permute-start.5 = (bf16[256,256]{1,0:T(8,128)(2,1)S(1)}, bf16[256,256]{1,0:T(8,128)(2,1)S(1)}, u32[]{:S(2)}, u32[]{:S(2)}) collective-permute-start(bf16[256,256]{1,0:T(8,128)(2,1)S(1)} %get-tuple-element.26.rows_ref), channel_id=1, source_target_pairs={{0,31},{1,0},{2,1},{3,2},{4,3},{5,4},{6,5},{7,6},{8,7},{9,8},{10,9... | collective-permute-start | bytes 393224 | tf_op jit(solution)/shard_map/ppermute | solution.py:28
  41.6 1.1 shard_map.72.acc_in_ref
  42.7 0.8 collective-permute-done.5.xq_ref
  43.6 1.3 %shard_map.73 = (bf16[256,256]{1,0:T(8,128)(2,1)S(1)}, bf16[1024,256]{1,0:T(8,128)(2,1)S(1)}, f32[4,256,256]{2,1,0:T(8,128)S(1)}) custom-call(s32[3,4]{1,0:T(4,128)S(1)} %copy-done.2, bf16[256,256]{1,0:T(8,128)(2,1)S(1)} %get-tuple-element.26.rows_ref, bf16[256,256]{1,0:T(8,128)(2,1)S(1)} %collective-permute-done.5.xq_ref, ...), custom_call_target="tpu_custom_call", output_to_operand_aliasing={{2}: (5, {})} | custom-call | flops 100663296 | bytes 6815744 | tf_op jit(solution)/shard_map/pallas_call | solution.py:371
  44.9 20.9 %all_to_all.15.in_ref = bf16[32,32,256]{2,1,0:T(8,128)(2,1)S(1)} all-to-all(bf16[32,32,256]{2,1,0:T(8,128)(2,1)S(1)} %bitcast.2), channel_id=1, replica_groups=mesh['xh'=2,'y'=4,'c'=2,'xl'=2,'zh'=8,'zl'=2] {'xh','y','c','xl'}, dimensions={0} | all-to-all | bytes 1048576 | tf_op jit(solution)/shard_map/all_to_all | solution.py:313
  65.8 0.1 shard_map.75
  65.9 18.6 %all_to_all.16.in_ref = bf16[16,32,256]{2,1,0:T(8,128)(2,1)S(1)} all-to-all(bf16[16,32,256]{2,1,0:T(8,128)(2,1)S(1)} %shard_map.75), channel_id=1, replica_groups=mesh['xh'=2,'y'=4,'c'=2,'xl'=2,'zh'=8,'zl'=2] {'zh','zl'}, dimensions={0} | all-to-all | bytes 524288 | tf_op jit(solution)/shard_map/all_to_all | solution.py:315
  84.4 0.9 shard_map.76
  85.3 10.5 %all-to-all-start.2 = ((bf16[32,32,256]{2,1,0:T(8,128)(2,1)}), bf16[32,32,256]{2,1,0:T(8,128)(2,1)S(1)}, u32[]{:S(2)}, u32[]{:S(2)}) async-start(bf16[32,32,256]{2,1,0:T(8,128)(2,1)} %shard_map.76), calls=%async_computation.2 | async-start | bytes 1048576 | tf_op jit(solution)/shard_map/all_to_all | solution.py:316
  95.8 3.4 %collective-permute-start.4 = (bf16[256,256]{1,0:T(8,128)(2,1)S(1)}, bf16[256,256]{1,0:T(8,128)(2,1)S(1)}, u32[]{:S(2)}, u32[]{:S(2)}) collective-permute-start(bf16[256,256]{1,0:T(8,128)(2,1)S(1)} %get-tuple-element.27.mapped_ref), channel_id=1, source_target_pairs={{0,1},{1,2},{2,3},{3,4},{4,5},{5,6},{6,7},{7,8},{8,9},{9,10},{10,1... | collective-permute-start | bytes 393224 | tf_op jit(solution)/shard_map/ppermute | solution.py:28
  99.2 7.0 %collective-permute-done.4.far_ref = bf16[256,256]{1,0:T(8,128)(2,1)S(1)} collective-permute-done((bf16[256,256]{1,0:T(8,128)(2,1)S(1)}, bf16[256,256]{1,0:T(8,128)(2,1)S(1)}, u32[]{:S(2)}, u32[]{:S(2)}) %collective-permute-start.4) | collective-permute-done | bytes 131104 | tf_op jit(solution)/shard_map/ppermute | solution.py:28
  106.2 2.6 %shard_map.74 = f32[256,256]{1,0:T(8,128)} custom-call(s32[3,4]{1,0:T(4,128)S(1)} %copy-done.2, bf16[256,256]{1,0:T(8,128)(2,1)S(1)} %get-tuple-element.26.rows_ref, bf16[256,256]{1,0:T(8,128)(2,1)S(1)} %collective-permute-done.4.far_ref, bf16[304,256]{1,0:T(8,128)(2,1)S(1)} %collective-permute-done.gi_ref, ...), custom_call_target="tpu_custom_call" | custom-call | flops 905969664 | bytes 1048576 | tf_op jit(solution)/shard_map/pallas_call | solution.py:375
  108.8 0.0 all-to-all-done.2
  108.8 1.1 %convert_multiply_fusion = f32[32,32,256]{2,1,0:T(8,128)} fusion(bf16[32,32,256]{2,1,0:T(8,128)(2,1)S(1)} %all-to-all-done.2), kind=kLoop, calls=%fused_computation | loop fusion | flops 524288 | bytes 1572864 | tf_op jit(solution)/shard_map/div | solution.py:381
Async XLA Ops:
  2.3 19.3 %collective-permute-start = (bf16[304,256]{1,0:T(8,128)(2,1)S(1)}, bf16[304,256]{1,0:T(8,128)(2,1)S(1)}, u32[]{:S(2)}, u32[]{:S(2)}) collective-permute-start(bf16[304,256]{1,0:T(8,128)(2,1)S(1)} %get-tuple-element.18.si_ref.si0_ref), channel_id=1, source_target_pairs={{0,1},{1,0},{2,3},{3,2},{4,5},{5,4},{6,7},{7,6},{8,9},{9,8},{10,11... | collective-permute-start | bytes 466952 | tf_op jit(solution)/shard_map/ppermute | solution.py:32
  6.7 15.0 %copy-start = (f32[4,256,256]{2,1,0:T(8,128)S(1)}, f32[4,256,256]{2,1,0:T(8,128)}, u32[]{:S(2)}) copy-start(f32[4,256,256]{2,1,0:T(8,128)} %rel_ref.5) | copy-start | bytes 3145732
  6.7 15.0 %copy-start.1 = (f32[256,256]{1,0:T(8,128)S(1)}, f32[256,256]{1,0:T(8,128)}, u32[]{:S(2)}) copy-start(f32[256,256]{1,0:T(8,128)} %x_ref.1) | copy-start | bytes 786436
  6.7 14.9 %collective-permute-start.1 = (bf16[304,256]{1,0:T(8,128)(2,1)S(1)}, bf16[304,256]{1,0:T(8,128)(2,1)S(1)}, u32[]{:S(2)}, u32[]{:S(2)}) collective-permute-start(bf16[304,256]{1,0:T(8,128)(2,1)S(1)} %get-tuple-element.19.so_ref.so0_ref), channel_id=1, source_target_pairs={{0,31},{1,2},{2,1},{3,4},{4,3},{5,6},{6,5},{7,8},{8,7},{9,10},{10,... | collective-permute-start | bytes 466952 | tf_op jit(solution)/shard_map/ppermute | solution.py:38
  21.6 0.7 copy-start.2
  24.7 6.3 %collective-permute-start.2 = (bf16[304,256]{1,0:T(8,128)(2,1)S(1)}, bf16[304,256]{1,0:T(8,128)(2,1)S(1)}, u32[]{:S(2)}, u32[]{:S(2)}) collective-permute-start(bf16[304,256]{1,0:T(8,128)(2,1)S(1)} %get-tuple-element.22.si_ref.si1_ref), channel_id=1, source_target_pairs={{0,32},{32,0},{64,96},{96,64},{128,160},{160,128},{192,224},{224,1... | collective-permute-start | bytes 466952 | tf_op jit(solution)/shard_map/ppermute | solution.py:32
  27.8 6.5 %collective-permute-start.3 = (bf16[304,256]{1,0:T(8,128)(2,1)S(1)}, bf16[304,256]{1,0:T(8,128)(2,1)S(1)}, u32[]{:S(2)}, u32[]{:S(2)}) collective-permute-start(bf16[304,256]{1,0:T(8,128)(2,1)S(1)} %get-tuple-element.23.so_ref.so1_ref), channel_id=1, source_target_pairs={{0,480},{32,64},{64,32},{96,128},{128,96},{160,192},{192,160},{224... | collective-permute-start | bytes 466952 | tf_op jit(solution)/shard_map/ppermute | solution.py:38
  36.7 6.8 %collective-permute-start.5 = (bf16[256,256]{1,0:T(8,128)(2,1)S(1)}, bf16[256,256]{1,0:T(8,128)(2,1)S(1)}, u32[]{:S(2)}, u32[]{:S(2)}) collective-permute-start(bf16[256,256]{1,0:T(8,128)(2,1)S(1)} %get-tuple-element.26.rows_ref), channel_id=1, source_target_pairs={{0,31},{1,0},{2,1},{3,2},{4,3},{5,4},{6,5},{7,6},{8,7},{9,8},{10,9... | collective-permute-start | bytes 393224 | tf_op jit(solution)/shard_map/ppermute | solution.py:28
  85.3 23.5 %all-to-all-start.2 = ((bf16[32,32,256]{2,1,0:T(8,128)(2,1)}), bf16[32,32,256]{2,1,0:T(8,128)(2,1)S(1)}, u32[]{:S(2)}, u32[]{:S(2)}) async-start(bf16[32,32,256]{2,1,0:T(8,128)(2,1)} %shard_map.76), calls=%async_computation.2 | async-start | bytes 1048576 | tf_op jit(solution)/shard_map/all_to_all | solution.py:316
  95.8 10.4 %collective-permute-start.4 = (bf16[256,256]{1,0:T(8,128)(2,1)S(1)}, bf16[256,256]{1,0:T(8,128)(2,1)S(1)}, u32[]{:S(2)}, u32[]{:S(2)}) collective-permute-start(bf16[256,256]{1,0:T(8,128)(2,1)S(1)} %get-tuple-element.27.mapped_ref), channel_id=1, source_target_pairs={{0,1},{1,2},{2,3},{3,4},{4,5},{5,6},{6,7},{7,8},{8,9},{9,10},{10,1... | collective-permute-start | bytes 393224 | tf_op jit(solution)/shard_map/ppermute | solution.py:28

commit v4 on v3

--- a/solution.py
+++ b/solution.py
@@ -1,3 +1,4 @@
+import functools
 import math
 
 import jax
@@ -12,8 +13,9 @@
 AXES = ("xh", "y", "c", "xl", "zh", "zl")
 GX = ("xh", "y", "c")
 GY = ("xl", "zh", "zl")
-NEAR = ("xh", "y", "c", "xl")
-FAR = ("zh", "zl")
+PLANE = ("xh", "y", "c", "xl")
+NEAR = PLANE + ("zl",)
+DEPTH = ("zh", "zl")
 LEARN_RATE = 0.5
 VMEM = pl.BlockSpec(memory_space=pltpu.VMEM)
 SMEM = pl.BlockSpec(memory_space=pltpu.SMEM)
@@ -90,7 +92,7 @@
     one = jnp.ones((16, count), BF16)
     zero = jnp.zeros((16, count), BF16)
     parts = [jnp.where(wide == index + BF16(16 * i), one, zero) for i in range(size // 16)]
-    return jnp.concatenate(parts, axis=0)
+    return jnp.concatenate(parts, axis=0).astype(jnp.float8_e4m3fn)
 
 
 def counted(row_of, col_of, pieces, size):
@@ -291,29 +293,32 @@
     xn_ref[...] = x_ref[...] - LEARN_RATE * grad
 
 
-def sum_kernel(in_ref, out_ref):
-    acc = in_ref[0].astype(F32)
-    for i in range(1, in_ref.shape[0]):
-        acc = acc + in_ref[i].astype(F32)
-    total = acc.astype(BF16)
-    for i in range(out_ref.shape[0]):
-        out_ref[i] = total
-
-
-def summed_for(parts, copies):
+def sum_kernel(apart, in_ref, out_ref):
+    share = in_ref.shape[1]
+    for i in range(apart):
+        acc = in_ref[i].astype(F32)
+        for j in range(i + apart, in_ref.shape[0], apart):
+            acc = acc + in_ref[j].astype(F32)
+        total = acc.astype(BF16)
+        for k in range(out_ref.shape[0]):
+            out_ref[k, i * share : (i + 1) * share, :] = total
+
+
+def summed_for(parts, copies, apart):
     count, share, width = parts.shape
-    out = jax.ShapeDtypeStruct((copies, share, width), BF16)
-    return call(sum_kernel, [out], [VMEM], count * share * width)(parts)[0]
+    out = jax.ShapeDtypeStruct((copies, apart * share, width), BF16)
+    kernel = functools.partial(sum_kernel, apart)
+    return call(kernel, [out], [VMEM], count * share * width)(parts)[0]
 
 
 def reduce_everywhere(payload):
     rows, width = payload.shape
     near = lax.axis_size(NEAR)
-    far = lax.axis_size(FAR)
     part = lax.all_to_all(payload.reshape(near, rows // near, width), NEAR, 0, 0)
-    part = summed_for(part, far)
-    part = lax.all_to_all(part, FAR, 0, 0)
-    part = lax.all_to_all(summed_for(part, near), NEAR, 0, 0)
+    part = summed_for(part, lax.axis_size(DEPTH), 1)
+    part = lax.all_to_all(part, DEPTH, 0, 0)
+    part = summed_for(part, lax.axis_size(PLANE), lax.axis_size(DEPTH[-1]))
+    part = lax.all_to_all(part, PLANE, 0, 0)
     return part.reshape(rows, width).astype(F32)
 
 

time: 110 us -> 107 us (0.973)
  starting transfers between devices: 40.7 us -> 36.8 us
  blocking collectives: 39.4 us -> 42.5 us
  Pallas kernels: 16 us -> 13.8 us
    all_to_all x1, starting transfers between devices: 10.5 us -> 5.52 us  [reduce_everywhere(): part = lax.all_to_all(part, PLANE, 0, 0)]
    all_to_all x1, blocking collectives: 20.9 us -> 23.3 us  [reduce_everywhere(): lax.all_to_all(payload.reshape(near, rows // near, width), NEAR, 0, 0)]
  transfers between devices with their start and end apart: 7 -> 7, of which waited for: 3 -> 5; matrix products, arithmetic and copies ran while one was open for 0% -> 0% of each run, Pallas kernels for 7% -> 6%
where the time goes in v4:
time: 107 us
  blocking collectives  42.5 us (40%)
  starting transfers between devices  36.8 us (34%)
  Pallas kernels  13.8 us (13%)
  waiting for transfers between devices  11.8 us (11%)
  other arithmetic  1.1 us (1%)
    all_to_all x1, blocking collectives, reduce_everywhere(): lax.all_to_all(payload.reshape(near, rows // near, width), NEAR, 0, 0)  23.3 us
    all_to_all x1, blocking collectives, reduce_everywhere(): part = lax.all_to_all(part, DEPTH, 0, 0)  19.2 us
    ppermute x2, starting transfers between devices, swapped_outer(): return lax.ppermute(value, axes, pairs)  14.4 us
    ppermute x2, starting transfers between devices, shifted(): return lax.ppermute(value, axes, pairs)  9.1 us
    ppermute x2, starting transfers between devices, swapped_inner(): lax.ppermute(value, axes, [(i, i ^ 1) for i in range(lax.axis_size(axes))])  7.8 us
    ppermute x2, waiting for transfers between devices, shifted(): return lax.ppermute(value, axes, pairs)  6.88 us
    all_to_all x1, starting transfers between devices, reduce_everywhere(): part = lax.all_to_all(part, PLANE, 0, 0)  5.52 us
    ppermute x2, waiting for transfers between devices, swapped_outer(): return lax.ppermute(value, axes, pairs)  4.08 us
  transfers between devices with their start and end apart: 7, of which 5 were waited for; matrix products, arithmetic and copies ran while one was open for 0% of the time, Pallas kernels for 6%

profile of v4, /device:TPU:1, one launch (start us, length us, event | category | flops | bytes accessed | tf_op | source)
XLA Modules:
  0.0 106.8 jit_solution(12665860182894488696)
XLA Ops:
  0.6 1.7 %shard_map.68 = (bf16[304,256]{1,0:T(8,128)(2,1)S(1)}, bf16[304,256]{1,0:T(8,128)(2,1)S(1)}) custom-call(s32[3,4]{1,0:T(4,128)} %ids_ref.9, f32[256,256]{1,0:T(8,128)} %x_ref.1, f32[4,256,256]{2,1,0:T(8,128)} %rel_ref.5, s32[3,6144]{1,0:T(4,128)} %src_hbm.3, s32[3,6144]{1,0:T(4,128)} %dst_hbm.3), custom_call_target="tpu_custom_call" | custom-call | flops 33554432 | bytes 1245184 | tf_op jit(solution)/shard_map/pallas_call | solution.py:348
  2.3 4.4 %collective-permute-start = (bf16[304,256]{1,0:T(8,128)(2,1)S(1)}, bf16[304,256]{1,0:T(8,128)(2,1)S(1)}, u32[]{:S(2)}, u32[]{:S(2)}) collective-permute-start(bf16[304,256]{1,0:T(8,128)(2,1)S(1)} %get-tuple-element.18.si_ref.si0_ref), channel_id=1, source_target_pairs={{0,1},{1,0},{2,3},{3,2},{4,5},{5,4},{6,7},{7,6},{8,9},{9,8},{10,11... | collective-permute-start | bytes 466952 | tf_op jit(solution)/shard_map/ppermute | solution.py:34
  6.7 0.0 copy-start
  6.7 0.0 copy-start.1
  6.7 11.3 %collective-permute-start.1 = (bf16[304,256]{1,0:T(8,128)(2,1)S(1)}, bf16[304,256]{1,0:T(8,128)(2,1)S(1)}, u32[]{:S(2)}, u32[]{:S(2)}) collective-permute-start(bf16[304,256]{1,0:T(8,128)(2,1)S(1)} %get-tuple-element.19.so_ref.so0_ref), channel_id=1, source_target_pairs={{0,31},{1,2},{2,1},{3,4},{4,3},{5,6},{6,5},{7,8},{8,7},{9,10},{10,... | collective-permute-start | bytes 466952 | tf_op jit(solution)/shard_map/ppermute | solution.py:40
  18.0 2.7 %shard_map.69 = (f32[256,256]{1,0:T(8,128)S(1)}, f32[256,256]{1,0:T(8,128)S(1)}, f32[256,256]{1,0:T(8,128)S(1)}, bf16[48,256]{1,0:T(8,128)(2,1)S(1)}) custom-call(s32[3,6144]{1,0:T(4,128)} %src_hbm.3, s32[3,6144]{1,0:T(4,128)} %dst_hbm.3), custom_call_target="tpu_custom_call" | custom-call | flops 2415919104 | bytes 3244032 | tf_op jit(solution)/shard_map/pallas_call | solution.py:355
  20.8 0.0 copy-start.2
  20.8 0.0 collective-permute-done.gi_ref
  20.8 0.7 collective-permute-done.1.go_ref
  21.4 0.0 copy-done
  21.4 0.0 copy-done.1
  21.4 0.0 copy-done.2
  21.4 1.9 %shard_map.70 = (f32[256,256]{1,0:T(8,128)S(1)}, bf16[256,256]{1,0:T(8,128)(2,1)S(1)}, bf16[304,256]{1,0:T(8,128)(2,1)S(1)}, bf16[304,256]{1,0:T(8,128)(2,1)S(1)}) custom-call(s32[3,4]{1,0:T(4,128)S(1)} %copy-done.2, bf16[304,256]{1,0:T(8,128)(2,1)S(1)} %get-tuple-element.18.si_ref.si0_ref, bf16[304,256]{1,0:T(8,128)(2,1)S(1)} %get-tuple-element.19.so_ref.so0_ref, ...), custom_call_target="tpu_custom_call" | custom-call | flops 1040187392 | bytes 2818048 | tf_op jit(solution)/shard_map/pallas_call | solution.py:359
  23.3 3.4 %collective-permute-start.2 = (bf16[304,256]{1,0:T(8,128)(2,1)S(1)}, bf16[304,256]{1,0:T(8,128)(2,1)S(1)}, u32[]{:S(2)}, u32[]{:S(2)}) collective-permute-start(bf16[304,256]{1,0:T(8,128)(2,1)S(1)} %get-tuple-element.22.si_ref.si1_ref), channel_id=1, source_target_pairs={{0,32},{32,0},{64,96},{96,64},{128,160},{160,128},{192,224},{224,1... | collective-permute-start | bytes 466952 | tf_op jit(solution)/shard_map/ppermute | solution.py:34
  26.8 3.1 %collective-permute-start.3 = (bf16[304,256]{1,0:T(8,128)(2,1)S(1)}, bf16[304,256]{1,0:T(8,128)(2,1)S(1)}, u32[]{:S(2)}, u32[]{:S(2)}) collective-permute-start(bf16[304,256]{1,0:T(8,128)(2,1)S(1)} %get-tuple-element.23.so_ref.so1_ref), channel_id=1, source_target_pairs={{0,480},{32,64},{64,32},{96,128},{128,96},{160,192},{192,160},{224... | collective-permute-start | bytes 466952 | tf_op jit(solution)/shard_map/ppermute | solution.py:40
  29.9 0.0 collective-permute-done.2.gi_ref
  29.9 3.4 %collective-permute-done.3.go_ref = bf16[304,256]{1,0:T(8,128)(2,1)S(1)} collective-permute-done((bf16[304,256]{1,0:T(8,128)(2,1)S(1)}, bf16[304,256]{1,0:T(8,128)(2,1)S(1)}, u32[]{:S(2)}, u32[]{:S(2)}) %collective-permute-start.3) | collective-permute-done | bytes 155680 | tf_op jit(solution)/shard_map/ppermute | solution.py:40
  33.3 1.9 %shard_map.71 = (f32[256,256]{1,0:T(8,128)S(1)}, bf16[256,256]{1,0:T(8,128)(2,1)S(1)}, bf16[256,256]{1,0:T(8,128)(2,1)S(1)}, bf16[256,256]{1,0:T(8,128)(2,1)S(1)}) custom-call(s32[3,4]{1,0:T(4,128)S(1)} %copy-done.2, bf16[304,256]{1,0:T(8,128)(2,1)S(1)} %get-tuple-element.22.si_ref.si1_ref, bf16[304,256]{1,0:T(8,128)(2,1)S(1)} %get-tuple-element.23.so_ref.so1_ref, ...), custom_call_target="tpu_custom_call" | custom-call | flops 1040187392 | bytes 2621440 | tf_op jit(solution)/shard_map/pallas_call | solution.py:365
  35.2 5.5 %collective-permute-start.5 = (bf16[256,256]{1,0:T(8,128)(2,1)S(1)}, bf16[256,256]{1,0:T(8,128)(2,1)S(1)}, u32[]{:S(2)}, u32[]{:S(2)}) collective-permute-start(bf16[256,256]{1,0:T(8,128)(2,1)S(1)} %get-tuple-element.26.rows_ref), channel_id=1, source_target_pairs={{0,31},{1,0},{2,1},{3,2},{4,3},{5,4},{6,5},{7,6},{8,7},{9,8},{10,9... | collective-permute-start | bytes 393224 | tf_op jit(solution)/shard_map/ppermute | solution.py:30
  40.7 1.1 %shard_map.72.acc_in_ref = f32[4,256,256]{2,1,0:T(8,128)S(1)} custom-call(s32[3,4]{1,0:T(4,128)S(1)} %copy-done.2, bf16[304,256]{1,0:T(8,128)(2,1)S(1)} %get-tuple-element.18.si_ref.si0_ref, bf16[304,256]{1,0:T(8,128)(2,1)S(1)} %get-tuple-element.19.so_ref.so0_ref, bf16[256,256]{1,0:T(8,128)(2,1)S(1)} %get-tuple-element.29.h0_ref, ...), custom_call_target="tpu_custom_call" | custom-call | flops 67108864 | bytes 4194304 | tf_op jit(solution)/shard_map/pallas_call | solution.py:373
  41.8 0.8 collective-permute-done.5.xq_ref
  42.6 1.3 %shard_map.73 = (bf16[256,256]{1,0:T(8,128)(2,1)S(1)}, bf16[1024,256]{1,0:T(8,128)(2,1)S(1)}, f32[4,256,256]{2,1,0:T(8,128)S(1)}) custom-call(s32[3,4]{1,0:T(4,128)S(1)} %copy-done.2, bf16[256,256]{1,0:T(8,128)(2,1)S(1)} %get-tuple-element.26.rows_ref, bf16[256,256]{1,0:T(8,128)(2,1)S(1)} %collective-permute-done.5.xq_ref, ...), custom_call_target="tpu_custom_call", output_to_operand_aliasing={{2}: (5, {})} | custom-call | flops 100663296 | bytes 6815744 | tf_op jit(solution)/shard_map/pallas_call | solution.py:376
  44.0 23.3 %all_to_all.15.in_ref = bf16[64,16,256]{2,1,0:T(8,128)(2,1)S(1)} all-to-all(bf16[64,16,256]{2,1,0:T(8,128)(2,1)S(1)} %bitcast.2), channel_id=1, replica_groups=mesh['xh'=2,'y'=4,'c'=2,'xl'=2,'zh'=8,'zl'=2] {'xh','y','c','xl','zl'}, dimensions={0} | all-to-all | bytes 1048576 | tf_op jit(solution)/shard_map/all_to_all | solution.py:317
  67.2 0.1 shard_map.75
  67.3 19.2 %all_to_all.16.in_ref = bf16[16,16,256]{2,1,0:T(8,128)(2,1)S(1)} all-to-all(bf16[16,16,256]{2,1,0:T(8,128)(2,1)S(1)} %shard_map.75), channel_id=1, replica_groups=mesh['xh'=2,'y'=4,'c'=2,'xl'=2,'zh'=8,'zl'=2] {'zh','zl'}, dimensions={0} | all-to-all | bytes 262144 | tf_op jit(solution)/shard_map/all_to_all | solution.py:319
  86.5 0.9 shard_map.76
  87.4 5.5 %all-to-all-start.2 = ((bf16[32,32,256]{2,1,0:T(8,128)(2,1)}), bf16[32,32,256]{2,1,0:T(8,128)(2,1)S(1)}, u32[]{:S(2)}, u32[]{:S(2)}) async-start(bf16[32,32,256]{2,1,0:T(8,128)(2,1)} %shard_map.76), calls=%async_computation.2 | async-start | bytes 1048576 | tf_op jit(solution)/shard_map/all_to_all | solution.py:321
  92.9 3.6 %collective-permute-start.4 = (bf16[256,256]{1,0:T(8,128)(2,1)S(1)}, bf16[256,256]{1,0:T(8,128)(2,1)S(1)}, u32[]{:S(2)}, u32[]{:S(2)}) collective-permute-start(bf16[256,256]{1,0:T(8,128)(2,1)S(1)} %get-tuple-element.27.mapped_ref), channel_id=1, source_target_pairs={{0,1},{1,2},{2,3},{3,4},{4,5},{5,6},{6,7},{7,8},{8,9},{9,10},{10,1... | collective-permute-start | bytes 393224 | tf_op jit(solution)/shard_map/ppermute | solution.py:30
  96.6 6.0 %collective-permute-done.4.far_ref = bf16[256,256]{1,0:T(8,128)(2,1)S(1)} collective-permute-done((bf16[256,256]{1,0:T(8,128)(2,1)S(1)}, bf16[256,256]{1,0:T(8,128)(2,1)S(1)}, u32[]{:S(2)}, u32[]{:S(2)}) %collective-permute-start.4) | collective-permute-done | bytes 131104 | tf_op jit(solution)/shard_map/ppermute | solution.py:30
  102.6 2.3 %shard_map.74 = f32[256,256]{1,0:T(8,128)} custom-call(s32[3,4]{1,0:T(4,128)S(1)} %copy-done.2, bf16[256,256]{1,0:T(8,128)(2,1)S(1)} %get-tuple-element.26.rows_ref, bf16[256,256]{1,0:T(8,128)(2,1)S(1)} %collective-permute-done.4.far_ref, bf16[304,256]{1,0:T(8,128)(2,1)S(1)} %collective-permute-done.gi_ref, ...), custom_call_target="tpu_custom_call" | custom-call | flops 905969664 | bytes 1048576 | tf_op jit(solution)/shard_map/pallas_call | solution.py:380
  104.9 0.8 all-to-all-done.2
  105.7 1.1 %convert_multiply_fusion = f32[32,32,256]{2,1,0:T(8,128)} fusion(bf16[32,32,256]{2,1,0:T(8,128)(2,1)S(1)} %all-to-all-done.2), kind=kLoop, calls=%fused_computation | loop fusion | flops 524288 | bytes 1572864 | tf_op jit(solution)/shard_map/div | solution.py:386
Async XLA Ops:
  2.3 18.4 %collective-permute-start = (bf16[304,256]{1,0:T(8,128)(2,1)S(1)}, bf16[304,256]{1,0:T(8,128)(2,1)S(1)}, u32[]{:S(2)}, u32[]{:S(2)}) collective-permute-start(bf16[304,256]{1,0:T(8,128)(2,1)S(1)} %get-tuple-element.18.si_ref.si0_ref), channel_id=1, source_target_pairs={{0,1},{1,0},{2,3},{3,2},{4,5},{5,4},{6,7},{7,6},{8,9},{9,8},{10,11... | collective-permute-start | bytes 466952 | tf_op jit(solution)/shard_map/ppermute | solution.py:34
  6.7 14.7 %copy-start = (f32[4,256,256]{2,1,0:T(8,128)S(1)}, f32[4,256,256]{2,1,0:T(8,128)}, u32[]{:S(2)}) copy-start(f32[4,256,256]{2,1,0:T(8,128)} %rel_ref.5) | copy-start | bytes 3145732
  6.7 14.7 %copy-start.1 = (f32[256,256]{1,0:T(8,128)S(1)}, f32[256,256]{1,0:T(8,128)}, u32[]{:S(2)}) copy-start(f32[256,256]{1,0:T(8,128)} %x_ref.1) | copy-start | bytes 786436
  6.7 14.7 %collective-permute-start.1 = (bf16[304,256]{1,0:T(8,128)(2,1)S(1)}, bf16[304,256]{1,0:T(8,128)(2,1)S(1)}, u32[]{:S(2)}, u32[]{:S(2)}) collective-permute-start(bf16[304,256]{1,0:T(8,128)(2,1)S(1)} %get-tuple-element.19.so_ref.so0_ref), channel_id=1, source_target_pairs={{0,31},{1,2},{2,1},{3,4},{4,3},{5,6},{6,5},{7,8},{8,7},{9,10},{10,... | collective-permute-start | bytes 466952 | tf_op jit(solution)/shard_map/ppermute | solution.py:40
  20.8 0.7 copy-start.2
  23.3 6.6 %collective-permute-start.2 = (bf16[304,256]{1,0:T(8,128)(2,1)S(1)}, bf16[304,256]{1,0:T(8,128)(2,1)S(1)}, u32[]{:S(2)}, u32[]{:S(2)}) collective-permute-start(bf16[304,256]{1,0:T(8,128)(2,1)S(1)} %get-tuple-element.22.si_ref.si1_ref), channel_id=1, source_target_pairs={{0,32},{32,0},{64,96},{96,64},{128,160},{160,128},{192,224},{224,1... | collective-permute-start | bytes 466952 | tf_op jit(solution)/shard_map/ppermute | solution.py:34
  26.8 6.5 %collective-permute-start.3 = (bf16[304,256]{1,0:T(8,128)(2,1)S(1)}, bf16[304,256]{1,0:T(8,128)(2,1)S(1)}, u32[]{:S(2)}, u32[]{:S(2)}) collective-permute-start(bf16[304,256]{1,0:T(8,128)(2,1)S(1)} %get-tuple-element.23.so_ref.so1_ref), channel_id=1, source_target_pairs={{0,480},{32,64},{64,32},{96,128},{128,96},{160,192},{192,160},{224... | collective-permute-start | bytes 466952 | tf_op jit(solution)/shard_map/ppermute | solution.py:40
  35.2 7.4 %collective-permute-start.5 = (bf16[256,256]{1,0:T(8,128)(2,1)S(1)}, bf16[256,256]{1,0:T(8,128)(2,1)S(1)}, u32[]{:S(2)}, u32[]{:S(2)}) collective-permute-start(bf16[256,256]{1,0:T(8,128)(2,1)S(1)} %get-tuple-element.26.rows_ref), channel_id=1, source_target_pairs={{0,31},{1,0},{2,1},{3,2},{4,3},{5,4},{6,5},{7,6},{8,7},{9,8},{10,9... | collective-permute-start | bytes 393224 | tf_op jit(solution)/shard_map/ppermute | solution.py:30
  87.4 18.3 %all-to-all-start.2 = ((bf16[32,32,256]{2,1,0:T(8,128)(2,1)}), bf16[32,32,256]{2,1,0:T(8,128)(2,1)S(1)}, u32[]{:S(2)}, u32[]{:S(2)}) async-start(bf16[32,32,256]{2,1,0:T(8,128)(2,1)} %shard_map.76), calls=%async_computation.2 | async-start | bytes 1048576 | tf_op jit(solution)/shard_map/all_to_all | solution.py:321
  92.9 9.7 %collective-permute-start.4 = (bf16[256,256]{1,0:T(8,128)(2,1)S(1)}, bf16[256,256]{1,0:T(8,128)(2,1)S(1)}, u32[]{:S(2)}, u32[]{:S(2)}) collective-permute-start(bf16[256,256]{1,0:T(8,128)(2,1)S(1)} %get-tuple-element.27.mapped_ref), channel_id=1, source_target_pairs={{0,1},{1,2},{2,3},{3,4},{4,5},{5,6},{6,7},{7,8},{8,9},{9,10},{10,1... | collective-permute-start | bytes 393224 | tf_op jit(solution)/shard_map/ppermute | solution.py:30

commit v5 on v4

--- a/solution.py
+++ b/solution.py
@@ -17,8 +17,8 @@
 NEAR = PLANE + ("zl",)
 DEPTH = ("zh", "zl")
 LEARN_RATE = 0.5
+GROUPS = 4
 VMEM = pl.BlockSpec(memory_space=pltpu.VMEM)
-SMEM = pl.BlockSpec(memory_space=pltpu.SMEM)
 HBM = pl.BlockSpec(memory_space=pltpu.HBM)
 F32 = jnp.float32
 BF16 = jnp.bfloat16
@@ -68,15 +68,16 @@
     )
 
 
-def map_rows(rows_b, rel_ref, ids_ref, turn):
-    groups = ids_ref.shape[1]
-    size = rows_b.shape[0] // groups
-    parts = []
-    for g in range(groups):
-        chosen = rel_ref[ids_ref[turn, g]].astype(BF16)
-        part = slice(g * size, (g + 1) * size)
-        parts.append(dot_nn(rows_b[part, :], chosen).astype(BF16))
+def map_rows(rows_b, chosen):
+    size = rows_b.shape[0] // GROUPS
+    parts = [
+        dot_nn(rows_b[g * size : (g + 1) * size, :], chosen(g)).astype(BF16) for g in range(GROUPS)
+    ]
     return jnp.concatenate(parts, axis=0)
+
+
+def chosen_of(wsel_ref, turn):
+    return lambda g: wsel_ref[turn * GROUPS + g]
 
 
 def folded(edge_ref, turn, width):
@@ -121,13 +122,9 @@
     return ((jax.nn.sigmoid(scores) - counts) * scaling).astype(BF16)
 
 
-def source_grad(pulled_b, rel_ref, ids_ref, turn):
-    groups = ids_ref.shape[1]
-    size = pulled_b.shape[0] // groups
-    parts = []
-    for g in range(groups):
-        chosen = rel_ref[ids_ref[turn, g]].astype(BF16)
-        parts.append(dot_nt(pulled_b[g * size : (g + 1) * size, :], chosen))
+def source_grad(pulled_b, chosen):
+    size = pulled_b.shape[0] // GROUPS
+    parts = [dot_nt(pulled_b[g * size : (g + 1) * size, :], chosen(g)) for g in range(GROUPS)]
     return jnp.concatenate(parts, axis=0)
 
 
@@ -136,13 +133,13 @@
     return dot_nn(slopes_t, mapped).astype(BF16).astype(F32)
 
 
-def add_relation(acc_ref, rows_b, pulled_b, ids_ref, turn):
-    groups = ids_ref.shape[1]
-    size = pulled_b.shape[0] // groups
-    for g in range(groups):
-        part = slice(g * size, (g + 1) * size)
-        kind = ids_ref[turn, g]
-        acc_ref[kind] = acc_ref[kind] + dot_tn(rows_b[part, :], pulled_b[part, :])
+def add_relation(acc_ref, rows_b, pulled_b, kind_of_row):
+    kinds, width = acc_ref.shape[:2]
+    zero = jnp.zeros_like(pulled_b)
+    apart = [jnp.where(kind_of_row == BF16(k), pulled_b, zero) for k in range(kinds)]
+    added = dot_tn(rows_b, jnp.concatenate(apart, axis=1))
+    for k in range(kinds):
+        acc_ref[k] = acc_ref[k] + added[:, k * width : (k + 1) * width]
 
 
 def fetched(pairs, sems):
@@ -205,33 +202,46 @@
     rows_b = x_ref[...].astype(BF16)
     copies[3].wait()
     copies[4].wait()
-    mapped = map_rows(rows_b, rel_ref, ids_ref, 0)
+    mapped = map_rows(rows_b, lambda g: rel_ref[ids_ref[0, g]].astype(BF16))
     put(even, rows_b, mapped, inner_ref, outer_ref, slice(0, size))
 
 
-def first_window_kernel(src_hbm, dst_hbm, *refs):
-    *out_refs, src_ref, dst_ref, sems = refs
-    near_ref = out_refs.pop()
-    for copy in fetched([(src_hbm, src_ref), (dst_hbm, dst_ref)], sems):
-        copy.wait()
-    size = out_refs[0].shape[0]
-    for turn, out_ref in enumerate(out_refs):
+def first_window_kernel(
+    ids_hbm, rel_hbm, src_hbm, dst_hbm, c0_ref, c1_ref, c2_ref, near_ref, wsel_ref, kinds_ref,
+    ids_ref, rel_ref, src_ref, dst_ref, sems,
+):
+    copies = fetched(
+        [(src_hbm, src_ref), (dst_hbm, dst_ref), (ids_hbm, ids_ref), (rel_hbm, rel_ref)], sems
+    )
+    copies[0].wait()
+    copies[1].wait()
+    size = c0_ref.shape[0]
+    for turn, out_ref in enumerate((c0_ref, c1_ref, c2_ref)):
         ends = folded_both(src_ref, dst_ref, turn, size)
         if turn == 1:
             near_ref[...] = ends
         out_ref[...] = own_count(ends.astype(F32), size)
-
-
-def relation_kernel(ids_ref, si0_ref, so0_ref, h0_ref, si1_ref, so1_ref, h1_ref, acc_ref):
+    copies[2].wait()
+    copies[3].wait()
+    group_rows = size // GROUPS
+    for turn in range(ids_ref.shape[0]):
+        for g in range(GROUPS):
+            kind = ids_ref[turn, g]
+            wsel_ref[turn * GROUPS + g] = rel_ref[kind].astype(BF16)
+            whole = jnp.full((group_rows, kinds_ref.shape[2]), kind, jnp.int32)
+            kinds_ref[turn, g * group_rows : (g + 1) * group_rows, :] = whole.astype(F32).astype(BF16)
+
+
+def relation_kernel(kinds_ref, si0_ref, so0_ref, h0_ref, si1_ref, so1_ref, h1_ref, acc_ref):
     top = slice(0, h0_ref.shape[0])
     acc_ref[...] = jnp.zeros_like(acc_ref)
     rows_b, _ = sent(is_even(GY[-1]), si0_ref, so0_ref, top)
-    add_relation(acc_ref, rows_b, h0_ref[...], ids_ref, 0)
+    add_relation(acc_ref, rows_b, h0_ref[...], kinds_ref[0])
     rows_b, _ = sent(is_even(GX[-1]), si1_ref, so1_ref, top)
-    add_relation(acc_ref, rows_b, h1_ref[...], ids_ref, 1)
-
-
-def stepped(turn, axis, ids_ref, sent_refs, got_refs, c_ref, x_ref, rel_ref, xn_ref, h_ref):
+    add_relation(acc_ref, rows_b, h1_ref[...], kinds_ref[1])
+
+
+def stepped(turn, axis, sent_refs, got_refs, c_ref, x_ref, wsel_ref, xn_ref, h_ref):
     size = x_ref.shape[0]
     even = is_even(axis)
     top, tail = slice(0, size), slice(size, sent_refs[0].shape[0])
@@ -242,20 +252,20 @@
     h_ref[...] = pulled
     _, far_ends = got(even, *got_refs, tail)
     counts_t = far_count(far_ends.astype(F32), size)
-    grad = source_grad(pulled, rel_ref, ids_ref, turn) + target_grad(rows_b, far, counts_t)
+    grad = source_grad(pulled, chosen_of(wsel_ref, turn)) + target_grad(rows_b, far, counts_t)
     moved = x_ref[...] - LEARN_RATE * grad
     xn_ref[...] = moved
     moved_b = moved.astype(BF16)
-    return moved_b, map_rows(moved_b, rel_ref, ids_ref, turn + 1)
+    return moved_b, map_rows(moved_b, chosen_of(wsel_ref, turn + 1))
 
 
 def first_round_kernel(
-    ids_ref, si_ref, so_ref, gi_ref, go_ref, c_ref, near_ref, x_ref, rel_ref,
+    si_ref, so_ref, gi_ref, go_ref, c_ref, near_ref, x_ref, wsel_ref,
     xn_ref, h_ref, inner_ref, outer_ref,
 ):
     size = x_ref.shape[0]
     rows_b, mapped = stepped(
-        0, GY[-1], ids_ref, (si_ref, so_ref), (gi_ref, go_ref), c_ref, x_ref, rel_ref, xn_ref, h_ref
+        0, GY[-1], (si_ref, so_ref), (gi_ref, go_ref), c_ref, x_ref, wsel_ref, xn_ref, h_ref
     )
     put(is_even(GX[-1]), rows_b, mapped, inner_ref, outer_ref, slice(0, size))
     inner_ref[size:, :] = near_ref[...]
@@ -263,32 +273,32 @@
 
 
 def second_round_kernel(
-    ids_ref, si_ref, so_ref, gi_ref, go_ref, c_ref, x_ref, rel_ref,
+    si_ref, so_ref, gi_ref, go_ref, c_ref, x_ref, wsel_ref,
     xn_ref, h_ref, rows_ref, mapped_ref,
 ):
     rows_b, mapped = stepped(
-        1, GX[-1], ids_ref, (si_ref, so_ref), (gi_ref, go_ref), c_ref, x_ref, rel_ref, xn_ref, h_ref
+        1, GX[-1], (si_ref, so_ref), (gi_ref, go_ref), c_ref, x_ref, wsel_ref, xn_ref, h_ref
     )
     rows_ref[...] = rows_b
     mapped_ref[...] = mapped
 
 
-def last_kernel(ids_ref, rows_ref, xq_ref, mapped_ref, c_ref, acc_in_ref, h_ref, out_ref, acc_ref):
+def last_kernel(kinds_ref, rows_ref, xq_ref, mapped_ref, c_ref, acc_in_ref, h_ref, out_ref, acc_ref):
     slopes_b = slopes(dot_nt(mapped_ref[...], xq_ref[...]), c_ref[...])
     pulled = dot_nn(slopes_b, xq_ref[...]).astype(BF16)
     h_ref[...] = pulled
     acc_ref[...] = acc_in_ref[...]
-    add_relation(acc_ref, rows_ref, pulled, ids_ref, 2)
+    add_relation(acc_ref, rows_ref[...], pulled, kinds_ref[2])
     kinds, width = acc_ref.shape[:2]
     for k in range(kinds):
         out_ref[k * width : (k + 1) * width, :] = acc_ref[k].astype(BF16)
 
 
-def finish_kernel(ids_ref, rows_ref, far_ref, gi_ref, go_ref, h_ref, x_ref, rel_ref, xn_ref):
+def finish_kernel(rows_ref, far_ref, gi_ref, go_ref, h_ref, x_ref, wsel_ref, xn_ref):
     size = x_ref.shape[0]
     ends, _ = got(is_even(GY[-1]), gi_ref, go_ref, slice(size, gi_ref.shape[0]))
     counts_t = far_count(ends.astype(F32), size)
-    grad = source_grad(h_ref[...], rel_ref, ids_ref, 2)
+    grad = source_grad(h_ref[...], chosen_of(wsel_ref, 2))
     grad = grad + target_grad(rows_ref[...], far_ref[...], counts_t)
     xn_ref[...] = x_ref[...] - LEARN_RATE * grad
 
@@ -336,7 +346,10 @@
     f_count = jax.ShapeDtypeStruct((rows, rows), F32)
     f_rel = jax.ShapeDtypeStruct(relations.shape, F32)
     b_rel = jax.ShapeDtypeStruct((kinds * width, width), BF16)
-    edge_scratch = [pltpu.VMEM(edge_src.shape, jnp.int32)] * 2
+    first_scratch = [
+        pltpu.SMEM(rel_ids.shape, jnp.int32), pltpu.VMEM(entity.shape, F32),
+        pltpu.VMEM(relations.shape, F32),
+    ] + [pltpu.VMEM(edge_src.shape, jnp.int32)] * 2
     buckets = ((GY, 1), (GX, 1), (GY, -1))
 
     def exchanged(turn, inner, outer):
@@ -347,39 +360,39 @@
 
     sent0 = call(
         prepare_kernel, [b_pay, b_pay], [HBM] * 5, square,
-        scratch=[pltpu.SMEM(rel_ids.shape, jnp.int32), pltpu.VMEM(entity.shape, F32)]
-        + [pltpu.VMEM(relations.shape, F32)] + edge_scratch + [pltpu.SemaphoreType.DMA((5,))],
+        scratch=first_scratch + [pltpu.SemaphoreType.DMA((5,))],
     )(*in_hbm(rel_ids, entity, relations, edge_src, edge_dst))
 
     got0 = exchanged(0, *sent0)
-    c0, c1, c2, ends1 = call(
-        first_window_kernel, [f_count] * turns + [b_ends], [HBM] * 2, turns * counting,
-        scratch=edge_scratch + [pltpu.SemaphoreType.DMA((2,))],
-    )(*in_hbm(edge_src, edge_dst))
+    b_wsel = jax.ShapeDtypeStruct((turns * GROUPS, width, width), BF16)
+    b_kinds = jax.ShapeDtypeStruct((turns, rows, width), BF16)
+    c0, c1, c2, ends1, wsel, of_row = call(
+        first_window_kernel, [f_count] * turns + [b_ends, b_wsel, b_kinds], [HBM] * 4,
+        turns * counting,
+        scratch=first_scratch[:1] + first_scratch[2:] + [pltpu.SemaphoreType.DMA((4,))],
+    )(*in_hbm(rel_ids, relations, edge_src, edge_dst))
     x1, h0, *sent1 = call(
         first_round_kernel, [f_rows, b_rows, b_pay, b_pay],
-        [SMEM] + [VMEM] * 8, 7 * square + counting,
-    )(rel_ids, *sent0, *got0, c0, ends1, entity, relations)
+        [VMEM] * 8, 7 * square + counting,
+    )(*sent0, *got0, c0, ends1, entity, wsel)
 
     got1 = exchanged(1, *sent1)
     x2, h1, rows2, mapped2 = call(
         second_round_kernel, [f_rows, b_rows, b_rows, b_rows],
-        [SMEM] + [VMEM] * 7, 7 * square + counting,
-    )(rel_ids, *sent1, *got1, c1, x1, relations)
+        [VMEM] * 7, 7 * square + counting,
+    )(*sent1, *got1, c1, x1, wsel)
 
     axes, offset = buckets[2]
     xq = shifted(rows2, axes, offset)
     far = shifted(mapped2, axes, -offset)
-    acc = call(
-        relation_kernel, [f_rel], [SMEM] + [VMEM] * 6, 2 * square,
-    )(rel_ids, *sent0, h0, *sent1, h1)[0]
+    acc = call(relation_kernel, [f_rel], [VMEM] * 7, 2 * square)(of_row, *sent0, h0, *sent1, h1)[0]
     h2, payload, _ = call(
         last_kernel, [b_rows, b_rel, f_rel],
-        [SMEM] + [VMEM] * 5, 3 * square, aliases={5: 2},
-    )(rel_ids, rows2, xq, mapped2, c2, acc)
+        [VMEM] * 6, 3 * square, aliases={5: 2},
+    )(of_row, rows2, xq, mapped2, c2, acc)
     x3 = call(
-        finish_kernel, [f_rows], [SMEM] + [VMEM] * 7, 3 * square + counting,
-    )(rel_ids, rows2, far, *got0, h2, x2, relations)[0]
+        finish_kernel, [f_rows], [VMEM] * 7, 3 * square + counting,
+    )(rows2, far, *got0, h2, x2, wsel)[0]
 
     summed = reduce_everywhere(payload)
     divisor = math.sqrt(turns * lax.axis_size(AXES))

time: 107 us -> 105 us (0.981)
  Pallas kernels: 13.8 us -> 11.1 us
    pallas_call x7, Pallas kernels: 12.9 us -> 10.1 us  [the longest x1 2.95 us: training(): call(first_window_kernel, [f_count] * turns + [b_ends, b_wsel, b_kinds],...]
  transfers between devices with their start and end apart: 7 -> 7, of which waited for: 5 -> 5; matrix products, arithmetic and copies ran while one was open for 0% -> 0% of each run, Pallas kernels for 6% -> 5%
where the time goes in v5:
time: 105 us
  blocking collectives  42.5 us (40%)
  starting transfers between devices  36.8 us (35%)
  waiting for transfers between devices  12.8 us (12%)
  Pallas kernels  11.1 us (11%)
  other arithmetic  1.1 us (1%)
    all_to_all x1, blocking collectives, reduce_everywhere(): lax.all_to_all(payload.reshape(near, rows // near, width), NEAR, 0, 0)  23.3 us
    all_to_all x1, blocking collectives, reduce_everywhere(): part = lax.all_to_all(part, DEPTH, 0, 0)  19.2 us
    ppermute x2, starting transfers between devices, swapped_outer(): return lax.ppermute(value, axes, pairs)  14.4 us
    ppermute x2, starting transfers between devices, shifted(): return lax.ppermute(value, axes, pairs)  9.1 us
    ppermute x2, starting transfers between devices, swapped_inner(): lax.ppermute(value, axes, [(i, i ^ 1) for i in range(lax.axis_size(axes))])  7.8 us
    ppermute x2, waiting for transfers between devices, shifted(): return lax.ppermute(value, axes, pairs)  7.49 us
    all_to_all x1, starting transfers between devices, reduce_everywhere(): part = lax.all_to_all(part, PLANE, 0, 0)  5.52 us
    ppermute x2, waiting for transfers between devices, swapped_outer(): return lax.ppermute(value, axes, pairs)  3.9 us
  transfers between devices with their start and end apart: 7, of which 5 were waited for; matrix products, arithmetic and copies ran while one was open for 0% of the time, Pallas kernels for 5%

profile of v5, /device:TPU:1, one launch (start us, length us, event | category | flops | bytes accessed | tf_op | source)
XLA Modules:
  0.0 105.0 jit_solution(16931706812917712040)
XLA Ops:
  0.6 1.7 %shard_map.68 = (bf16[304,256]{1,0:T(8,128)(2,1)S(1)}, bf16[304,256]{1,0:T(8,128)(2,1)S(1)}) custom-call(s32[3,4]{1,0:T(4,128)} %ids_hbm.3, f32[256,256]{1,0:T(8,128)} %x_ref.1, f32[4,256,256]{2,1,0:T(8,128)} %rel_hbm.3, s32[3,6144]{1,0:T(4,128)} %src_hbm.3, s32[3,6144]{1,0:T(4,128)} %dst_hbm.3), custom_call_target="tpu_custom_call" | custom-call | flops 33554432 | bytes 1245184 | tf_op jit(solution)/shard_map/pallas_call | solution.py:361
  2.3 4.4 %collective-permute-start = (bf16[304,256]{1,0:T(8,128)(2,1)S(1)}, bf16[304,256]{1,0:T(8,128)(2,1)S(1)}, u32[]{:S(2)}, u32[]{:S(2)}) collective-permute-start(bf16[304,256]{1,0:T(8,128)(2,1)S(1)} %get-tuple-element.20.si_ref.si0_ref), channel_id=1, source_target_pairs={{0,1},{1,0},{2,3},{3,2},{4,5},{5,4},{6,7},{7,6},{8,9},{9,8},{10,11... | collective-permute-start | bytes 466952 | tf_op jit(solution)/shard_map/ppermute | solution.py:34
  6.7 0.0 copy-start
  6.7 11.3 %collective-permute-start.1 = (bf16[304,256]{1,0:T(8,128)(2,1)S(1)}, bf16[304,256]{1,0:T(8,128)(2,1)S(1)}, u32[]{:S(2)}, u32[]{:S(2)}) collective-permute-start(bf16[304,256]{1,0:T(8,128)(2,1)S(1)} %get-tuple-element.21.so_ref.so0_ref), channel_id=1, source_target_pairs={{0,31},{1,2},{2,1},{3,4},{4,3},{5,6},{6,5},{7,8},{8,7},{9,10},{10,... | collective-permute-start | bytes 466952 | tf_op jit(solution)/shard_map/ppermute | solution.py:40
  18.0 2.9 %shard_map.69 = (f32[256,256]{1,0:T(8,128)S(1)}, f32[256,256]{1,0:T(8,128)S(1)}, f32[256,256]{1,0:T(8,128)S(1)}, bf16[48,256]{1,0:T(8,128)(2,1)S(1)}, bf16[12,25...) custom-call(s32[3,4]{1,0:T(4,128)} %ids_hbm.3, f32[4,256,256]{2,1,0:T(8,128)} %rel_hbm.3, s32[3,6144]{1,0:T(4,128)} %src_hbm.3, ...), custom_call_target="tpu_custom_call" | custom-call | flops 2415919104 | bytes 11108352 | tf_op jit(solution)/shard_map/pallas_call | solution.py:369
  20.9 0.0 collective-permute-done.gi_ref
  21.0 0.5 collective-permute-done.1.go_ref
  21.4 0.0 copy-done
  21.4 1.3 %shard_map.70 = (f32[256,256]{1,0:T(8,128)S(1)}, bf16[256,256]{1,0:T(8,128)(2,1)S(1)}, bf16[304,256]{1,0:T(8,128)(2,1)S(1)}, bf16[304,256]{1,0:T(8,128)(2,1)S(1)}) custom-call(bf16[304,256]{1,0:T(8,128)(2,1)S(1)} %get-tuple-element.20.si_ref.si0_ref, bf16[304,256]{1,0:T(8,128)(2,1)S(1)} %get-tuple-element.21.so_ref.so0_ref, ...), custom_call_target="tpu_custom_call" | custom-call | flops 1040187392 | bytes 2818048 | tf_op jit(solution)/shard_map/pallas_call | solution.py:374
  22.7 3.4 %collective-permute-start.2 = (bf16[304,256]{1,0:T(8,128)(2,1)S(1)}, bf16[304,256]{1,0:T(8,128)(2,1)S(1)}, u32[]{:S(2)}, u32[]{:S(2)}) collective-permute-start(bf16[304,256]{1,0:T(8,128)(2,1)S(1)} %get-tuple-element.25.si_ref.si1_ref), channel_id=1, source_target_pairs={{0,32},{32,0},{64,96},{96,64},{128,160},{160,128},{192,224},{224,1... | collective-permute-start | bytes 466952 | tf_op jit(solution)/shard_map/ppermute | solution.py:34
  26.2 3.1 %collective-permute-start.3 = (bf16[304,256]{1,0:T(8,128)(2,1)S(1)}, bf16[304,256]{1,0:T(8,128)(2,1)S(1)}, u32[]{:S(2)}, u32[]{:S(2)}) collective-permute-start(bf16[304,256]{1,0:T(8,128)(2,1)S(1)} %get-tuple-element.26.so_ref.so1_ref), channel_id=1, source_target_pairs={{0,480},{32,64},{64,32},{96,128},{128,96},{160,192},{192,160},{224... | collective-permute-start | bytes 466952 | tf_op jit(solution)/shard_map/ppermute | solution.py:40
  29.3 0.0 collective-permute-done.2.gi_ref
  29.3 3.4 %collective-permute-done.3.go_ref = bf16[304,256]{1,0:T(8,128)(2,1)S(1)} collective-permute-done((bf16[304,256]{1,0:T(8,128)(2,1)S(1)}, bf16[304,256]{1,0:T(8,128)(2,1)S(1)}, u32[]{:S(2)}, u32[]{:S(2)}) %collective-permute-start.3) | collective-permute-done | bytes 155680 | tf_op jit(solution)/shard_map/ppermute | solution.py:40
  32.7 1.3 %shard_map.71 = (f32[256,256]{1,0:T(8,128)S(1)}, bf16[256,256]{1,0:T(8,128)(2,1)S(1)}, bf16[256,256]{1,0:T(8,128)(2,1)S(1)}, bf16[256,256]{1,0:T(8,128)(2,1)S(1)}) custom-call(bf16[304,256]{1,0:T(8,128)(2,1)S(1)} %get-tuple-element.25.si_ref.si1_ref, bf16[304,256]{1,0:T(8,128)(2,1)S(1)} %get-tuple-element.26.so_ref.so1_ref, ...), custom_call_target="tpu_custom_call" | custom-call | flops 1040187392 | bytes 2621440 | tf_op jit(solution)/shard_map/pallas_call | solution.py:380
  34.0 5.5 %collective-permute-start.5 = (bf16[256,256]{1,0:T(8,128)(2,1)S(1)}, bf16[256,256]{1,0:T(8,128)(2,1)S(1)}, u32[]{:S(2)}, u32[]{:S(2)}) collective-permute-start(bf16[256,256]{1,0:T(8,128)(2,1)S(1)} %get-tuple-element.29.rows_ref), channel_id=1, source_target_pairs={{0,31},{1,0},{2,1},{3,2},{4,3},{5,4},{6,5},{7,6},{8,7},{9,8},{10,9... | collective-permute-start | bytes 393224 | tf_op jit(solution)/shard_map/ppermute | solution.py:30
  39.5 0.5 shard_map.72.acc_in_ref
  40.0 1.5 %collective-permute-done.5.xq_ref = bf16[256,256]{1,0:T(8,128)(2,1)S(1)} collective-permute-done((bf16[256,256]{1,0:T(8,128)(2,1)S(1)}, bf16[256,256]{1,0:T(8,128)(2,1)S(1)}, u32[]{:S(2)}, u32[]{:S(2)}) %collective-permute-start.5) | collective-permute-done | bytes 131104 | tf_op jit(solution)/shard_map/ppermute | solution.py:30
  41.5 0.7 shard_map.73
  42.2 23.3 %all_to_all.15.in_ref = bf16[64,16,256]{2,1,0:T(8,128)(2,1)S(1)} all-to-all(bf16[64,16,256]{2,1,0:T(8,128)(2,1)S(1)} %bitcast.2), channel_id=1, replica_groups=mesh['xh'=2,'y'=4,'c'=2,'xl'=2,'zh'=8,'zl'=2] {'xh','y','c','xl','zl'}, dimensions={0} | all-to-all | bytes 1048576 | tf_op jit(solution)/shard_map/all_to_all | solution.py:327
  65.4 0.1 shard_map.75
  65.5 19.2 %all_to_all.16.in_ref = bf16[16,16,256]{2,1,0:T(8,128)(2,1)S(1)} all-to-all(bf16[16,16,256]{2,1,0:T(8,128)(2,1)S(1)} %shard_map.75), channel_id=1, replica_groups=mesh['xh'=2,'y'=4,'c'=2,'xl'=2,'zh'=8,'zl'=2] {'zh','zl'}, dimensions={0} | all-to-all | bytes 262144 | tf_op jit(solution)/shard_map/all_to_all | solution.py:329
  84.7 0.9 shard_map.76
  85.6 5.5 %all-to-all-start.2 = ((bf16[32,32,256]{2,1,0:T(8,128)(2,1)}), bf16[32,32,256]{2,1,0:T(8,128)(2,1)S(1)}, u32[]{:S(2)}, u32[]{:S(2)}) async-start(bf16[32,32,256]{2,1,0:T(8,128)(2,1)} %shard_map.76), calls=%async_computation.2 | async-start | bytes 1048576 | tf_op jit(solution)/shard_map/all_to_all | solution.py:331
  91.1 3.6 %collective-permute-start.4 = (bf16[256,256]{1,0:T(8,128)(2,1)S(1)}, bf16[256,256]{1,0:T(8,128)(2,1)S(1)}, u32[]{:S(2)}, u32[]{:S(2)}) collective-permute-start(bf16[256,256]{1,0:T(8,128)(2,1)S(1)} %get-tuple-element.30.mapped_ref), channel_id=1, source_target_pairs={{0,1},{1,2},{2,3},{3,4},{4,5},{5,6},{6,7},{7,8},{8,9},{9,10},{10,1... | collective-permute-start | bytes 393224 | tf_op jit(solution)/shard_map/ppermute | solution.py:30
  94.8 6.0 %collective-permute-done.4.far_ref = bf16[256,256]{1,0:T(8,128)(2,1)S(1)} collective-permute-done((bf16[256,256]{1,0:T(8,128)(2,1)S(1)}, bf16[256,256]{1,0:T(8,128)(2,1)S(1)}, u32[]{:S(2)}, u32[]{:S(2)}) %collective-permute-start.4) | collective-permute-done | bytes 131104 | tf_op jit(solution)/shard_map/ppermute | solution.py:30
  100.8 1.7 %shard_map.74 = f32[256,256]{1,0:T(8,128)} custom-call(bf16[256,256]{1,0:T(8,128)(2,1)S(1)} %get-tuple-element.29.rows_ref, bf16[256,256]{1,0:T(8,128)(2,1)S(1)} %collective-permute-done.4.far_ref, bf16[304,256]{1,0:T(8,128)(2,1)S(1)} %collective-permute-done.gi_ref, bf16[304,256]{1,0:T(8,128)(2,1)S(1)} %collective-permute-done.1.go_ref, ...), custom_call_target="tpu_custom_call" | custom-call | flops 905969664 | bytes 1048576 | tf_op jit(solution)/shard_map/pallas_call | solution.py:393
  102.5 1.4 %all-to-all-done.2 = bf16[32,32,256]{2,1,0:T(8,128)(2,1)S(1)} async-done(((bf16[32,32,256]{2,1,0:T(8,128)(2,1)}), bf16[32,32,256]{2,1,0:T(8,128)(2,1)S(1)}, u32[]{:S(2)}, u32[]{:S(2)}) %all-to-all-start.2) | async-done | bytes 524320 | tf_op jit(solution)/shard_map/all_to_all | solution.py:331
  103.9 1.1 %convert_multiply_fusion = f32[32,32,256]{2,1,0:T(8,128)} fusion(bf16[32,32,256]{2,1,0:T(8,128)(2,1)S(1)} %all-to-all-done.2), kind=kLoop, calls=%fused_computation | loop fusion | flops 524288 | bytes 1572864 | tf_op jit(solution)/shard_map/div | solution.py:399
Async XLA Ops:
  2.3 18.6 %collective-permute-start = (bf16[304,256]{1,0:T(8,128)(2,1)S(1)}, bf16[304,256]{1,0:T(8,128)(2,1)S(1)}, u32[]{:S(2)}, u32[]{:S(2)}) collective-permute-start(bf16[304,256]{1,0:T(8,128)(2,1)S(1)} %get-tuple-element.20.si_ref.si0_ref), channel_id=1, source_target_pairs={{0,1},{1,0},{2,3},{3,2},{4,5},{5,4},{6,7},{7,6},{8,9},{9,8},{10,11... | collective-permute-start | bytes 466952 | tf_op jit(solution)/shard_map/ppermute | solution.py:34
  6.7 14.7 %copy-start = (f32[256,256]{1,0:T(8,128)S(1)}, f32[256,256]{1,0:T(8,128)}, u32[]{:S(2)}) copy-start(f32[256,256]{1,0:T(8,128)} %x_ref.1) | copy-start | bytes 786436
  6.7 14.7 %collective-permute-start.1 = (bf16[304,256]{1,0:T(8,128)(2,1)S(1)}, bf16[304,256]{1,0:T(8,128)(2,1)S(1)}, u32[]{:S(2)}, u32[]{:S(2)}) collective-permute-start(bf16[304,256]{1,0:T(8,128)(2,1)S(1)} %get-tuple-element.21.so_ref.so0_ref), channel_id=1, source_target_pairs={{0,31},{1,2},{2,1},{3,4},{4,3},{5,6},{6,5},{7,8},{8,7},{9,10},{10,... | collective-permute-start | bytes 466952 | tf_op jit(solution)/shard_map/ppermute | solution.py:40
  22.7 6.6 %collective-permute-start.2 = (bf16[304,256]{1,0:T(8,128)(2,1)S(1)}, bf16[304,256]{1,0:T(8,128)(2,1)S(1)}, u32[]{:S(2)}, u32[]{:S(2)}) collective-permute-start(bf16[304,256]{1,0:T(8,128)(2,1)S(1)} %get-tuple-element.25.si_ref.si1_ref), channel_id=1, source_target_pairs={{0,32},{32,0},{64,96},{96,64},{128,160},{160,128},{192,224},{224,1... | collective-permute-start | bytes 466952 | tf_op jit(solution)/shard_map/ppermute | solution.py:34
  26.2 6.5 %collective-permute-start.3 = (bf16[304,256]{1,0:T(8,128)(2,1)S(1)}, bf16[304,256]{1,0:T(8,128)(2,1)S(1)}, u32[]{:S(2)}, u32[]{:S(2)}) collective-permute-start(bf16[304,256]{1,0:T(8,128)(2,1)S(1)} %get-tuple-element.26.so_ref.so1_ref), channel_id=1, source_target_pairs={{0,480},{32,64},{64,32},{96,128},{128,96},{160,192},{192,160},{224... | collective-permute-start | bytes 466952 | tf_op jit(solution)/shard_map/ppermute | solution.py:40
  34.0 7.4 %collective-permute-start.5 = (bf16[256,256]{1,0:T(8,128)(2,1)S(1)}, bf16[256,256]{1,0:T(8,128)(2,1)S(1)}, u32[]{:S(2)}, u32[]{:S(2)}) collective-permute-start(bf16[256,256]{1,0:T(8,128)(2,1)S(1)} %get-tuple-element.29.rows_ref), channel_id=1, source_target_pairs={{0,31},{1,0},{2,1},{3,2},{4,3},{5,4},{6,5},{7,6},{8,7},{9,8},{10,9... | collective-permute-start | bytes 393224 | tf_op jit(solution)/shard_map/ppermute | solution.py:30
  85.6 18.3 %all-to-all-start.2 = ((bf16[32,32,256]{2,1,0:T(8,128)(2,1)}), bf16[32,32,256]{2,1,0:T(8,128)(2,1)S(1)}, u32[]{:S(2)}, u32[]{:S(2)}) async-start(bf16[32,32,256]{2,1,0:T(8,128)(2,1)} %shard_map.76), calls=%async_computation.2 | async-start | bytes 1048576 | tf_op jit(solution)/shard_map/all_to_all | solution.py:331
  91.1 9.7 %collective-permute-start.4 = (bf16[256,256]{1,0:T(8,128)(2,1)S(1)}, bf16[256,256]{1,0:T(8,128)(2,1)S(1)}, u32[]{:S(2)}, u32[]{:S(2)}) collective-permute-start(bf16[256,256]{1,0:T(8,128)(2,1)S(1)} %get-tuple-element.30.mapped_ref), channel_id=1, source_target_pairs={{0,1},{1,2},{2,3},{3,4},{4,5},{5,6},{6,7},{7,8},{8,9},{9,10},{10,1... | collective-permute-start | bytes 393224 | tf_op jit(solution)/shard_map/ppermute | solution.py:30

commit v6 on v5

--- a/solution.py
+++ b/solution.py
@@ -11,6 +11,7 @@
 
 
 AXES = ("xh", "y", "c", "xl", "zh", "zl")
+CORE = "c"
 GX = ("xh", "y", "c")
 GY = ("xl", "zh", "zl")
 PLANE = ("xh", "y", "c", "xl")
@@ -30,14 +31,26 @@
     return lax.ppermute(value, axes, pairs)
 
 
-def swapped_inner(value, axes):
-    return lax.ppermute(value, axes, [(i, i ^ 1) for i in range(lax.axis_size(axes))])
-
-
-def swapped_outer(value, axes):
+def inner_partner(i, count):
+    return i ^ 1
+
+
+def outer_partner(i, count):
+    return (i + (1 if i % 2 else -1)) % count
+
+
+def swapped(value, axes, partner):
     count = lax.axis_size(axes)
-    pairs = [(i, (i + (1 if i % 2 else -1)) % count) for i in range(count)]
-    return lax.ppermute(value, axes, pairs)
+    return lax.ppermute(value, axes, [(i, partner(i, count)) for i in range(count)])
+
+
+def swapped_by_core(value, axes, partners):
+    count = lax.axis_size(axes)
+    pairs = [
+        (core * count + i, core * count + partners[core](i, count))
+        for core in range(2) for i in range(count)
+    ]
+    return lax.ppermute(value, (CORE,) + axes, pairs)
 
 
 def dot_nn(left, right):
@@ -152,8 +165,9 @@
     return copies
 
 
-def is_even(axis):
-    return lax.axis_index(axis) == 0
+def is_even(turn):
+    core = lax.axis_index(CORE)
+    return core == (0 if turn else lax.axis_index(GY[-1]))
 
 
 def put(even, rows, mapped, inner_ref, outer_ref, part):
@@ -186,7 +200,7 @@
     ids_ref, x_ref, rel_ref, src_ref, dst_ref, sems,
 ):
     size, width = x_ref.shape
-    even = is_even(GY[-1])
+    even = is_even(0)
     copies = fetched(
         [
             (src_hbm, src_ref), (dst_hbm, dst_ref), (x_hbm, x_ref), (rel_hbm, rel_ref),
@@ -235,15 +249,15 @@
 def relation_kernel(kinds_ref, si0_ref, so0_ref, h0_ref, si1_ref, so1_ref, h1_ref, acc_ref):
     top = slice(0, h0_ref.shape[0])
     acc_ref[...] = jnp.zeros_like(acc_ref)
-    rows_b, _ = sent(is_even(GY[-1]), si0_ref, so0_ref, top)
+    rows_b, _ = sent(is_even(0), si0_ref, so0_ref, top)
     add_relation(acc_ref, rows_b, h0_ref[...], kinds_ref[0])
-    rows_b, _ = sent(is_even(GX[-1]), si1_ref, so1_ref, top)
+    rows_b, _ = sent(is_even(1), si1_ref, so1_ref, top)
     add_relation(acc_ref, rows_b, h1_ref[...], kinds_ref[1])
 
 
-def stepped(turn, axis, sent_refs, got_refs, c_ref, x_ref, wsel_ref, xn_ref, h_ref):
+def stepped(turn, sent_refs, got_refs, c_ref, x_ref, wsel_ref, xn_ref, h_ref):
     size = x_ref.shape[0]
-    even = is_even(axis)
+    even = is_even(turn)
     top, tail = slice(0, size), slice(size, sent_refs[0].shape[0])
     rows_b, mapped = sent(even, *sent_refs, top)
     target, far = got(even, *got_refs, top)
@@ -265,9 +279,9 @@
 ):
     size = x_ref.shape[0]
     rows_b, mapped = stepped(
-        0, GY[-1], (si_ref, so_ref), (gi_ref, go_ref), c_ref, x_ref, wsel_ref, xn_ref, h_ref
-    )
-    put(is_even(GX[-1]), rows_b, mapped, inner_ref, outer_ref, slice(0, size))
+        0, (si_ref, so_ref), (gi_ref, go_ref), c_ref, x_ref, wsel_ref, xn_ref, h_ref
+    )
+    put(is_even(1), rows_b, mapped, inner_ref, outer_ref, slice(0, size))
     inner_ref[size:, :] = near_ref[...]
     outer_ref[size:, :] = near_ref[...]
 
@@ -277,7 +291,7 @@
     xn_ref, h_ref, rows_ref, mapped_ref,
 ):
     rows_b, mapped = stepped(
-        1, GX[-1], (si_ref, so_ref), (gi_ref, go_ref), c_ref, x_ref, wsel_ref, xn_ref, h_ref
+        1, (si_ref, so_ref), (gi_ref, go_ref), c_ref, x_ref, wsel_ref, xn_ref, h_ref
     )
     rows_ref[...] = rows_b
     mapped_ref[...] = mapped
@@ -296,7 +310,7 @@
 
 def finish_kernel(rows_ref, far_ref, gi_ref, go_ref, h_ref, x_ref, wsel_ref, xn_ref):
     size = x_ref.shape[0]
-    ends, _ = got(is_even(GY[-1]), gi_ref, go_ref, slice(size, gi_ref.shape[0]))
+    ends, _ = got(is_even(0), gi_ref, go_ref, slice(size, gi_ref.shape[0]))
     counts_t = far_count(ends.astype(F32), size)
     grad = source_grad(h_ref[...], chosen_of(wsel_ref, 2))
     grad = grad + target_grad(rows_ref[...], far_ref[...], counts_t)
@@ -354,8 +368,15 @@
 
     def exchanged(turn, inner, outer):
         axes = buckets[turn][0]
-        outer_got = swapped_outer(outer, axes)
-        inner_got = swapped_inner(inner, axes)
+        partners = (inner_partner, outer_partner)
+        if CORE in axes:
+            outer_got = swapped(outer, axes, outer_partner)
+        else:
+            outer_got = swapped_by_core(outer, axes, partners[::-1])
+        if CORE in axes:
+            inner_got = swapped(inner, axes, inner_partner)
+        else:
+            inner_got = swapped_by_core(inner, axes, partners)
         return inner_got, outer_got
 
     sent0 = call(

time: 105 us -> 105 us (level)
  starting transfers between devices: 36.8 us -> 35.6 us
    ppermute x4, starting transfers between devices: 22.2 us -> 20.7 us  [the longest x2 14.9 us: swapped_by_core(): return lax.ppermute(value, (CORE,) + axes, pairs)]
where the time goes in v6:
time: 105 us
  blocking collectives  42.5 us (40%)
  starting transfers between devices  35.6 us (34%)
  waiting for transfers between devices  13.7 us (13%)
  Pallas kernels  11.1 us (11%)
  other arithmetic  1.1 us (1%)
    all_to_all x1, blocking collectives, reduce_everywhere(): lax.all_to_all(payload.reshape(near, rows // near, width), NEAR, 0, 0)  23.3 us
    all_to_all x1, blocking collectives, reduce_everywhere(): part = lax.all_to_all(part, DEPTH, 0, 0)  19.2 us
    ppermute x2, starting transfers between devices, swapped_by_core(): return lax.ppermute(value, (CORE,) + axes, pairs)  14.9 us
    ppermute x2, starting transfers between devices, shifted(): return lax.ppermute(value, axes, pairs)  9.38 us
    ppermute x2, waiting for transfers between devices, shifted(): return lax.ppermute(value, axes, pairs)  7.47 us
    ppermute x2, starting transfers between devices, swapped(): lax.ppermute(value, axes, [(i, partner(i, count)) for i in range(count)])  5.81 us
    all_to_all x1, starting transfers between devices, reduce_everywhere(): part = lax.all_to_all(part, PLANE, 0, 0)  5.52 us
    ppermute x2, waiting for transfers between devices, swapped(): lax.ppermute(value, axes, [(i, partner(i, count)) for i in range(count)])  3.43 us
  transfers between devices with their start and end apart: 7, of which 5 were waited for; matrix products, arithmetic and copies ran while one was open for 0% of the time, Pallas kernels for 5%

profile of v6, /device:TPU:1, one launch (start us, length us, event | category | flops | bytes accessed | tf_op | source)
XLA Modules:
  0.0 104.7 jit_solution(12256730440817936243)
XLA Ops:
  0.6 1.7 %shard_map.68 = (bf16[304,256]{1,0:T(8,128)(2,1)S(1)}, bf16[304,256]{1,0:T(8,128)(2,1)S(1)}) custom-call(s32[3,4]{1,0:T(4,128)} %ids_hbm.3, f32[256,256]{1,0:T(8,128)} %x_ref.1, f32[4,256,256]{2,1,0:T(8,128)} %rel_hbm.3, s32[3,6144]{1,0:T(4,128)} %src_hbm.3, s32[3,6144]{1,0:T(4,128)} %dst_hbm.3), custom_call_target="tpu_custom_call" | custom-call | flops 33554432 | bytes 1245184 | tf_op jit(solution)/shard_map/pallas_call | solution.py:382
  2.3 12.9 %collective-permute-start = (bf16[304,256]{1,0:T(8,128)(2,1)S(1)}, bf16[304,256]{1,0:T(8,128)(2,1)S(1)}, u32[]{:S(2)}, u32[]{:S(2)}) collective-permute-start(bf16[304,256]{1,0:T(8,128)(2,1)S(1)} %get-tuple-element.20.si_ref.si0_ref), channel_id=1, source_target_pairs={{0,1},{1,0},{2,3},{3,2},{4,5},{5,4},{6,7},{7,6},{8,9},{9,8},{10,11... | collective-permute-start | bytes 466952 | tf_op jit(solution)/shard_map/ppermute | solution.py:53
  15.2 0.0 copy-start
  15.2 2.1 %collective-permute-start.1 = (bf16[304,256]{1,0:T(8,128)(2,1)S(1)}, bf16[304,256]{1,0:T(8,128)(2,1)S(1)}, u32[]{:S(2)}, u32[]{:S(2)}) collective-permute-start(bf16[304,256]{1,0:T(8,128)(2,1)S(1)} %get-tuple-element.21.so_ref.so0_ref), channel_id=1, source_target_pairs={{0,31},{1,2},{2,1},{3,4},{4,3},{5,6},{6,5},{7,8},{8,7},{9,10},{10,... | collective-permute-start | bytes 466952 | tf_op jit(solution)/shard_map/ppermute | solution.py:53
  17.3 2.9 %shard_map.69 = (f32[256,256]{1,0:T(8,128)S(1)}, f32[256,256]{1,0:T(8,128)S(1)}, f32[256,256]{1,0:T(8,128)S(1)}, bf16[48,256]{1,0:T(8,128)(2,1)S(1)}, bf16[12,25...) custom-call(s32[3,4]{1,0:T(4,128)} %ids_hbm.3, f32[4,256,256]{2,1,0:T(8,128)} %rel_hbm.3, s32[3,6144]{1,0:T(4,128)} %src_hbm.3, ...), custom_call_target="tpu_custom_call" | custom-call | flops 2415919104 | bytes 11108352 | tf_op jit(solution)/shard_map/pallas_call | solution.py:390
  20.2 0.0 collective-permute-done.gi_ref
  20.2 1.4 %collective-permute-done.1.go_ref = bf16[304,256]{1,0:T(8,128)(2,1)S(1)} collective-permute-done((bf16[304,256]{1,0:T(8,128)(2,1)S(1)}, bf16[304,256]{1,0:T(8,128)(2,1)S(1)}, u32[]{:S(2)}, u32[]{:S(2)}) %collective-permute-start.1) | collective-permute-done | bytes 155680 | tf_op jit(solution)/shard_map/ppermute | solution.py:53
  21.6 0.0 copy-done
  21.6 1.3 %shard_map.70 = (f32[256,256]{1,0:T(8,128)S(1)}, bf16[256,256]{1,0:T(8,128)(2,1)S(1)}, bf16[304,256]{1,0:T(8,128)(2,1)S(1)}, bf16[304,256]{1,0:T(8,128)(2,1)S(1)}) custom-call(bf16[304,256]{1,0:T(8,128)(2,1)S(1)} %get-tuple-element.20.si_ref.si0_ref, bf16[304,256]{1,0:T(8,128)(2,1)S(1)} %get-tuple-element.21.so_ref.so0_ref, ...), custom_call_target="tpu_custom_call" | custom-call | flops 1040187392 | bytes 2818048 | tf_op jit(solution)/shard_map/pallas_call | solution.py:395
  22.9 2.7 %collective-permute-start.2 = (bf16[304,256]{1,0:T(8,128)(2,1)S(1)}, bf16[304,256]{1,0:T(8,128)(2,1)S(1)}, u32[]{:S(2)}, u32[]{:S(2)}) collective-permute-start(bf16[304,256]{1,0:T(8,128)(2,1)S(1)} %get-tuple-element.25.si_ref.si1_ref), channel_id=1, source_target_pairs={{0,32},{32,0},{64,96},{96,64},{128,160},{160,128},{192,224},{224,1... | collective-permute-start | bytes 466952 | tf_op jit(solution)/shard_map/ppermute | solution.py:44
  25.7 3.1 %collective-permute-start.3 = (bf16[304,256]{1,0:T(8,128)(2,1)S(1)}, bf16[304,256]{1,0:T(8,128)(2,1)S(1)}, u32[]{:S(2)}, u32[]{:S(2)}) collective-permute-start(bf16[304,256]{1,0:T(8,128)(2,1)S(1)} %get-tuple-element.26.so_ref.so1_ref), channel_id=1, source_target_pairs={{0,480},{32,64},{64,32},{96,128},{128,96},{160,192},{192,160},{224... | collective-permute-start | bytes 466952 | tf_op jit(solution)/shard_map/ppermute | solution.py:44
  28.8 0.0 collective-permute-done.2.gi_ref
  28.8 3.4 %collective-permute-done.3.go_ref = bf16[304,256]{1,0:T(8,128)(2,1)S(1)} collective-permute-done((bf16[304,256]{1,0:T(8,128)(2,1)S(1)}, bf16[304,256]{1,0:T(8,128)(2,1)S(1)}, u32[]{:S(2)}, u32[]{:S(2)}) %collective-permute-start.3) | collective-permute-done | bytes 155680 | tf_op jit(solution)/shard_map/ppermute | solution.py:44
  32.2 1.3 %shard_map.71 = (f32[256,256]{1,0:T(8,128)S(1)}, bf16[256,256]{1,0:T(8,128)(2,1)S(1)}, bf16[256,256]{1,0:T(8,128)(2,1)S(1)}, bf16[256,256]{1,0:T(8,128)(2,1)S(1)}) custom-call(bf16[304,256]{1,0:T(8,128)(2,1)S(1)} %get-tuple-element.25.si_ref.si1_ref, bf16[304,256]{1,0:T(8,128)(2,1)S(1)} %get-tuple-element.26.so_ref.so1_ref, ...), custom_call_target="tpu_custom_call" | custom-call | flops 1040187392 | bytes 2621440 | tf_op jit(solution)/shard_map/pallas_call | solution.py:401
  33.5 5.8 %collective-permute-start.5 = (bf16[256,256]{1,0:T(8,128)(2,1)S(1)}, bf16[256,256]{1,0:T(8,128)(2,1)S(1)}, u32[]{:S(2)}, u32[]{:S(2)}) collective-permute-start(bf16[256,256]{1,0:T(8,128)(2,1)S(1)} %get-tuple-element.29.rows_ref), channel_id=1, source_target_pairs={{0,31},{1,0},{2,1},{3,2},{4,3},{5,4},{6,5},{7,6},{8,7},{9,8},{10,9... | collective-permute-start | bytes 393224 | tf_op jit(solution)/shard_map/ppermute | solution.py:31
  39.3 0.5 shard_map.72.acc_in_ref
  39.8 1.4 %collective-permute-done.5.xq_ref = bf16[256,256]{1,0:T(8,128)(2,1)S(1)} collective-permute-done((bf16[256,256]{1,0:T(8,128)(2,1)S(1)}, bf16[256,256]{1,0:T(8,128)(2,1)S(1)}, u32[]{:S(2)}, u32[]{:S(2)}) %collective-permute-start.5) | collective-permute-done | bytes 131104 | tf_op jit(solution)/shard_map/ppermute | solution.py:31
  41.2 0.7 shard_map.73
  41.9 23.3 %all_to_all.15.in_ref = bf16[64,16,256]{2,1,0:T(8,128)(2,1)S(1)} all-to-all(bf16[64,16,256]{2,1,0:T(8,128)(2,1)S(1)} %bitcast.2), channel_id=1, replica_groups=mesh['xh'=2,'y'=4,'c'=2,'xl'=2,'zh'=8,'zl'=2] {'xh','y','c','xl','zl'}, dimensions={0} | all-to-all | bytes 1048576 | tf_op jit(solution)/shard_map/all_to_all | solution.py:341
  65.2 0.1 shard_map.75
  65.3 19.2 %all_to_all.16.in_ref = bf16[16,16,256]{2,1,0:T(8,128)(2,1)S(1)} all-to-all(bf16[16,16,256]{2,1,0:T(8,128)(2,1)S(1)} %shard_map.75), channel_id=1, replica_groups=mesh['xh'=2,'y'=4,'c'=2,'xl'=2,'zh'=8,'zl'=2] {'zh','zl'}, dimensions={0} | all-to-all | bytes 262144 | tf_op jit(solution)/shard_map/all_to_all | solution.py:343
  84.5 0.9 shard_map.76
  85.3 5.5 %all-to-all-start.2 = ((bf16[32,32,256]{2,1,0:T(8,128)(2,1)}), bf16[32,32,256]{2,1,0:T(8,128)(2,1)S(1)}, u32[]{:S(2)}, u32[]{:S(2)}) async-start(bf16[32,32,256]{2,1,0:T(8,128)(2,1)} %shard_map.76), calls=%async_computation.2 | async-start | bytes 1048576 | tf_op jit(solution)/shard_map/all_to_all | solution.py:345
  90.9 3.6 %collective-permute-start.4 = (bf16[256,256]{1,0:T(8,128)(2,1)S(1)}, bf16[256,256]{1,0:T(8,128)(2,1)S(1)}, u32[]{:S(2)}, u32[]{:S(2)}) collective-permute-start(bf16[256,256]{1,0:T(8,128)(2,1)S(1)} %get-tuple-element.30.mapped_ref), channel_id=1, source_target_pairs={{0,1},{1,2},{2,3},{3,4},{4,5},{5,6},{6,7},{7,8},{8,9},{9,10},{10,1... | collective-permute-start | bytes 393224 | tf_op jit(solution)/shard_map/ppermute | solution.py:31
  94.5 6.0 %collective-permute-done.4.far_ref = bf16[256,256]{1,0:T(8,128)(2,1)S(1)} collective-permute-done((bf16[256,256]{1,0:T(8,128)(2,1)S(1)}, bf16[256,256]{1,0:T(8,128)(2,1)S(1)}, u32[]{:S(2)}, u32[]{:S(2)}) %collective-permute-start.4) | collective-permute-done | bytes 131104 | tf_op jit(solution)/shard_map/ppermute | solution.py:31
  100.5 1.7 %shard_map.74 = f32[256,256]{1,0:T(8,128)} custom-call(bf16[256,256]{1,0:T(8,128)(2,1)S(1)} %get-tuple-element.29.rows_ref, bf16[256,256]{1,0:T(8,128)(2,1)S(1)} %collective-permute-done.4.far_ref, bf16[304,256]{1,0:T(8,128)(2,1)S(1)} %collective-permute-done.gi_ref, bf16[304,256]{1,0:T(8,128)(2,1)S(1)} %collective-permute-done.1.go_ref, ...), custom_call_target="tpu_custom_call" | custom-call | flops 905969664 | bytes 1048576 | tf_op jit(solution)/shard_map/pallas_call | solution.py:414
  102.2 1.4 %all-to-all-done.2 = bf16[32,32,256]{2,1,0:T(8,128)(2,1)S(1)} async-done(((bf16[32,32,256]{2,1,0:T(8,128)(2,1)}), bf16[32,32,256]{2,1,0:T(8,128)(2,1)S(1)}, u32[]{:S(2)}, u32[]{:S(2)}) %all-to-all-start.2) | async-done | bytes 524320 | tf_op jit(solution)/shard_map/all_to_all | solution.py:345
  103.6 1.1 %convert_multiply_fusion = f32[32,32,256]{2,1,0:T(8,128)} fusion(bf16[32,32,256]{2,1,0:T(8,128)(2,1)S(1)} %all-to-all-done.2), kind=kLoop, calls=%fused_computation | loop fusion | flops 524288 | bytes 1572864 | tf_op jit(solution)/shard_map/div | solution.py:420
Async XLA Ops:
  2.3 17.9 %collective-permute-start = (bf16[304,256]{1,0:T(8,128)(2,1)S(1)}, bf16[304,256]{1,0:T(8,128)(2,1)S(1)}, u32[]{:S(2)}, u32[]{:S(2)}) collective-permute-start(bf16[304,256]{1,0:T(8,128)(2,1)S(1)} %get-tuple-element.20.si_ref.si0_ref), channel_id=1, source_target_pairs={{0,1},{1,0},{2,3},{3,2},{4,5},{5,4},{6,7},{7,6},{8,9},{9,8},{10,11... | collective-permute-start | bytes 466952 | tf_op jit(solution)/shard_map/ppermute | solution.py:53
  15.2 6.4 %copy-start = (f32[256,256]{1,0:T(8,128)S(1)}, f32[256,256]{1,0:T(8,128)}, u32[]{:S(2)}) copy-start(f32[256,256]{1,0:T(8,128)} %x_ref.1) | copy-start | bytes 786436
  15.2 6.4 %collective-permute-start.1 = (bf16[304,256]{1,0:T(8,128)(2,1)S(1)}, bf16[304,256]{1,0:T(8,128)(2,1)S(1)}, u32[]{:S(2)}, u32[]{:S(2)}) collective-permute-start(bf16[304,256]{1,0:T(8,128)(2,1)S(1)} %get-tuple-element.21.so_ref.so0_ref), channel_id=1, source_target_pairs={{0,31},{1,2},{2,1},{3,4},{4,3},{5,6},{6,5},{7,8},{8,7},{9,10},{10,... | collective-permute-start | bytes 466952 | tf_op jit(solution)/shard_map/ppermute | solution.py:53
  22.9 5.8 %collective-permute-start.2 = (bf16[304,256]{1,0:T(8,128)(2,1)S(1)}, bf16[304,256]{1,0:T(8,128)(2,1)S(1)}, u32[]{:S(2)}, u32[]{:S(2)}) collective-permute-start(bf16[304,256]{1,0:T(8,128)(2,1)S(1)} %get-tuple-element.25.si_ref.si1_ref), channel_id=1, source_target_pairs={{0,32},{32,0},{64,96},{96,64},{128,160},{160,128},{192,224},{224,1... | collective-permute-start | bytes 466952 | tf_op jit(solution)/shard_map/ppermute | solution.py:44
  25.7 6.5 %collective-permute-start.3 = (bf16[304,256]{1,0:T(8,128)(2,1)S(1)}, bf16[304,256]{1,0:T(8,128)(2,1)S(1)}, u32[]{:S(2)}, u32[]{:S(2)}) collective-permute-start(bf16[304,256]{1,0:T(8,128)(2,1)S(1)} %get-tuple-element.26.so_ref.so1_ref), channel_id=1, source_target_pairs={{0,480},{32,64},{64,32},{96,128},{128,96},{160,192},{192,160},{224... | collective-permute-start | bytes 466952 | tf_op jit(solution)/shard_map/ppermute | solution.py:44
  33.5 7.7 %collective-permute-start.5 = (bf16[256,256]{1,0:T(8,128)(2,1)S(1)}, bf16[256,256]{1,0:T(8,128)(2,1)S(1)}, u32[]{:S(2)}, u32[]{:S(2)}) collective-permute-start(bf16[256,256]{1,0:T(8,128)(2,1)S(1)} %get-tuple-element.29.rows_ref), channel_id=1, source_target_pairs={{0,31},{1,0},{2,1},{3,2},{4,3},{5,4},{6,5},{7,6},{8,7},{9,8},{10,9... | collective-permute-start | bytes 393224 | tf_op jit(solution)/shard_map/ppermute | solution.py:31
  85.3 18.3 %all-to-all-start.2 = ((bf16[32,32,256]{2,1,0:T(8,128)(2,1)}), bf16[32,32,256]{2,1,0:T(8,128)(2,1)S(1)}, u32[]{:S(2)}, u32[]{:S(2)}) async-start(bf16[32,32,256]{2,1,0:T(8,128)(2,1)} %shard_map.76), calls=%async_computation.2 | async-start | bytes 1048576 | tf_op jit(solution)/shard_map/all_to_all | solution.py:345
  90.9 9.7 %collective-permute-start.4 = (bf16[256,256]{1,0:T(8,128)(2,1)S(1)}, bf16[256,256]{1,0:T(8,128)(2,1)S(1)}, u32[]{:S(2)}, u32[]{:S(2)}) collective-permute-start(bf16[256,256]{1,0:T(8,128)(2,1)S(1)} %get-tuple-element.30.mapped_ref), channel_id=1, source_target_pairs={{0,1},{1,2},{2,3},{3,4},{4,5},{5,6},{6,7},{7,8},{8,9},{9,10},{10,1... | collective-permute-start | bytes 393224 | tf_op jit(solution)/shard_map/ppermute | solution.py:31

commit v7 on v6

--- a/solution.py
+++ b/solution.py
@@ -1,4 +1,5 @@
 import functools
+import itertools
 import math
 
 import jax
@@ -14,9 +15,9 @@
 CORE = "c"
 GX = ("xh", "y", "c")
 GY = ("xl", "zh", "zl")
-PLANE = ("xh", "y", "c", "xl")
-NEAR = PLANE + ("zl",)
-DEPTH = ("zh", "zl")
+NEAR = ("xh", "y", "c", "xl", "zl")
+DEPTH = ("zl", "zh")
+PLANE = ("y", "xh", "xl", "c")
 LEARN_RATE = 0.5
 GROUPS = 4
 VMEM = pl.BlockSpec(memory_space=pltpu.VMEM)
@@ -297,15 +298,31 @@
     mapped_ref[...] = mapped
 
 
-def last_kernel(kinds_ref, rows_ref, xq_ref, mapped_ref, c_ref, acc_in_ref, h_ref, out_ref, acc_ref):
+def block_order():
+    sizes = [lax.axis_size(axis) for axis in NEAR]
+    order = []
+    for place in itertools.product(*map(range, sizes)):
+        at = dict(zip(NEAR, place))
+        block = 0
+        for axis in PLANE + (DEPTH[0],):
+            block = block * lax.axis_size(axis) + at[axis]
+        order.append(block)
+    return order
+
+
+def last_kernel(order, kinds_ref, rows_ref, xq_ref, mapped_ref, c_ref, acc_in_ref, h_ref, out_ref, acc_ref):
     slopes_b = slopes(dot_nt(mapped_ref[...], xq_ref[...]), c_ref[...])
     pulled = dot_nn(slopes_b, xq_ref[...]).astype(BF16)
     h_ref[...] = pulled
     acc_ref[...] = acc_in_ref[...]
     add_relation(acc_ref, rows_ref[...], pulled, kinds_ref[2])
-    kinds, width = acc_ref.shape[:2]
-    for k in range(kinds):
-        out_ref[k * width : (k + 1) * width, :] = acc_ref[k].astype(BF16)
+    width = acc_ref.shape[1]
+    share = out_ref.shape[0] // len(order)
+    for place, block in enumerate(order):
+        kind, first = divmod(block * share, width)
+        out_ref[place * share : (place + 1) * share, :] = acc_ref[
+            kind, first : first + share, :
+        ].astype(BF16)
 
 
 def finish_kernel(rows_ref, far_ref, gi_ref, go_ref, h_ref, x_ref, wsel_ref, xn_ref):
@@ -318,10 +335,11 @@
 
 
 def sum_kernel(apart, in_ref, out_ref):
-    share = in_ref.shape[1]
+    count, share = in_ref.shape[:2]
+    run = count // apart
     for i in range(apart):
-        acc = in_ref[i].astype(F32)
-        for j in range(i + apart, in_ref.shape[0], apart):
+        acc = in_ref[i * run].astype(F32)
+        for j in range(i * run + 1, (i + 1) * run):
             acc = acc + in_ref[j].astype(F32)
         total = acc.astype(BF16)
         for k in range(out_ref.shape[0]):
@@ -341,7 +359,7 @@
     part = lax.all_to_all(payload.reshape(near, rows // near, width), NEAR, 0, 0)
     part = summed_for(part, lax.axis_size(DEPTH), 1)
     part = lax.all_to_all(part, DEPTH, 0, 0)
-    part = summed_for(part, lax.axis_size(PLANE), lax.axis_size(DEPTH[-1]))
+    part = summed_for(part, lax.axis_size(PLANE), lax.axis_size(DEPTH[0]))
     part = lax.all_to_all(part, PLANE, 0, 0)
     return part.reshape(rows, width).astype(F32)
 
@@ -408,7 +426,7 @@
     far = shifted(mapped2, axes, -offset)
     acc = call(relation_kernel, [f_rel], [VMEM] * 7, 2 * square)(of_row, *sent0, h0, *sent1, h1)[0]
     h2, payload, _ = call(
-        last_kernel, [b_rows, b_rel, f_rel],
+        functools.partial(last_kernel, block_order()), [b_rows, b_rel, f_rel],
         [VMEM] * 6, 3 * square, aliases={5: 2},
     )(of_row, rows2, xq, mapped2, c2, acc)
     x3 = call(

time: 105 us -> 107 us (1.019)
  waiting for transfers between devices: 13.7 us -> 16.6 us
    all_to_all x1, waiting for transfers between devices: 1.39 us -> 3.4 us  [reduce_everywhere(): part = lax.all_to_all(part, PLANE, 0, 0)]
    ppermute x2, starting transfers between devices: 9.38 us -> 8.01 us  [shifted(): return lax.ppermute(value, axes, pairs)]
where the time goes in v7:
time: 107 us
  blocking collectives  42.5 us (40%)
  starting transfers between devices  34.6 us (32%)
  waiting for transfers between devices  16.6 us (16%)
  Pallas kernels  11.1 us (10%)
  other arithmetic  1.1 us (1%)
    all_to_all x1, blocking collectives, reduce_everywhere(): lax.all_to_all(payload.reshape(near, rows // near, width), NEAR, 0, 0)  23.3 us
    all_to_all x1, blocking collectives, reduce_everywhere(): part = lax.all_to_all(part, DEPTH, 0, 0)  19.2 us
    ppermute x2, starting transfers between devices, swapped_by_core(): return lax.ppermute(value, (CORE,) + axes, pairs)  14.9 us
    ppermute x2, waiting for transfers between devices, shifted(): return lax.ppermute(value, axes, pairs)  8.4 us
    ppermute x2, starting transfers between devices, shifted(): return lax.ppermute(value, axes, pairs)  8.01 us
    all_to_all x1, starting transfers between devices, reduce_everywhere(): part = lax.all_to_all(part, PLANE, 0, 0)  5.88 us
    ppermute x2, starting transfers between devices, swapped(): lax.ppermute(value, axes, [(i, partner(i, count)) for i in range(count)])  5.81 us
    ppermute x2, waiting for transfers between devices, swapped(): lax.ppermute(value, axes, [(i, partner(i, count)) for i in range(count)])  3.43 us
  transfers between devices with their start and end apart: 7, of which 5 were waited for; matrix products, arithmetic and copies ran while one was open for 0% of the time, Pallas kernels for 5%

profile of v7, /device:TPU:1, one launch (start us, length us, event | category | flops | bytes accessed | tf_op | source)
XLA Modules:
  0.0 106.6 jit_solution(16973881272597370399)
XLA Ops:
  0.6 1.7 %shard_map.68 = (bf16[304,256]{1,0:T(8,128)(2,1)S(1)}, bf16[304,256]{1,0:T(8,128)(2,1)S(1)}) custom-call(s32[3,4]{1,0:T(4,128)} %ids_hbm.3, f32[256,256]{1,0:T(8,128)} %x_ref.1, f32[4,256,256]{2,1,0:T(8,128)} %rel_hbm.3, s32[3,6144]{1,0:T(4,128)} %src_hbm.3, s32[3,6144]{1,0:T(4,128)} %dst_hbm.3), custom_call_target="tpu_custom_call" | custom-call | flops 33554432 | bytes 1245184 | tf_op jit(solution)/shard_map/pallas_call | solution.py:400
  2.3 12.9 %collective-permute-start = (bf16[304,256]{1,0:T(8,128)(2,1)S(1)}, bf16[304,256]{1,0:T(8,128)(2,1)S(1)}, u32[]{:S(2)}, u32[]{:S(2)}) collective-permute-start(bf16[304,256]{1,0:T(8,128)(2,1)S(1)} %get-tuple-element.20.si_ref.si0_ref), channel_id=1, source_target_pairs={{0,1},{1,0},{2,3},{3,2},{4,5},{5,4},{6,7},{7,6},{8,9},{9,8},{10,11... | collective-permute-start | bytes 466952 | tf_op jit(solution)/shard_map/ppermute | solution.py:54
  15.2 0.0 copy-start
  15.2 2.1 %collective-permute-start.1 = (bf16[304,256]{1,0:T(8,128)(2,1)S(1)}, bf16[304,256]{1,0:T(8,128)(2,1)S(1)}, u32[]{:S(2)}, u32[]{:S(2)}) collective-permute-start(bf16[304,256]{1,0:T(8,128)(2,1)S(1)} %get-tuple-element.21.so_ref.so0_ref), channel_id=1, source_target_pairs={{0,31},{1,2},{2,1},{3,4},{4,3},{5,6},{6,5},{7,8},{8,7},{9,10},{10,... | collective-permute-start | bytes 466952 | tf_op jit(solution)/shard_map/ppermute | solution.py:54
  17.3 2.9 %shard_map.69 = (f32[256,256]{1,0:T(8,128)S(1)}, f32[256,256]{1,0:T(8,128)S(1)}, f32[256,256]{1,0:T(8,128)S(1)}, bf16[48,256]{1,0:T(8,128)(2,1)S(1)}, bf16[12,25...) custom-call(s32[3,4]{1,0:T(4,128)} %ids_hbm.3, f32[4,256,256]{2,1,0:T(8,128)} %rel_hbm.3, s32[3,6144]{1,0:T(4,128)} %src_hbm.3, ...), custom_call_target="tpu_custom_call" | custom-call | flops 2415919104 | bytes 11108352 | tf_op jit(solution)/shard_map/pallas_call | solution.py:408
  20.2 0.0 collective-permute-done.gi_ref
  20.2 1.4 %collective-permute-done.1.go_ref = bf16[304,256]{1,0:T(8,128)(2,1)S(1)} collective-permute-done((bf16[304,256]{1,0:T(8,128)(2,1)S(1)}, bf16[304,256]{1,0:T(8,128)(2,1)S(1)}, u32[]{:S(2)}, u32[]{:S(2)}) %collective-permute-start.1) | collective-permute-done | bytes 155680 | tf_op jit(solution)/shard_map/ppermute | solution.py:54
  21.6 0.0 copy-done
  21.6 1.3 %shard_map.70 = (f32[256,256]{1,0:T(8,128)S(1)}, bf16[256,256]{1,0:T(8,128)(2,1)S(1)}, bf16[304,256]{1,0:T(8,128)(2,1)S(1)}, bf16[304,256]{1,0:T(8,128)(2,1)S(1)}) custom-call(bf16[304,256]{1,0:T(8,128)(2,1)S(1)} %get-tuple-element.20.si_ref.si0_ref, bf16[304,256]{1,0:T(8,128)(2,1)S(1)} %get-tuple-element.21.so_ref.so0_ref, ...), custom_call_target="tpu_custom_call" | custom-call | flops 1040187392 | bytes 2818048 | tf_op jit(solution)/shard_map/pallas_call | solution.py:413
  22.9 2.7 %collective-permute-start.2 = (bf16[304,256]{1,0:T(8,128)(2,1)S(1)}, bf16[304,256]{1,0:T(8,128)(2,1)S(1)}, u32[]{:S(2)}, u32[]{:S(2)}) collective-permute-start(bf16[304,256]{1,0:T(8,128)(2,1)S(1)} %get-tuple-element.25.si_ref.si1_ref), channel_id=1, source_target_pairs={{0,32},{32,0},{64,96},{96,64},{128,160},{160,128},{192,224},{224,1... | collective-permute-start | bytes 466952 | tf_op jit(solution)/shard_map/ppermute | solution.py:45
  25.7 3.1 %collective-permute-start.3 = (bf16[304,256]{1,0:T(8,128)(2,1)S(1)}, bf16[304,256]{1,0:T(8,128)(2,1)S(1)}, u32[]{:S(2)}, u32[]{:S(2)}) collective-permute-start(bf16[304,256]{1,0:T(8,128)(2,1)S(1)} %get-tuple-element.26.so_ref.so1_ref), channel_id=1, source_target_pairs={{0,480},{32,64},{64,32},{96,128},{128,96},{160,192},{192,160},{224... | collective-permute-start | bytes 466952 | tf_op jit(solution)/shard_map/ppermute | solution.py:45
  28.8 0.0 collective-permute-done.2.gi_ref
  28.8 3.4 %collective-permute-done.3.go_ref = bf16[304,256]{1,0:T(8,128)(2,1)S(1)} collective-permute-done((bf16[304,256]{1,0:T(8,128)(2,1)S(1)}, bf16[304,256]{1,0:T(8,128)(2,1)S(1)}, u32[]{:S(2)}, u32[]{:S(2)}) %collective-permute-start.3) | collective-permute-done | bytes 155680 | tf_op jit(solution)/shard_map/ppermute | solution.py:45
  32.2 1.3 %shard_map.71 = (f32[256,256]{1,0:T(8,128)S(1)}, bf16[256,256]{1,0:T(8,128)(2,1)S(1)}, bf16[256,256]{1,0:T(8,128)(2,1)S(1)}, bf16[256,256]{1,0:T(8,128)(2,1)S(1)}) custom-call(bf16[304,256]{1,0:T(8,128)(2,1)S(1)} %get-tuple-element.25.si_ref.si1_ref, bf16[304,256]{1,0:T(8,128)(2,1)S(1)} %get-tuple-element.26.so_ref.so1_ref, ...), custom_call_target="tpu_custom_call" | custom-call | flops 1040187392 | bytes 2621440 | tf_op jit(solution)/shard_map/pallas_call | solution.py:419
  33.5 5.8 %collective-permute-start.5 = (bf16[256,256]{1,0:T(8,128)(2,1)S(1)}, bf16[256,256]{1,0:T(8,128)(2,1)S(1)}, u32[]{:S(2)}, u32[]{:S(2)}) collective-permute-start(bf16[256,256]{1,0:T(8,128)(2,1)S(1)} %get-tuple-element.29.rows_ref), channel_id=1, source_target_pairs={{0,31},{1,0},{2,1},{3,2},{4,3},{5,4},{6,5},{7,6},{8,7},{9,8},{10,9... | collective-permute-start | bytes 393224 | tf_op jit(solution)/shard_map/ppermute | solution.py:32
  39.3 0.5 shard_map.72.acc_in_ref
  39.8 1.4 %collective-permute-done.5.xq_ref = bf16[256,256]{1,0:T(8,128)(2,1)S(1)} collective-permute-done((bf16[256,256]{1,0:T(8,128)(2,1)S(1)}, bf16[256,256]{1,0:T(8,128)(2,1)S(1)}, u32[]{:S(2)}, u32[]{:S(2)}) %collective-permute-start.5) | collective-permute-done | bytes 131104 | tf_op jit(solution)/shard_map/ppermute | solution.py:32
  41.2 0.7 shard_map.73
  41.9 23.3 %all_to_all.15.in_ref = bf16[64,16,256]{2,1,0:T(8,128)(2,1)S(1)} all-to-all(bf16[64,16,256]{2,1,0:T(8,128)(2,1)S(1)} %bitcast.2), channel_id=1, replica_groups=mesh['xh'=2,'y'=4,'c'=2,'xl'=2,'zh'=8,'zl'=2] {'xh','y','c','xl','zl'}, dimensions={0} | all-to-all | bytes 1048576 | tf_op jit(solution)/shard_map/all_to_all | solution.py:359
  65.2 0.1 shard_map.75
  65.3 19.2 %all_to_all.16.in_ref = bf16[16,16,256]{2,1,0:T(8,128)(2,1)S(1)} all-to-all(bf16[16,16,256]{2,1,0:T(8,128)(2,1)S(1)} %shard_map.75), channel_id=1, replica_groups=mesh['xh'=2,'y'=4,'c'=2,'xl'=2,'zh'=8,'zl'=2] {'zl','zh'}, dimensions={0} | all-to-all | bytes 262144 | tf_op jit(solution)/shard_map/all_to_all | solution.py:361
  84.5 0.9 shard_map.76
  85.3 5.9 %all-to-all-start.2 = ((bf16[32,32,256]{2,1,0:T(8,128)(2,1)}), bf16[32,32,256]{2,1,0:T(8,128)(2,1)S(1)}, u32[]{:S(2)}, u32[]{:S(2)}) async-start(bf16[32,32,256]{2,1,0:T(8,128)(2,1)} %shard_map.76), calls=%async_computation.2 | async-start | bytes 1048576 | tf_op jit(solution)/shard_map/all_to_all | solution.py:363
  91.2 2.3 %collective-permute-start.4 = (bf16[256,256]{1,0:T(8,128)(2,1)S(1)}, bf16[256,256]{1,0:T(8,128)(2,1)S(1)}, u32[]{:S(2)}, u32[]{:S(2)}) collective-permute-start(bf16[256,256]{1,0:T(8,128)(2,1)S(1)} %get-tuple-element.30.mapped_ref), channel_id=1, source_target_pairs={{0,1},{1,2},{2,3},{3,4},{4,5},{5,6},{6,7},{7,8},{8,9},{9,10},{10,1... | collective-permute-start | bytes 393224 | tf_op jit(solution)/shard_map/ppermute | solution.py:32
  93.5 7.0 %collective-permute-done.4.far_ref = bf16[256,256]{1,0:T(8,128)(2,1)S(1)} collective-permute-done((bf16[256,256]{1,0:T(8,128)(2,1)S(1)}, bf16[256,256]{1,0:T(8,128)(2,1)S(1)}, u32[]{:S(2)}, u32[]{:S(2)}) %collective-permute-start.4) | collective-permute-done | bytes 131104 | tf_op jit(solution)/shard_map/ppermute | solution.py:32
  100.4 1.7 %shard_map.74 = f32[256,256]{1,0:T(8,128)} custom-call(bf16[256,256]{1,0:T(8,128)(2,1)S(1)} %get-tuple-element.29.rows_ref, bf16[256,256]{1,0:T(8,128)(2,1)S(1)} %collective-permute-done.4.far_ref, bf16[304,256]{1,0:T(8,128)(2,1)S(1)} %collective-permute-done.gi_ref, bf16[304,256]{1,0:T(8,128)(2,1)S(1)} %collective-permute-done.1.go_ref, ...), custom_call_target="tpu_custom_call" | custom-call | flops 905969664 | bytes 1048576 | tf_op jit(solution)/shard_map/pallas_call | solution.py:432
  102.1 3.4 %all-to-all-done.2 = bf16[32,32,256]{2,1,0:T(8,128)(2,1)S(1)} async-done(((bf16[32,32,256]{2,1,0:T(8,128)(2,1)}), bf16[32,32,256]{2,1,0:T(8,128)(2,1)S(1)}, u32[]{:S(2)}, u32[]{:S(2)}) %all-to-all-start.2) | async-done | bytes 524320 | tf_op jit(solution)/shard_map/all_to_all | solution.py:363
  105.5 1.1 %convert_multiply_fusion = f32[32,32,256]{2,1,0:T(8,128)} fusion(bf16[32,32,256]{2,1,0:T(8,128)(2,1)S(1)} %all-to-all-done.2), kind=kLoop, calls=%fused_computation | loop fusion | flops 524288 | bytes 1572864 | tf_op jit(solution)/shard_map/div | solution.py:438
Async XLA Ops:
  2.3 17.9 %collective-permute-start = (bf16[304,256]{1,0:T(8,128)(2,1)S(1)}, bf16[304,256]{1,0:T(8,128)(2,1)S(1)}, u32[]{:S(2)}, u32[]{:S(2)}) collective-permute-start(bf16[304,256]{1,0:T(8,128)(2,1)S(1)} %get-tuple-element.20.si_ref.si0_ref), channel_id=1, source_target_pairs={{0,1},{1,0},{2,3},{3,2},{4,5},{5,4},{6,7},{7,6},{8,9},{9,8},{10,11... | collective-permute-start | bytes 466952 | tf_op jit(solution)/shard_map/ppermute | solution.py:54
  15.2 6.4 %copy-start = (f32[256,256]{1,0:T(8,128)S(1)}, f32[256,256]{1,0:T(8,128)}, u32[]{:S(2)}) copy-start(f32[256,256]{1,0:T(8,128)} %x_ref.1) | copy-start | bytes 786436
  15.2 6.4 %collective-permute-start.1 = (bf16[304,256]{1,0:T(8,128)(2,1)S(1)}, bf16[304,256]{1,0:T(8,128)(2,1)S(1)}, u32[]{:S(2)}, u32[]{:S(2)}) collective-permute-start(bf16[304,256]{1,0:T(8,128)(2,1)S(1)} %get-tuple-element.21.so_ref.so0_ref), channel_id=1, source_target_pairs={{0,31},{1,2},{2,1},{3,4},{4,3},{5,6},{6,5},{7,8},{8,7},{9,10},{10,... | collective-permute-start | bytes 466952 | tf_op jit(solution)/shard_map/ppermute | solution.py:54
  22.9 5.8 %collective-permute-start.2 = (bf16[304,256]{1,0:T(8,128)(2,1)S(1)}, bf16[304,256]{1,0:T(8,128)(2,1)S(1)}, u32[]{:S(2)}, u32[]{:S(2)}) collective-permute-start(bf16[304,256]{1,0:T(8,128)(2,1)S(1)} %get-tuple-element.25.si_ref.si1_ref), channel_id=1, source_target_pairs={{0,32},{32,0},{64,96},{96,64},{128,160},{160,128},{192,224},{224,1... | collective-permute-start | bytes 466952 | tf_op jit(solution)/shard_map/ppermute | solution.py:45
  25.7 6.5 %collective-permute-start.3 = (bf16[304,256]{1,0:T(8,128)(2,1)S(1)}, bf16[304,256]{1,0:T(8,128)(2,1)S(1)}, u32[]{:S(2)}, u32[]{:S(2)}) collective-permute-start(bf16[304,256]{1,0:T(8,128)(2,1)S(1)} %get-tuple-element.26.so_ref.so1_ref), channel_id=1, source_target_pairs={{0,480},{32,64},{64,32},{96,128},{128,96},{160,192},{192,160},{224... | collective-permute-start | bytes 466952 | tf_op jit(solution)/shard_map/ppermute | solution.py:45
  33.5 7.7 %collective-permute-start.5 = (bf16[256,256]{1,0:T(8,128)(2,1)S(1)}, bf16[256,256]{1,0:T(8,128)(2,1)S(1)}, u32[]{:S(2)}, u32[]{:S(2)}) collective-permute-start(bf16[256,256]{1,0:T(8,128)(2,1)S(1)} %get-tuple-element.29.rows_ref), channel_id=1, source_target_pairs={{0,31},{1,0},{2,1},{3,2},{4,3},{5,4},{6,5},{7,6},{8,7},{9,8},{10,9... | collective-permute-start | bytes 393224 | tf_op jit(solution)/shard_map/ppermute | solution.py:32
  85.3 20.2 %all-to-all-start.2 = ((bf16[32,32,256]{2,1,0:T(8,128)(2,1)}), bf16[32,32,256]{2,1,0:T(8,128)(2,1)S(1)}, u32[]{:S(2)}, u32[]{:S(2)}) async-start(bf16[32,32,256]{2,1,0:T(8,128)(2,1)} %shard_map.76), calls=%async_computation.2 | async-start | bytes 1048576 | tf_op jit(solution)/shard_map/all_to_all | solution.py:363
  91.2 9.2 %collective-permute-start.4 = (bf16[256,256]{1,0:T(8,128)(2,1)S(1)}, bf16[256,256]{1,0:T(8,128)(2,1)S(1)}, u32[]{:S(2)}, u32[]{:S(2)}) collective-permute-start(bf16[256,256]{1,0:T(8,128)(2,1)S(1)} %get-tuple-element.30.mapped_ref), channel_id=1, source_target_pairs={{0,1},{1,2},{2,3},{3,4},{4,5},{5,6},{6,7},{7,8},{8,9},{9,10},{10,1... | collective-permute-start | bytes 393224 | tf_op jit(solution)/shard_map/ppermute | solution.py:32

commit v8 on v6

--- a/solution.py
+++ b/solution.py
@@ -328,6 +328,17 @@
             out_ref[k, i * share : (i + 1) * share, :] = total
 
 
+def widen_kernel(scale, in_ref, out_hbm, wide_ref, sems):
+    kinds, width = wide_ref.shape[:2]
+    copies = []
+    for k in range(kinds):
+        wide_ref[k] = in_ref[k * width : (k + 1) * width, :].astype(F32) * scale
+        copies.append(pltpu.make_async_copy(wide_ref.at[k], out_hbm.at[k], sems.at[k]))
+        copies[-1].start()
+    for copy in copies:
+        copy.wait()
+
+
 def summed_for(parts, copies, apart):
     count, share, width = parts.shape
     out = jax.ShapeDtypeStruct((copies, apart * share, width), BF16)
@@ -342,8 +353,7 @@
     part = summed_for(part, lax.axis_size(DEPTH), 1)
     part = lax.all_to_all(part, DEPTH, 0, 0)
     part = summed_for(part, lax.axis_size(PLANE), lax.axis_size(DEPTH[-1]))
-    part = lax.all_to_all(part, PLANE, 0, 0)
-    return part.reshape(rows, width).astype(F32)
+    return lax.all_to_all(part, PLANE, 0, 0).reshape(rows, width)
 
 
 def training(entity, relations, rel_ids, edge_src, edge_dst):
@@ -415,9 +425,17 @@
         finish_kernel, [f_rows], [VMEM] * 7, 3 * square + counting,
     )(rows2, far, *got0, h2, x2, wsel)[0]
 
-    summed = reduce_everywhere(payload)
-    divisor = math.sqrt(turns * lax.axis_size(AXES))
-    return x3, (summed / divisor).reshape(relations.shape)
+    scale = 1.0 / math.sqrt(turns * lax.axis_size(AXES))
+    rel_grad = pl.pallas_call(
+        functools.partial(widen_kernel, scale),
+        out_shape=f_rel,
+        in_specs=[VMEM],
+        out_specs=HBM,
+        scratch_shapes=[pltpu.VMEM(relations.shape, F32), pltpu.SemaphoreType.DMA((kinds,))],
+        compiler_params=pltpu.CompilerParams(vmem_limit_bytes=16 * 2**20),
+        name="widen",
+    )(reduce_everywhere(payload))
+    return x3, rel_grad
 
 
 def solution(mesh):

time: 105 us -> 105 us (level)
  other arithmetic: 1.1 us -> 0 us
    div x1 -> x0, other arithmetic: 1.1 us -> none  [training(): return (x3, (summed / divisor).reshape(relations.shape))]
where the time goes in v8:
time: 105 us
  blocking collectives  42.5 us (40%)
  starting transfers between devices  35.6 us (34%)
  waiting for transfers between devices  13.7 us (13%)
  Pallas kernels  12.1 us (12%)
    all_to_all x1, blocking collectives, reduce_everywhere(): lax.all_to_all(payload.reshape(near, rows // near, width), NEAR, 0, 0)  23.3 us
    all_to_all x1, blocking collectives, reduce_everywhere(): part = lax.all_to_all(part, DEPTH, 0, 0)  19.2 us
    ppermute x2, starting transfers between devices, swapped_by_core(): return lax.ppermute(value, (CORE,) + axes, pairs)  14.9 us
    ppermute x2, starting transfers between devices, shifted(): return lax.ppermute(value, axes, pairs)  9.38 us
    ppermute x2, waiting for transfers between devices, shifted(): return lax.ppermute(value, axes, pairs)  7.47 us
    ppermute x2, starting transfers between devices, swapped(): lax.ppermute(value, axes, [(i, partner(i, count)) for i in range(count)])  5.81 us
    all_to_all x1, starting transfers between devices, reduce_everywhere(): return lax.all_to_all(part, PLANE, 0, 0).reshape(rows, width)  5.52 us
    ppermute x2, waiting for transfers between devices, swapped(): lax.ppermute(value, axes, [(i, partner(i, count)) for i in range(count)])  3.43 us
  transfers between devices with their start and end apart: 7, of which 5 were waited for; matrix products, arithmetic and copies ran while one was open for 0% of the time, Pallas kernels for 5%

profile of v8, /device:TPU:1, one launch (start us, length us, event | category | flops | bytes accessed | tf_op | source)
XLA Modules:
  0.0 104.6 jit_solution(12038560223597470619)
XLA Ops:
  0.6 1.7 %shard_map.68 = (bf16[304,256]{1,0:T(8,128)(2,1)S(1)}, bf16[304,256]{1,0:T(8,128)(2,1)S(1)}) custom-call(s32[3,4]{1,0:T(4,128)} %ids_hbm.3, f32[256,256]{1,0:T(8,128)} %x_ref.1, f32[4,256,256]{2,1,0:T(8,128)} %rel_hbm.3, s32[3,6144]{1,0:T(4,128)} %src_hbm.3, s32[3,6144]{1,0:T(4,128)} %dst_hbm.3), custom_call_target="tpu_custom_call" | custom-call | flops 33554432 | bytes 1245184 | tf_op jit(solution)/shard_map/pallas_call | solution.py:392
  2.3 12.9 %collective-permute-start = (bf16[304,256]{1,0:T(8,128)(2,1)S(1)}, bf16[304,256]{1,0:T(8,128)(2,1)S(1)}, u32[]{:S(2)}, u32[]{:S(2)}) collective-permute-start(bf16[304,256]{1,0:T(8,128)(2,1)S(1)} %get-tuple-element.20.si_ref.si0_ref), channel_id=1, source_target_pairs={{0,1},{1,0},{2,3},{3,2},{4,5},{5,4},{6,7},{7,6},{8,9},{9,8},{10,11... | collective-permute-start | bytes 466952 | tf_op jit(solution)/shard_map/ppermute | solution.py:53
  15.2 0.0 copy-start
  15.2 2.1 %collective-permute-start.1 = (bf16[304,256]{1,0:T(8,128)(2,1)S(1)}, bf16[304,256]{1,0:T(8,128)(2,1)S(1)}, u32[]{:S(2)}, u32[]{:S(2)}) collective-permute-start(bf16[304,256]{1,0:T(8,128)(2,1)S(1)} %get-tuple-element.21.so_ref.so0_ref), channel_id=1, source_target_pairs={{0,31},{1,2},{2,1},{3,4},{4,3},{5,6},{6,5},{7,8},{8,7},{9,10},{10,... | collective-permute-start | bytes 466952 | tf_op jit(solution)/shard_map/ppermute | solution.py:53
  17.3 2.9 %shard_map.69 = (f32[256,256]{1,0:T(8,128)S(1)}, f32[256,256]{1,0:T(8,128)S(1)}, f32[256,256]{1,0:T(8,128)S(1)}, bf16[48,256]{1,0:T(8,128)(2,1)S(1)}, bf16[12,25...) custom-call(s32[3,4]{1,0:T(4,128)} %ids_hbm.3, f32[4,256,256]{2,1,0:T(8,128)} %rel_hbm.3, s32[3,6144]{1,0:T(4,128)} %src_hbm.3, ...), custom_call_target="tpu_custom_call" | custom-call | flops 2415919104 | bytes 11108352 | tf_op jit(solution)/shard_map/pallas_call | solution.py:400
  20.2 0.0 collective-permute-done.gi_ref
  20.2 1.4 %collective-permute-done.1.go_ref = bf16[304,256]{1,0:T(8,128)(2,1)S(1)} collective-permute-done((bf16[304,256]{1,0:T(8,128)(2,1)S(1)}, bf16[304,256]{1,0:T(8,128)(2,1)S(1)}, u32[]{:S(2)}, u32[]{:S(2)}) %collective-permute-start.1) | collective-permute-done | bytes 155680 | tf_op jit(solution)/shard_map/ppermute | solution.py:53
  21.6 0.0 copy-done
  21.6 1.3 %shard_map.70 = (f32[256,256]{1,0:T(8,128)S(1)}, bf16[256,256]{1,0:T(8,128)(2,1)S(1)}, bf16[304,256]{1,0:T(8,128)(2,1)S(1)}, bf16[304,256]{1,0:T(8,128)(2,1)S(1)}) custom-call(bf16[304,256]{1,0:T(8,128)(2,1)S(1)} %get-tuple-element.20.si_ref.si0_ref, bf16[304,256]{1,0:T(8,128)(2,1)S(1)} %get-tuple-element.21.so_ref.so0_ref, ...), custom_call_target="tpu_custom_call" | custom-call | flops 1040187392 | bytes 2818048 | tf_op jit(solution)/shard_map/pallas_call | solution.py:405
  22.9 2.7 %collective-permute-start.2 = (bf16[304,256]{1,0:T(8,128)(2,1)S(1)}, bf16[304,256]{1,0:T(8,128)(2,1)S(1)}, u32[]{:S(2)}, u32[]{:S(2)}) collective-permute-start(bf16[304,256]{1,0:T(8,128)(2,1)S(1)} %get-tuple-element.25.si_ref.si1_ref), channel_id=1, source_target_pairs={{0,32},{32,0},{64,96},{96,64},{128,160},{160,128},{192,224},{224,1... | collective-permute-start | bytes 466952 | tf_op jit(solution)/shard_map/ppermute | solution.py:44
  25.7 3.1 %collective-permute-start.3 = (bf16[304,256]{1,0:T(8,128)(2,1)S(1)}, bf16[304,256]{1,0:T(8,128)(2,1)S(1)}, u32[]{:S(2)}, u32[]{:S(2)}) collective-permute-start(bf16[304,256]{1,0:T(8,128)(2,1)S(1)} %get-tuple-element.26.so_ref.so1_ref), channel_id=1, source_target_pairs={{0,480},{32,64},{64,32},{96,128},{128,96},{160,192},{192,160},{224... | collective-permute-start | bytes 466952 | tf_op jit(solution)/shard_map/ppermute | solution.py:44
  28.8 0.0 collective-permute-done.2.gi_ref
  28.8 3.4 %collective-permute-done.3.go_ref = bf16[304,256]{1,0:T(8,128)(2,1)S(1)} collective-permute-done((bf16[304,256]{1,0:T(8,128)(2,1)S(1)}, bf16[304,256]{1,0:T(8,128)(2,1)S(1)}, u32[]{:S(2)}, u32[]{:S(2)}) %collective-permute-start.3) | collective-permute-done | bytes 155680 | tf_op jit(solution)/shard_map/ppermute | solution.py:44
  32.2 1.3 %shard_map.71 = (f32[256,256]{1,0:T(8,128)S(1)}, bf16[256,256]{1,0:T(8,128)(2,1)S(1)}, bf16[256,256]{1,0:T(8,128)(2,1)S(1)}, bf16[256,256]{1,0:T(8,128)(2,1)S(1)}) custom-call(bf16[304,256]{1,0:T(8,128)(2,1)S(1)} %get-tuple-element.25.si_ref.si1_ref, bf16[304,256]{1,0:T(8,128)(2,1)S(1)} %get-tuple-element.26.so_ref.so1_ref, ...), custom_call_target="tpu_custom_call" | custom-call | flops 1040187392 | bytes 2621440 | tf_op jit(solution)/shard_map/pallas_call | solution.py:411
  33.5 5.8 %collective-permute-start.5 = (bf16[256,256]{1,0:T(8,128)(2,1)S(1)}, bf16[256,256]{1,0:T(8,128)(2,1)S(1)}, u32[]{:S(2)}, u32[]{:S(2)}) collective-permute-start(bf16[256,256]{1,0:T(8,128)(2,1)S(1)} %get-tuple-element.29.rows_ref), channel_id=1, source_target_pairs={{0,31},{1,0},{2,1},{3,2},{4,3},{5,4},{6,5},{7,6},{8,7},{9,8},{10,9... | collective-permute-start | bytes 393224 | tf_op jit(solution)/shard_map/ppermute | solution.py:31
  39.3 0.5 shard_map.72.acc_in_ref
  39.8 1.4 %collective-permute-done.5.xq_ref = bf16[256,256]{1,0:T(8,128)(2,1)S(1)} collective-permute-done((bf16[256,256]{1,0:T(8,128)(2,1)S(1)}, bf16[256,256]{1,0:T(8,128)(2,1)S(1)}, u32[]{:S(2)}, u32[]{:S(2)}) %collective-permute-start.5) | collective-permute-done | bytes 131104 | tf_op jit(solution)/shard_map/ppermute | solution.py:31
  41.2 0.7 shard_map.73
  41.9 23.3 %all_to_all.15.in_ref = bf16[64,16,256]{2,1,0:T(8,128)(2,1)S(1)} all-to-all(bf16[64,16,256]{2,1,0:T(8,128)(2,1)S(1)} %bitcast.3), channel_id=1, replica_groups=mesh['xh'=2,'y'=4,'c'=2,'xl'=2,'zh'=8,'zl'=2] {'xh','y','c','xl','zl'}, dimensions={0} | all-to-all | bytes 1048576 | tf_op jit(solution)/shard_map/all_to_all | solution.py:352
  65.2 0.1 shard_map.75
  65.3 19.2 %all_to_all.16.in_ref = bf16[16,16,256]{2,1,0:T(8,128)(2,1)S(1)} all-to-all(bf16[16,16,256]{2,1,0:T(8,128)(2,1)S(1)} %shard_map.75), channel_id=1, replica_groups=mesh['xh'=2,'y'=4,'c'=2,'xl'=2,'zh'=8,'zl'=2] {'zh','zl'}, dimensions={0} | all-to-all | bytes 262144 | tf_op jit(solution)/shard_map/all_to_all | solution.py:354
  84.5 0.9 shard_map.76
  85.3 5.5 %all-to-all-start.2 = ((bf16[32,32,256]{2,1,0:T(8,128)(2,1)}), bf16[32,32,256]{2,1,0:T(8,128)(2,1)S(1)}, u32[]{:S(2)}, u32[]{:S(2)}) async-start(bf16[32,32,256]{2,1,0:T(8,128)(2,1)} %shard_map.76), calls=%async_computation.2 | async-start | bytes 1048576 | tf_op jit(solution)/shard_map/all_to_all | solution.py:356
  90.9 3.6 %collective-permute-start.4 = (bf16[256,256]{1,0:T(8,128)(2,1)S(1)}, bf16[256,256]{1,0:T(8,128)(2,1)S(1)}, u32[]{:S(2)}, u32[]{:S(2)}) collective-permute-start(bf16[256,256]{1,0:T(8,128)(2,1)S(1)} %get-tuple-element.30.mapped_ref), channel_id=1, source_target_pairs={{0,1},{1,2},{2,3},{3,4},{4,5},{5,6},{6,7},{7,8},{8,9},{9,10},{10,1... | collective-permute-start | bytes 393224 | tf_op jit(solution)/shard_map/ppermute | solution.py:31
  94.5 6.0 %collective-permute-done.4.far_ref = bf16[256,256]{1,0:T(8,128)(2,1)S(1)} collective-permute-done((bf16[256,256]{1,0:T(8,128)(2,1)S(1)}, bf16[256,256]{1,0:T(8,128)(2,1)S(1)}, u32[]{:S(2)}, u32[]{:S(2)}) %collective-permute-start.4) | collective-permute-done | bytes 131104 | tf_op jit(solution)/shard_map/ppermute | solution.py:31
  100.5 1.7 %shard_map.74 = f32[256,256]{1,0:T(8,128)} custom-call(bf16[256,256]{1,0:T(8,128)(2,1)S(1)} %get-tuple-element.29.rows_ref, bf16[256,256]{1,0:T(8,128)(2,1)S(1)} %collective-permute-done.4.far_ref, bf16[304,256]{1,0:T(8,128)(2,1)S(1)} %collective-permute-done.gi_ref, bf16[304,256]{1,0:T(8,128)(2,1)S(1)} %collective-permute-done.1.go_ref, ...), custom_call_target="tpu_custom_call" | custom-call | flops 905969664 | bytes 1048576 | tf_op jit(solution)/shard_map/pallas_call | solution.py:424
  102.2 1.4 %all-to-all-done.2 = bf16[32,32,256]{2,1,0:T(8,128)(2,1)S(1)} async-done(((bf16[32,32,256]{2,1,0:T(8,128)(2,1)}), bf16[32,32,256]{2,1,0:T(8,128)(2,1)S(1)}, u32[]{:S(2)}, u32[]{:S(2)}) %all-to-all-start.2) | async-done | bytes 524320 | tf_op jit(solution)/shard_map/all_to_all | solution.py:356
  103.6 1.0 widen.1
Async XLA Ops:
  2.3 17.9 %collective-permute-start = (bf16[304,256]{1,0:T(8,128)(2,1)S(1)}, bf16[304,256]{1,0:T(8,128)(2,1)S(1)}, u32[]{:S(2)}, u32[]{:S(2)}) collective-permute-start(bf16[304,256]{1,0:T(8,128)(2,1)S(1)} %get-tuple-element.20.si_ref.si0_ref), channel_id=1, source_target_pairs={{0,1},{1,0},{2,3},{3,2},{4,5},{5,4},{6,7},{7,6},{8,9},{9,8},{10,11... | collective-permute-start | bytes 466952 | tf_op jit(solution)/shard_map/ppermute | solution.py:53
  15.2 6.4 %copy-start = (f32[256,256]{1,0:T(8,128)S(1)}, f32[256,256]{1,0:T(8,128)}, u32[]{:S(2)}) copy-start(f32[256,256]{1,0:T(8,128)} %x_ref.1) | copy-start | bytes 786436
  15.2 6.4 %collective-permute-start.1 = (bf16[304,256]{1,0:T(8,128)(2,1)S(1)}, bf16[304,256]{1,0:T(8,128)(2,1)S(1)}, u32[]{:S(2)}, u32[]{:S(2)}) collective-permute-start(bf16[304,256]{1,0:T(8,128)(2,1)S(1)} %get-tuple-element.21.so_ref.so0_ref), channel_id=1, source_target_pairs={{0,31},{1,2},{2,1},{3,4},{4,3},{5,6},{6,5},{7,8},{8,7},{9,10},{10,... | collective-permute-start | bytes 466952 | tf_op jit(solution)/shard_map/ppermute | solution.py:53
  22.9 5.8 %collective-permute-start.2 = (bf16[304,256]{1,0:T(8,128)(2,1)S(1)}, bf16[304,256]{1,0:T(8,128)(2,1)S(1)}, u32[]{:S(2)}, u32[]{:S(2)}) collective-permute-start(bf16[304,256]{1,0:T(8,128)(2,1)S(1)} %get-tuple-element.25.si_ref.si1_ref), channel_id=1, source_target_pairs={{0,32},{32,0},{64,96},{96,64},{128,160},{160,128},{192,224},{224,1... | collective-permute-start | bytes 466952 | tf_op jit(solution)/shard_map/ppermute | solution.py:44
  25.7 6.5 %collective-permute-start.3 = (bf16[304,256]{1,0:T(8,128)(2,1)S(1)}, bf16[304,256]{1,0:T(8,128)(2,1)S(1)}, u32[]{:S(2)}, u32[]{:S(2)}) collective-permute-start(bf16[304,256]{1,0:T(8,128)(2,1)S(1)} %get-tuple-element.26.so_ref.so1_ref), channel_id=1, source_target_pairs={{0,480},{32,64},{64,32},{96,128},{128,96},{160,192},{192,160},{224... | collective-permute-start | bytes 466952 | tf_op jit(solution)/shard_map/ppermute | solution.py:44
  33.5 7.7 %collective-permute-start.5 = (bf16[256,256]{1,0:T(8,128)(2,1)S(1)}, bf16[256,256]{1,0:T(8,128)(2,1)S(1)}, u32[]{:S(2)}, u32[]{:S(2)}) collective-permute-start(bf16[256,256]{1,0:T(8,128)(2,1)S(1)} %get-tuple-element.29.rows_ref), channel_id=1, source_target_pairs={{0,31},{1,0},{2,1},{3,2},{4,3},{5,4},{6,5},{7,6},{8,7},{9,8},{10,9... | collective-permute-start | bytes 393224 | tf_op jit(solution)/shard_map/ppermute | solution.py:31
  85.3 18.3 %all-to-all-start.2 = ((bf16[32,32,256]{2,1,0:T(8,128)(2,1)}), bf16[32,32,256]{2,1,0:T(8,128)(2,1)S(1)}, u32[]{:S(2)}, u32[]{:S(2)}) async-start(bf16[32,32,256]{2,1,0:T(8,128)(2,1)} %shard_map.76), calls=%async_computation.2 | async-start | bytes 1048576 | tf_op jit(solution)/shard_map/all_to_all | solution.py:356
  90.9 9.7 %collective-permute-start.4 = (bf16[256,256]{1,0:T(8,128)(2,1)S(1)}, bf16[256,256]{1,0:T(8,128)(2,1)S(1)}, u32[]{:S(2)}, u32[]{:S(2)}) collective-permute-start(bf16[256,256]{1,0:T(8,128)(2,1)S(1)} %get-tuple-element.30.mapped_ref), channel_id=1, source_target_pairs={{0,1},{1,2},{2,3},{3,4},{4,5},{5,6},{6,7},{7,8},{8,9},{9,10},{10,1... | collective-permute-start | bytes 393224 | tf_op jit(solution)/shard_map/ppermute | solution.py:31

commit v9 on v7

--- a/solution.py
+++ b/solution.py
@@ -16,7 +16,7 @@
 GX = ("xh", "y", "c")
 GY = ("xl", "zh", "zl")
 NEAR = ("xh", "y", "c", "xl", "zl")
-DEPTH = ("zl", "zh")
+DEPTH = ("zh", "zl")
 PLANE = ("y", "xh", "xl", "c")
 LEARN_RATE = 0.5
 GROUPS = 4
@@ -304,7 +304,7 @@
     for place in itertools.product(*map(range, sizes)):
         at = dict(zip(NEAR, place))
         block = 0
-        for axis in PLANE + (DEPTH[0],):
+        for axis in PLANE + (DEPTH[-1],):
             block = block * lax.axis_size(axis) + at[axis]
         order.append(block)
     return order
@@ -335,11 +335,10 @@
 
 
 def sum_kernel(apart, in_ref, out_ref):
-    count, share = in_ref.shape[:2]
-    run = count // apart
+    share = in_ref.shape[1]
     for i in range(apart):
-        acc = in_ref[i * run].astype(F32)
-        for j in range(i * run + 1, (i + 1) * run):
+        acc = in_ref[i].astype(F32)
+        for j in range(i + apart, in_ref.shape[0], apart):
             acc = acc + in_ref[j].astype(F32)
         total = acc.astype(BF16)
         for k in range(out_ref.shape[0]):
@@ -359,7 +358,7 @@
     part = lax.all_to_all(payload.reshape(near, rows // near, width), NEAR, 0, 0)
     part = summed_for(part, lax.axis_size(DEPTH), 1)
     part = lax.all_to_all(part, DEPTH, 0, 0)
-    part = summed_for(part, lax.axis_size(PLANE), lax.axis_size(DEPTH[0]))
+    part = summed_for(part, lax.axis_size(PLANE), lax.axis_size(DEPTH[-1]))
     part = lax.all_to_all(part, PLANE, 0, 0)
     return part.reshape(rows, width).astype(F32)
 

time: 107 us -> 107 us (level)
  waiting for transfers between devices: 16.6 us -> 15.1 us
    ppermute x2, starting transfers between devices: 8.01 us -> 9.37 us  [shifted(): return lax.ppermute(value, axes, pairs)]
where the time goes in v9:
time: 107 us; the launch traced here: 106 us
  blocking collectives  42.5 us (40%)
  starting transfers between devices  35.6 us (33%)
  waiting for transfers between devices  15.1 us (14%)
  Pallas kernels  11.1 us (10%)
  other arithmetic  1.1 us (1%)
    all_to_all x1, blocking collectives, reduce_everywhere(): lax.all_to_all(payload.reshape(near, rows // near, width), NEAR, 0, 0)  23.3 us
    all_to_all x1, blocking collectives, reduce_everywhere(): part = lax.all_to_all(part, DEPTH, 0, 0)  19.2 us
    ppermute x2, starting transfers between devices, swapped_by_core(): return lax.ppermute(value, (CORE,) + axes, pairs)  14.9 us
    ppermute x2, starting transfers between devices, shifted(): return lax.ppermute(value, axes, pairs)  9.37 us
    ppermute x2, waiting for transfers between devices, shifted(): return lax.ppermute(value, axes, pairs)  7.47 us
    ppermute x2, starting transfers between devices, swapped(): lax.ppermute(value, axes, [(i, partner(i, count)) for i in range(count)])  5.81 us
    all_to_all x1, starting transfers between devices, reduce_everywhere(): part = lax.all_to_all(part, PLANE, 0, 0)  5.52 us
    ppermute x2, waiting for transfers between devices, swapped(): lax.ppermute(value, axes, [(i, partner(i, count)) for i in range(count)])  3.43 us
  transfers between devices with their start and end apart: 7, of which 5 were waited for; matrix products, arithmetic and copies ran while one was open for 0% of the time, Pallas kernels for 5%

profile of v9, /device:TPU:1, one launch (start us, length us, event | category | flops | bytes accessed | tf_op | source)
XLA Modules:
  0.0 106.2 jit_solution(5442699898732697823)
XLA Ops:
  0.6 1.7 %shard_map.68 = (bf16[304,256]{1,0:T(8,128)(2,1)S(1)}, bf16[304,256]{1,0:T(8,128)(2,1)S(1)}) custom-call(s32[3,4]{1,0:T(4,128)} %ids_hbm.3, f32[256,256]{1,0:T(8,128)} %x_ref.1, f32[4,256,256]{2,1,0:T(8,128)} %rel_hbm.3, s32[3,6144]{1,0:T(4,128)} %src_hbm.3, s32[3,6144]{1,0:T(4,128)} %dst_hbm.3), custom_call_target="tpu_custom_call" | custom-call | flops 33554432 | bytes 1245184 | tf_op jit(solution)/shard_map/pallas_call | solution.py:399
  2.3 12.9 %collective-permute-start = (bf16[304,256]{1,0:T(8,128)(2,1)S(1)}, bf16[304,256]{1,0:T(8,128)(2,1)S(1)}, u32[]{:S(2)}, u32[]{:S(2)}) collective-permute-start(bf16[304,256]{1,0:T(8,128)(2,1)S(1)} %get-tuple-element.20.si_ref.si0_ref), channel_id=1, source_target_pairs={{0,1},{1,0},{2,3},{3,2},{4,5},{5,4},{6,7},{7,6},{8,9},{9,8},{10,11... | collective-permute-start | bytes 466952 | tf_op jit(solution)/shard_map/ppermute | solution.py:54
  15.2 0.0 copy-start
  15.2 2.1 %collective-permute-start.1 = (bf16[304,256]{1,0:T(8,128)(2,1)S(1)}, bf16[304,256]{1,0:T(8,128)(2,1)S(1)}, u32[]{:S(2)}, u32[]{:S(2)}) collective-permute-start(bf16[304,256]{1,0:T(8,128)(2,1)S(1)} %get-tuple-element.21.so_ref.so0_ref), channel_id=1, source_target_pairs={{0,31},{1,2},{2,1},{3,4},{4,3},{5,6},{6,5},{7,8},{8,7},{9,10},{10,... | collective-permute-start | bytes 466952 | tf_op jit(solution)/shard_map/ppermute | solution.py:54
  17.3 2.9 %shard_map.69 = (f32[256,256]{1,0:T(8,128)S(1)}, f32[256,256]{1,0:T(8,128)S(1)}, f32[256,256]{1,0:T(8,128)S(1)}, bf16[48,256]{1,0:T(8,128)(2,1)S(1)}, bf16[12,25...) custom-call(s32[3,4]{1,0:T(4,128)} %ids_hbm.3, f32[4,256,256]{2,1,0:T(8,128)} %rel_hbm.3, s32[3,6144]{1,0:T(4,128)} %src_hbm.3, ...), custom_call_target="tpu_custom_call" | custom-call | flops 2415919104 | bytes 11108352 | tf_op jit(solution)/shard_map/pallas_call | solution.py:407
  20.2 0.0 collective-permute-done.gi_ref
  20.2 1.4 %collective-permute-done.1.go_ref = bf16[304,256]{1,0:T(8,128)(2,1)S(1)} collective-permute-done((bf16[304,256]{1,0:T(8,128)(2,1)S(1)}, bf16[304,256]{1,0:T(8,128)(2,1)S(1)}, u32[]{:S(2)}, u32[]{:S(2)}) %collective-permute-start.1) | collective-permute-done | bytes 155680 | tf_op jit(solution)/shard_map/ppermute | solution.py:54
  21.6 0.0 copy-done
  21.6 1.3 %shard_map.70 = (f32[256,256]{1,0:T(8,128)S(1)}, bf16[256,256]{1,0:T(8,128)(2,1)S(1)}, bf16[304,256]{1,0:T(8,128)(2,1)S(1)}, bf16[304,256]{1,0:T(8,128)(2,1)S(1)}) custom-call(bf16[304,256]{1,0:T(8,128)(2,1)S(1)} %get-tuple-element.20.si_ref.si0_ref, bf16[304,256]{1,0:T(8,128)(2,1)S(1)} %get-tuple-element.21.so_ref.so0_ref, ...), custom_call_target="tpu_custom_call" | custom-call | flops 1040187392 | bytes 2818048 | tf_op jit(solution)/shard_map/pallas_call | solution.py:412
  22.9 2.7 %collective-permute-start.2 = (bf16[304,256]{1,0:T(8,128)(2,1)S(1)}, bf16[304,256]{1,0:T(8,128)(2,1)S(1)}, u32[]{:S(2)}, u32[]{:S(2)}) collective-permute-start(bf16[304,256]{1,0:T(8,128)(2,1)S(1)} %get-tuple-element.25.si_ref.si1_ref), channel_id=1, source_target_pairs={{0,32},{32,0},{64,96},{96,64},{128,160},{160,128},{192,224},{224,1... | collective-permute-start | bytes 466952 | tf_op jit(solution)/shard_map/ppermute | solution.py:45
  25.7 3.1 %collective-permute-start.3 = (bf16[304,256]{1,0:T(8,128)(2,1)S(1)}, bf16[304,256]{1,0:T(8,128)(2,1)S(1)}, u32[]{:S(2)}, u32[]{:S(2)}) collective-permute-start(bf16[304,256]{1,0:T(8,128)(2,1)S(1)} %get-tuple-element.26.so_ref.so1_ref), channel_id=1, source_target_pairs={{0,480},{32,64},{64,32},{96,128},{128,96},{160,192},{192,160},{224... | collective-permute-start | bytes 466952 | tf_op jit(solution)/shard_map/ppermute | solution.py:45
  28.8 0.0 collective-permute-done.2.gi_ref
  28.8 3.4 %collective-permute-done.3.go_ref = bf16[304,256]{1,0:T(8,128)(2,1)S(1)} collective-permute-done((bf16[304,256]{1,0:T(8,128)(2,1)S(1)}, bf16[304,256]{1,0:T(8,128)(2,1)S(1)}, u32[]{:S(2)}, u32[]{:S(2)}) %collective-permute-start.3) | collective-permute-done | bytes 155680 | tf_op jit(solution)/shard_map/ppermute | solution.py:45
  32.2 1.3 %shard_map.71 = (f32[256,256]{1,0:T(8,128)S(1)}, bf16[256,256]{1,0:T(8,128)(2,1)S(1)}, bf16[256,256]{1,0:T(8,128)(2,1)S(1)}, bf16[256,256]{1,0:T(8,128)(2,1)S(1)}) custom-call(bf16[304,256]{1,0:T(8,128)(2,1)S(1)} %get-tuple-element.25.si_ref.si1_ref, bf16[304,256]{1,0:T(8,128)(2,1)S(1)} %get-tuple-element.26.so_ref.so1_ref, ...), custom_call_target="tpu_custom_call" | custom-call | flops 1040187392 | bytes 2621440 | tf_op jit(solution)/shard_map/pallas_call | solution.py:418
  33.5 5.8 %collective-permute-start.5 = (bf16[256,256]{1,0:T(8,128)(2,1)S(1)}, bf16[256,256]{1,0:T(8,128)(2,1)S(1)}, u32[]{:S(2)}, u32[]{:S(2)}) collective-permute-start(bf16[256,256]{1,0:T(8,128)(2,1)S(1)} %get-tuple-element.29.rows_ref), channel_id=1, source_target_pairs={{0,31},{1,0},{2,1},{3,2},{4,3},{5,4},{6,5},{7,6},{8,7},{9,8},{10,9... | collective-permute-start | bytes 393224 | tf_op jit(solution)/shard_map/ppermute | solution.py:32
  39.3 0.5 shard_map.72.acc_in_ref
  39.8 1.4 %collective-permute-done.5.xq_ref = bf16[256,256]{1,0:T(8,128)(2,1)S(1)} collective-permute-done((bf16[256,256]{1,0:T(8,128)(2,1)S(1)}, bf16[256,256]{1,0:T(8,128)(2,1)S(1)}, u32[]{:S(2)}, u32[]{:S(2)}) %collective-permute-start.5) | collective-permute-done | bytes 131104 | tf_op jit(solution)/shard_map/ppermute | solution.py:32
  41.2 0.7 shard_map.73
  41.9 23.3 %all_to_all.15.in_ref = bf16[64,16,256]{2,1,0:T(8,128)(2,1)S(1)} all-to-all(bf16[64,16,256]{2,1,0:T(8,128)(2,1)S(1)} %bitcast.2), channel_id=1, replica_groups=mesh['xh'=2,'y'=4,'c'=2,'xl'=2,'zh'=8,'zl'=2] {'xh','y','c','xl','zl'}, dimensions={0} | all-to-all | bytes 1048576 | tf_op jit(solution)/shard_map/all_to_all | solution.py:358
  65.2 0.1 shard_map.75
  65.3 19.2 %all_to_all.16.in_ref = bf16[16,16,256]{2,1,0:T(8,128)(2,1)S(1)} all-to-all(bf16[16,16,256]{2,1,0:T(8,128)(2,1)S(1)} %shard_map.75), channel_id=1, replica_groups=mesh['xh'=2,'y'=4,'c'=2,'xl'=2,'zh'=8,'zl'=2] {'zh','zl'}, dimensions={0} | all-to-all | bytes 262144 | tf_op jit(solution)/shard_map/all_to_all | solution.py:360
  84.5 0.9 shard_map.76
  85.3 5.5 %all-to-all-start.2 = ((bf16[32,32,256]{2,1,0:T(8,128)(2,1)}), bf16[32,32,256]{2,1,0:T(8,128)(2,1)S(1)}, u32[]{:S(2)}, u32[]{:S(2)}) async-start(bf16[32,32,256]{2,1,0:T(8,128)(2,1)} %shard_map.76), calls=%async_computation.2 | async-start | bytes 1048576 | tf_op jit(solution)/shard_map/all_to_all | solution.py:362
  90.9 3.6 %collective-permute-start.4 = (bf16[256,256]{1,0:T(8,128)(2,1)S(1)}, bf16[256,256]{1,0:T(8,128)(2,1)S(1)}, u32[]{:S(2)}, u32[]{:S(2)}) collective-permute-start(bf16[256,256]{1,0:T(8,128)(2,1)S(1)} %get-tuple-element.30.mapped_ref), channel_id=1, source_target_pairs={{0,1},{1,2},{2,3},{3,4},{4,5},{5,6},{6,7},{7,8},{8,9},{9,10},{10,1... | collective-permute-start | bytes 393224 | tf_op jit(solution)/shard_map/ppermute | solution.py:32
  94.5 6.0 %collective-permute-done.4.far_ref = bf16[256,256]{1,0:T(8,128)(2,1)S(1)} collective-permute-done((bf16[256,256]{1,0:T(8,128)(2,1)S(1)}, bf16[256,256]{1,0:T(8,128)(2,1)S(1)}, u32[]{:S(2)}, u32[]{:S(2)}) %collective-permute-start.4) | collective-permute-done | bytes 131104 | tf_op jit(solution)/shard_map/ppermute | solution.py:32
  100.5 1.7 %shard_map.74 = f32[256,256]{1,0:T(8,128)} custom-call(bf16[256,256]{1,0:T(8,128)(2,1)S(1)} %get-tuple-element.29.rows_ref, bf16[256,256]{1,0:T(8,128)(2,1)S(1)} %collective-permute-done.4.far_ref, bf16[304,256]{1,0:T(8,128)(2,1)S(1)} %collective-permute-done.gi_ref, bf16[304,256]{1,0:T(8,128)(2,1)S(1)} %collective-permute-done.1.go_ref, ...), custom_call_target="tpu_custom_call" | custom-call | flops 905969664 | bytes 1048576 | tf_op jit(solution)/shard_map/pallas_call | solution.py:431
  102.2 2.9 %all-to-all-done.2 = bf16[32,32,256]{2,1,0:T(8,128)(2,1)S(1)} async-done(((bf16[32,32,256]{2,1,0:T(8,128)(2,1)}), bf16[32,32,256]{2,1,0:T(8,128)(2,1)S(1)}, u32[]{:S(2)}, u32[]{:S(2)}) %all-to-all-start.2) | async-done | bytes 524320 | tf_op jit(solution)/shard_map/all_to_all | solution.py:362
  105.1 1.1 %convert_multiply_fusion = f32[32,32,256]{2,1,0:T(8,128)} fusion(bf16[32,32,256]{2,1,0:T(8,128)(2,1)S(1)} %all-to-all-done.2), kind=kLoop, calls=%fused_computation | loop fusion | flops 524288 | bytes 1572864 | tf_op jit(solution)/shard_map/div | solution.py:437
Async XLA Ops:
  2.3 17.9 %collective-permute-start = (bf16[304,256]{1,0:T(8,128)(2,1)S(1)}, bf16[304,256]{1,0:T(8,128)(2,1)S(1)}, u32[]{:S(2)}, u32[]{:S(2)}) collective-permute-start(bf16[304,256]{1,0:T(8,128)(2,1)S(1)} %get-tuple-element.20.si_ref.si0_ref), channel_id=1, source_target_pairs={{0,1},{1,0},{2,3},{3,2},{4,5},{5,4},{6,7},{7,6},{8,9},{9,8},{10,11... | collective-permute-start | bytes 466952 | tf_op jit(solution)/shard_map/ppermute | solution.py:54
  15.2 6.4 %copy-start = (f32[256,256]{1,0:T(8,128)S(1)}, f32[256,256]{1,0:T(8,128)}, u32[]{:S(2)}) copy-start(f32[256,256]{1,0:T(8,128)} %x_ref.1) | copy-start | bytes 786436
  15.2 6.4 %collective-permute-start.1 = (bf16[304,256]{1,0:T(8,128)(2,1)S(1)}, bf16[304,256]{1,0:T(8,128)(2,1)S(1)}, u32[]{:S(2)}, u32[]{:S(2)}) collective-permute-start(bf16[304,256]{1,0:T(8,128)(2,1)S(1)} %get-tuple-element.21.so_ref.so0_ref), channel_id=1, source_target_pairs={{0,31},{1,2},{2,1},{3,4},{4,3},{5,6},{6,5},{7,8},{8,7},{9,10},{10,... | collective-permute-start | bytes 466952 | tf_op jit(solution)/shard_map/ppermute | solution.py:54
  22.9 5.8 %collective-permute-start.2 = (bf16[304,256]{1,0:T(8,128)(2,1)S(1)}, bf16[304,256]{1,0:T(8,128)(2,1)S(1)}, u32[]{:S(2)}, u32[]{:S(2)}) collective-permute-start(bf16[304,256]{1,0:T(8,128)(2,1)S(1)} %get-tuple-element.25.si_ref.si1_ref), channel_id=1, source_target_pairs={{0,32},{32,0},{64,96},{96,64},{128,160},{160,128},{192,224},{224,1... | collective-permute-start | bytes 466952 | tf_op jit(solution)/shard_map/ppermute | solution.py:45
  25.7 6.5 %collective-permute-start.3 = (bf16[304,256]{1,0:T(8,128)(2,1)S(1)}, bf16[304,256]{1,0:T(8,128)(2,1)S(1)}, u32[]{:S(2)}, u32[]{:S(2)}) collective-permute-start(bf16[304,256]{1,0:T(8,128)(2,1)S(1)} %get-tuple-element.26.so_ref.so1_ref), channel_id=1, source_target_pairs={{0,480},{32,64},{64,32},{96,128},{128,96},{160,192},{192,160},{224... | collective-permute-start | bytes 466952 | tf_op jit(solution)/shard_map/ppermute | solution.py:45
  33.5 7.7 %collective-permute-start.5 = (bf16[256,256]{1,0:T(8,128)(2,1)S(1)}, bf16[256,256]{1,0:T(8,128)(2,1)S(1)}, u32[]{:S(2)}, u32[]{:S(2)}) collective-permute-start(bf16[256,256]{1,0:T(8,128)(2,1)S(1)} %get-tuple-element.29.rows_ref), channel_id=1, source_target_pairs={{0,31},{1,0},{2,1},{3,2},{4,3},{5,4},{6,5},{7,6},{8,7},{9,8},{10,9... | collective-permute-start | bytes 393224 | tf_op jit(solution)/shard_map/ppermute | solution.py:32
  85.3 19.8 %all-to-all-start.2 = ((bf16[32,32,256]{2,1,0:T(8,128)(2,1)}), bf16[32,32,256]{2,1,0:T(8,128)(2,1)S(1)}, u32[]{:S(2)}, u32[]{:S(2)}) async-start(bf16[32,32,256]{2,1,0:T(8,128)(2,1)} %shard_map.76), calls=%async_computation.2 | async-start | bytes 1048576 | tf_op jit(solution)/shard_map/all_to_all | solution.py:362
  90.9 9.7 %collective-permute-start.4 = (bf16[256,256]{1,0:T(8,128)(2,1)S(1)}, bf16[256,256]{1,0:T(8,128)(2,1)S(1)}, u32[]{:S(2)}, u32[]{:S(2)}) collective-permute-start(bf16[256,256]{1,0:T(8,128)(2,1)S(1)} %get-tuple-element.30.mapped_ref), channel_id=1, source_target_pairs={{0,1},{1,2},{2,3},{3,4},{4,5},{5,6},{6,7},{7,8},{8,9},{9,10},{10,1... | collective-permute-start | bytes 393224 | tf_op jit(solution)/shard_map/ppermute | solution.py:32
